TPU v7x, 32 devices: a whole 2x2x4 slice. The times are simulated.
32 devices in a mesh: rows: 8 (over z, x), tm: 4 (over y, core).
Axes of the slice: x: 2, y: 2, z: 4, core: 2. Of those that a mesh axis runs over, the one named last changes fastest.
Arguments:
- features: bfloat16 [8, 1536, 1024], P('rows', 'tm'), may hold values from -6 to 6
- lengths: int32 [8], P('rows'), may hold values from 50 to 1536, as said below
- buckets: int32 [3071], replicated, may hold values from 0 to 63
- gain_first: float32 [1024], replicated, may hold values from 0.25 to 1.75
- first_in: bfloat16 [1024, 4096], replicated, may hold values from -0.1875 to 0.1875
- first_out: bfloat16 [4096, 1024], replicated, may hold values from -0.1875 to 0.1875
- gain_attend: float32 [1024], replicated, may hold values from 0.25 to 1.75
- query_weight: bfloat16 [1024, 1024], replicated, may hold values from -0.1875 to 0.1875
- key_weight: bfloat16 [1024, 1024], replicated, may hold values from -0.1875 to 0.1875
- value_weight: bfloat16 [1024, 1024], replicated, may hold values from -0.1875 to 0.1875
- output_weight: bfloat16 [1024, 1024], replicated, may hold values from -1 to 1
- bias_table: float32 [8, 64], replicated, may hold values from -4 to 4
- gain_conv: float32 [1024], replicated, may hold values from 0.25 to 1.75
- point_in: bfloat16 [1024, 2048], replicated, may hold values from -0.1875 to 0.1875
- depth_weight: float32 [5, 1024], replicated, may hold values from -2.5 to 2.5
- batch_scale: float32 [1024], replicated, may hold values from 0.25 to 1.75
- batch_shift: float32 [1024], replicated, may hold values from -3 to 3
- point_out: bfloat16 [1024, 1024], replicated, may hold values from -0.1875 to 0.1875
- gain_second: float32 [1024], replicated, may hold values from 0.25 to 1.75
- second_in: bfloat16 [1024, 4096], replicated, may hold values from -0.1875 to 0.1875
- second_out: bfloat16 [4096, 1024], replicated, may hold values from -0.1875 to 0.1875
- gain_final: float32 [1024], replicated, may hold values from 0.25 to 1.75
- cotangent: bfloat16 [8, 1536, 1024], P('rows', 'tm'), may hold values from -6 to 6
Outputs:
- output: bfloat16 [8, 1536, 1024], P('rows', 'tm')
- grad_features: bfloat16 [8, 1536, 1024], P('rows', 'tm')
- grad_gain_first: float32 [1024], P('rows')
- grad_first_in: float32 [1024, 4096], P('rows')
- grad_first_out: float32 [4096, 1024], P('rows')
- grad_gain_attend: float32 [1024], P('rows')
- grad_query: float32 [1024, 1024], P('rows')
- grad_key: float32 [1024, 1024], P('rows')
- grad_value: float32 [1024, 1024], P('rows')
- grad_output: float32 [1024, 1024], P('rows')
- grad_table: float32 [8, 64], replicated
- grad_gain_conv: float32 [1024], P('rows')
- grad_point_in: float32 [1024, 2048], P('rows')
- grad_depth: float32 [5, 1024], replicated
- grad_batch_scale: float32 [1024], replicated
- grad_batch_shift: float32 [1024], replicated
- grad_point_out: float32 [1024, 1024], P('rows')
- grad_gain_second: float32 [1024], P('rows')
- grad_second_in: float32 [1024, 4096], P('rows')
- grad_second_out: float32 [4096, 1024], P('rows')
- grad_gain_final: float32 [1024], P('rows')
Inputs may be any that keep to these rules, and one draw needn't show every extreme that they name: `lengths`: in each aligned pair of rows (rows 2k and 2k + 1) one row, drawn from the seed, holds all 1536 frames.
All inputs are finite; a program needn't handle non-finite values.
Results may differ from a plain program's by a relative error of at most 0.02.
Values may be sent and summed in bfloat16 or wider, within the bound.
No kernel may reach another device: no remote copies, remote signals or barrier semaphores. Data moves between devices by JAX's collectives and lax.ppermute only.
A program may use at most 448 MiB of HBM per device.

v0:
```python
import jax
import jax.numpy as jnp
from jax import lax
from jax.sharding import PartitionSpec as P

EPS = 1e-05
NEGATIVE = -1e30


def padded_2(shard, sides, width):
    for axis, dim in sides:
        count, length = (lax.axis_size(axis), shard.shape[dim])
        up = [(i, (i + 1) % count) for i in range(count - 1)]
        down = [(j, i) for i, j in up]
        last = lax.slice_in_dim(shard, length - width, length, axis=dim)
        first = lax.slice_in_dim(shard, 0, width, axis=dim)
        before = lax.ppermute(last, axis, up)
        after = lax.ppermute(first, axis, down)
        shard = jnp.concatenate([before, shard, after], axis=dim)
    return shard


def matmul(left, right):
    return jnp.dot(left, right, preferred_element_type=jnp.float32)


def back_prop(grad, weight):
    return lax.dot_general(
        grad, weight, (((1,), (1,)), ((), ())), preferred_element_type=jnp.float32
    )


def weight_grad(inputs, grad):
    return lax.dot_general(
        inputs, grad, (((0,), (0,)), ((), ())), preferred_element_type=jnp.float32
    )


def norm_forward(values, gain):
    mean = jnp.mean(values, axis=-1, keepdims=True)
    centered = values - mean
    rstd = lax.rsqrt(jnp.mean(centered * centered, axis=-1, keepdims=True) + EPS)
    scaled = centered * rstd
    return (scaled * gain, scaled, rstd)


def norm_backward(grad, scaled, rstd, gain):
    weighted = grad * gain
    inner = weighted - jnp.mean(weighted, axis=-1, keepdims=True)
    inner = inner - scaled * jnp.mean(weighted * scaled, axis=-1, keepdims=True)
    return (rstd * inner, jnp.sum(grad * scaled, axis=0))


def silu_slope(hidden):
    sigma = jax.nn.sigmoid(hidden)
    return sigma * (1.0 + hidden * (1.0 - sigma))


def ffn_forward(values, gain, weight_in, weight_out):
    normed, scaled, rstd = norm_forward(values, gain)
    act_in = normed.astype(jnp.bfloat16)
    hidden = matmul(act_in, weight_in)
    act_mid = jax.nn.silu(hidden).astype(jnp.bfloat16)
    return (values + 0.5 * matmul(act_mid, weight_out), (act_in, hidden, act_mid, scaled, rstd))


def ffn_backward(grad, kept, gain, weight_in, weight_out):
    act_in, hidden, act_mid, scaled, rstd = kept
    d_branch = (0.5 * grad).astype(jnp.bfloat16)
    grad_out = weight_grad(act_mid, d_branch)
    d_hidden = (back_prop(d_branch, weight_out) * silu_slope(hidden)).astype(jnp.bfloat16)
    grad_in = weight_grad(act_in, d_hidden)
    d_values, grad_gain = norm_backward(back_prop(d_hidden, weight_in), scaled, rstd, gain)
    return (grad + d_values, grad_gain, grad_in, grad_out)


def toeplitz(vector, row_total, col_total):
    heads = vector.shape[0]
    length = row_total + col_total
    padded = jnp.pad(vector, ((0, 0), (0, 1)))
    tiled = jnp.tile(padded, (1, row_total + 1))[:, : row_total * (length + 1)]
    hankel = tiled.reshape(heads, row_total, length + 1)[:, :, :col_total]
    return hankel[:, ::-1, :]


def diagonal_sums(matrix, row_total, col_total):
    heads = matrix.shape[0]
    length = row_total + col_total
    hankel = matrix[:, ::-1, :]
    wide = jnp.pad(hankel, ((0, 0), (0, 0), (0, length + 1 - col_total)))
    flat = wide.reshape(heads, row_total * (length + 1))
    flat = jnp.pad(flat, ((0, 0), (0, (row_total + 1) * length - row_total * (length + 1))))
    return jnp.sum(flat.reshape(heads, row_total + 1, length), axis=1)[:, : length - 1]


def over_blocks(update, carry, shared, lengths, block_count):
    for block in range(block_count):
        carry, shared = update(carry, shared, block=block, first=0, last=lengths.shape[0])
    return (carry, shared)


def shards(
    features,
    lengths,
    buckets,
    gain_first,
    first_in,
    first_out,
    gain_attend,
    query_weight,
    key_weight,
    value_weight,
    output_weight,
    bias_table,
    gain_conv,
    point_in,
    depth_weight,
    batch_scale,
    batch_shift,
    point_out,
    gain_second,
    second_in,
    second_out,
    gain_final,
    cotangent,
):
    row_count, width, model = features.shape
    tokens = row_count * width
    heads, bucket_count = bias_table.shape
    head_dim = model // heads
    scale = head_dim ** (-0.5)
    block_count = lax.axis_size("tm")
    frames = width * block_count
    half = depth_weight.shape[0] // 2
    offset = lax.axis_index("tm") * width
    valid = ((offset + jnp.arange(width))[None, :] < lengths[:, None]).astype(jnp.float32)
    valid_flat = valid.reshape(tokens, 1)
    valid_three = valid[:, :, None]
    state = features.astype(jnp.float32).reshape(tokens, model)
    state, kept_first = ffn_forward(state, gain_first, first_in, first_out)
    normed, scaled_attend, rstd_attend = norm_forward(state, gain_attend)
    act_attend = normed.astype(jnp.bfloat16)
    query = matmul(act_attend, query_weight).astype(jnp.bfloat16)
    key_here = matmul(act_attend, key_weight).astype(jnp.bfloat16).reshape(row_count, width, model)
    value_here = (
        matmul(act_attend, value_weight).astype(jnp.bfloat16).reshape(row_count, width, model)
    )
    keys, values = (
        lax.all_gather(key_here, "tm", axis=1, tiled=True),
        lax.all_gather(value_here, "tm", axis=1, tiled=True),
    )
    query_heads = query.reshape(row_count, width, heads, head_dim)
    key_heads = keys.reshape(row_count, frames, heads, head_dim)
    value_heads = values.reshape(row_count, frames, heads, head_dim)
    window = lax.dynamic_slice_in_dim(buckets, frames - width - offset, width + frames - 1)
    one_hot = (window[:, None] == jnp.arange(bucket_count)[None, :]).astype(jnp.float32)
    bias_vector = lax.dot_general(
        bias_table, one_hot, (((1,), (1,)), ((), ())), precision=lax.Precision.HIGHEST
    )
    bias = toeplitz(bias_vector, width, frames)

    def scores_at(block, first, last):
        begin = block * width
        part = key_heads[first:last, begin : begin + width]
        scores = (
            jnp.einsum("rqhd,rkhd->rhqk", query_heads, part, preferred_element_type=jnp.float32)
            * scale
        )
        scores = scores + bias[None, :, :, begin : begin + width]
        live = ((begin + jnp.arange(width))[None, :] < lengths[first:last, None])[:, None, None, :]
        return (jnp.where(live, scores, NEGATIVE), live)

    def max_sum(carry, shared, block, first, last):
        top_now, total_now = carry
        masked, live = scores_at(block, first, last)
        new_top = jnp.maximum(top_now, jnp.max(masked, axis=-1))
        weights = jnp.where(live, jnp.exp(masked - new_top[..., None]), 0.0)
        return (
            (new_top, total_now * jnp.exp(top_now - new_top) + jnp.sum(weights, axis=-1)),
            shared,
        )

    start_stats = (
        jnp.full((row_count, heads, width), NEGATIVE, jnp.float32),
        jnp.zeros((row_count, heads, width), jnp.float32),
    )
    (top, total), unused = over_blocks(max_sum, start_stats, (), lengths, block_count)

    def probs_at(block, first, last):
        masked, live = scores_at(block, first, last)
        weights = jnp.where(live, jnp.exp(masked - top[first:last, :, :, None]), 0.0)
        return weights / total[first:last, :, :, None]

    def weighted_sum(carry, shared, block, first, last):
        begin = block * width
        probs = probs_at(block, first, last).astype(jnp.bfloat16)
        part = value_heads[first:last, begin : begin + width]
        return (
            (
                carry[0]
                + jnp.einsum("rhqk,rkhd->rqhd", probs, part, preferred_element_type=jnp.float32),
            ),
            shared,
        )

    start_mixed = (jnp.zeros((row_count, width, heads, head_dim), jnp.float32),)
    (mixed,), unused = over_blocks(weighted_sum, start_mixed, (), lengths, block_count)
    attended = mixed.reshape(tokens, model).astype(jnp.bfloat16)
    state = state + matmul(attended, output_weight)
    normed, scaled_conv, rstd_conv = norm_forward(state, gain_conv)
    act_conv = normed.astype(jnp.bfloat16)
    joined = matmul(act_conv, point_in)
    gate_sig = jax.nn.sigmoid(joined[:, model:])
    gated = (joined[:, :model] * gate_sig * valid_flat).reshape(row_count, width, model)
    rimmed = padded_2(gated.astype(jnp.bfloat16), (("tm", 1),), half).astype(gated.dtype)
    filtered = jnp.zeros_like(gated)
    for tap in range(depth_weight.shape[0]):
        filtered = filtered + depth_weight[tap] * rimmed[:, tap : tap + width]
    local_count = jnp.sum(valid)
    sums, count = lax.psum(
        (jnp.sum(filtered * valid_three, axis=(0, 1)), local_count), ("rows", "tm")
    )
    batch_mean = sums / count
    centered = (filtered - batch_mean) * valid_three
    batch_var = lax.psum(jnp.sum(centered * centered, axis=(0, 1)), ("rows", "tm")) / count
    rstd_batch = lax.rsqrt(batch_var + EPS)
    scaled_batch = ((filtered - batch_mean) * rstd_batch).reshape(tokens, model)
    normalized = scaled_batch * batch_scale + batch_shift
    act_batch = jax.nn.silu(normalized).astype(jnp.bfloat16)
    state = state + matmul(act_batch, point_out)
    state, kept_second = ffn_forward(state, gain_second, second_in, second_out)
    normed, scaled_final, rstd_final = norm_forward(state, gain_final)
    output = (normed * valid_flat).astype(jnp.bfloat16).reshape(row_count, width, model)
    grad, grad_gain_final = norm_backward(
        cotangent.astype(jnp.float32).reshape(tokens, model) * valid_flat,
        scaled_final,
        rstd_final,
        gain_final,
    )
    grad, grad_gain_second, grad_second_in, grad_second_out = ffn_backward(
        grad, kept_second, gain_second, second_in, second_out
    )
    d_branch = grad.astype(jnp.bfloat16)
    grad_point_out = weight_grad(act_batch, d_branch)
    d_normal = back_prop(d_branch, point_out) * silu_slope(normalized) * valid_flat
    grad_batch_shift, grad_batch_scale = lax.psum(
        (jnp.sum(d_normal, axis=0), jnp.sum(d_normal * scaled_batch, axis=0)), ("rows", "tm")
    )
    d_filtered = (
        valid_flat
        * (batch_scale * rstd_batch)
        * (d_normal - grad_batch_shift / count - scaled_batch * grad_batch_scale / count)
    )
    d_filtered = d_filtered.reshape(row_count, width, model)
    rimmed_grad = padded_2(d_filtered.astype(jnp.bfloat16), (("tm", 1),), half).astype(
        d_filtered.dtype
    )
    d_gated = jnp.zeros_like(gated)
    taps = []
    for tap in range(depth_weight.shape[0]):
        d_gated = (
            d_gated + depth_weight[tap] * rimmed_grad[:, 2 * half - tap : 2 * half - tap + width]
        )
        taps.append(jnp.sum(d_filtered * rimmed[:, tap : tap + width], axis=(0, 1)))
    grad_depth = jnp.stack(taps)
    d_gated = d_gated.reshape(tokens, model) * valid_flat
    d_joined = jnp.concatenate(
        [d_gated * gate_sig, d_gated * joined[:, :model] * gate_sig * (1.0 - gate_sig)], axis=1
    ).astype(jnp.bfloat16)
    grad_point_in = weight_grad(act_conv, d_joined)
    d_values, grad_gain_conv = norm_backward(
        back_prop(d_joined, point_in), scaled_conv, rstd_conv, gain_conv
    )
    grad = grad + d_values
    d_attend = grad.astype(jnp.bfloat16)
    grad_output = weight_grad(attended, d_attend)
    d_mixed = back_prop(d_attend, output_weight).astype(jnp.bfloat16)
    grad_heads = d_mixed.reshape(row_count, width, heads, head_dim)

    def probs_grad(block, first, last):
        begin = block * width
        return jnp.einsum(
            "rqhd,rkhd->rhqk",
            grad_heads,
            value_heads[first:last, begin : begin + width],
            preferred_element_type=jnp.float32,
        )

    def delta_step(carry, shared, block, first, last):
        return (
            (
                carry[0]
                + jnp.sum(probs_at(block, first, last) * probs_grad(block, first, last), axis=-1),
            ),
            shared,
        )

    (delta,), unused = over_blocks(
        delta_step, (jnp.zeros((row_count, heads, width), jnp.float32),), (), lengths, block_count
    )

    def grad_step(carry, shared, block, first, last):
        query_grads, key_grads, value_grads = carry
        begin = block * width
        rows_now = last - first
        probs = probs_at(block, first, last)
        d_scores = (
            probs * (probs_grad(block, first, last) - delta[first:last, :, :, None])
        ).astype(jnp.bfloat16)
        query_grads = (
            query_grads
            + jnp.einsum(
                "rhqk,rkhd->rqhd",
                d_scores,
                key_heads[first:last, begin : begin + width],
                preferred_element_type=jnp.float32,
            )
            * scale
        )
        key_part = (
            jnp.einsum("rhqk,rqhd->rkhd", d_scores, query_heads, preferred_element_type=jnp.float32)
            * scale
        )
        value_part = jnp.einsum(
            "rhqk,rqhd->rkhd",
            probs.astype(jnp.bfloat16),
            grad_heads,
            preferred_element_type=jnp.float32,
        )
        key_grads = key_grads.at[:, begin : begin + width].set(
            key_part.reshape(rows_now, width, model)
        )
        value_grads = value_grads.at[:, begin : begin + width].set(
            value_part.reshape(rows_now, width, model)
        )
        bias_grad = (
            shared[0]
            .at[:, :, begin : begin + width]
            .add(jnp.sum(d_scores.astype(jnp.float32), axis=0))
        )
        return ((query_grads, key_grads, value_grads), (bias_grad,))

    start_grads = (
        jnp.zeros((row_count, width, heads, head_dim), jnp.float32),
        jnp.zeros((row_count, frames, model), jnp.float32),
        jnp.zeros((row_count, frames, model), jnp.float32),
    )
    (query_grads, key_grads, value_grads), (bias_grad,) = over_blocks(
        grad_step,
        start_grads,
        (jnp.zeros((heads, width, frames), jnp.float32),),
        lengths,
        block_count,
    )
    own_keys, own_values = (
        lax.psum_scatter(
            key_grads.astype(jnp.bfloat16), "tm", scatter_dimension=1, tiled=True
        ).astype(jnp.float32),
        lax.psum_scatter(
            value_grads.astype(jnp.bfloat16), "tm", scatter_dimension=1, tiled=True
        ).astype(jnp.float32),
    )
    grad_table = lax.dot_general(
        diagonal_sums(bias_grad, width, frames),
        one_hot,
        (((1,), (0,)), ((), ())),
        precision=lax.Precision.HIGHEST,
    )
    query_low = query_grads.reshape(tokens, model).astype(jnp.bfloat16)
    key_low = own_keys.reshape(tokens, model).astype(jnp.bfloat16)
    value_low = own_values.reshape(tokens, model).astype(jnp.bfloat16)
    grad_query = weight_grad(act_attend, query_low)
    grad_key = weight_grad(act_attend, key_low)
    grad_value = weight_grad(act_attend, value_low)
    d_input = (
        back_prop(query_low, query_weight)
        + back_prop(key_low, key_weight)
        + back_prop(value_low, value_weight)
    )
    d_values, grad_gain_attend = norm_backward(d_input, scaled_attend, rstd_attend, gain_attend)
    grad = grad + d_values
    grad, grad_gain_first, grad_first_in, grad_first_out = ffn_backward(
        grad, kept_first, gain_first, first_in, first_out
    )
    grad_features = grad.astype(jnp.bfloat16).reshape(row_count, width, model)
    (
        grad_gain_final,
        grad_second_in,
        grad_second_out,
        grad_gain_second,
        grad_point_out,
        grad_point_in,
        grad_gain_conv,
        grad_gain_first,
        grad_first_in,
        grad_first_out,
        grad_gain_attend,
        grad_query,
        grad_key,
        grad_value,
        grad_output,
    ) = (
        lax.psum_scatter(grad_gain_final, "rows", scatter_dimension=0, tiled=True),
        lax.psum_scatter(grad_second_in, "rows", scatter_dimension=0, tiled=True),
        lax.psum_scatter(grad_second_out, "rows", scatter_dimension=0, tiled=True),
        lax.psum_scatter(grad_gain_second, "rows", scatter_dimension=0, tiled=True),
        lax.psum_scatter(grad_point_out, "rows", scatter_dimension=0, tiled=True),
        lax.psum_scatter(grad_point_in, "rows", scatter_dimension=0, tiled=True),
        lax.psum_scatter(grad_gain_conv, "rows", scatter_dimension=0, tiled=True),
        lax.psum_scatter(grad_gain_first, "rows", scatter_dimension=0, tiled=True),
        lax.psum_scatter(grad_first_in, "rows", scatter_dimension=0, tiled=True),
        lax.psum_scatter(grad_first_out, "rows", scatter_dimension=0, tiled=True),
        lax.psum_scatter(grad_gain_attend, "rows", scatter_dimension=0, tiled=True),
        lax.psum_scatter(grad_query, "rows", scatter_dimension=0, tiled=True),
        lax.psum_scatter(grad_key, "rows", scatter_dimension=0, tiled=True),
        lax.psum_scatter(grad_value, "rows", scatter_dimension=0, tiled=True),
        lax.psum_scatter(grad_output, "rows", scatter_dimension=0, tiled=True),
    )
    (
        grad_gain_final,
        grad_second_in,
        grad_second_out,
        grad_gain_second,
        grad_point_out,
        grad_point_in,
        grad_gain_conv,
        grad_gain_first,
        grad_first_in,
        grad_first_out,
        grad_gain_attend,
        grad_query,
        grad_key,
        grad_value,
        grad_output,
    ) = (
        lax.psum(grad_gain_final.astype(jnp.bfloat16), "tm").astype(jnp.float32),
        lax.psum(grad_second_in.astype(jnp.bfloat16), "tm").astype(jnp.float32),
        lax.psum(grad_second_out.astype(jnp.bfloat16), "tm").astype(jnp.float32),
        lax.psum(grad_gain_second.astype(jnp.bfloat16), "tm").astype(jnp.float32),
        lax.psum(grad_point_out.astype(jnp.bfloat16), "tm").astype(jnp.float32),
        lax.psum(grad_point_in.astype(jnp.bfloat16), "tm").astype(jnp.float32),
        lax.psum(grad_gain_conv.astype(jnp.bfloat16), "tm").astype(jnp.float32),
        lax.psum(grad_gain_first.astype(jnp.bfloat16), "tm").astype(jnp.float32),
        lax.psum(grad_first_in.astype(jnp.bfloat16), "tm").astype(jnp.float32),
        lax.psum(grad_first_out.astype(jnp.bfloat16), "tm").astype(jnp.float32),
        lax.psum(grad_gain_attend.astype(jnp.bfloat16), "tm").astype(jnp.float32),
        lax.psum(grad_query.astype(jnp.bfloat16), "tm").astype(jnp.float32),
        lax.psum(grad_key.astype(jnp.bfloat16), "tm").astype(jnp.float32),
        lax.psum(grad_value.astype(jnp.bfloat16), "tm").astype(jnp.float32),
        lax.psum(grad_output.astype(jnp.bfloat16), "tm").astype(jnp.float32),
    )
    grad_table, grad_depth = lax.psum((grad_table, grad_depth), ("rows", "tm"))
    return (
        output,
        grad_features,
        grad_gain_first,
        grad_first_in,
        grad_first_out,
        grad_gain_attend,
        grad_query,
        grad_key,
        grad_value,
        grad_output,
        grad_table,
        grad_gain_conv,
        grad_point_in,
        grad_depth,
        grad_batch_scale,
        grad_batch_shift,
        grad_point_out,
        grad_gain_second,
        grad_second_in,
        grad_second_out,
        grad_gain_final,
    )


def solution(mesh):
    in_specs = (
        P("rows", "tm", None),
        P("rows"),
        P(),
        P(),
        P(),
        P(),
        P(),
        P(),
        P(),
        P(),
        P(),
        P(),
        P(),
        P(),
        P(),
        P(),
        P(),
        P(),
        P(),
        P(),
        P(),
        P(),
        P("rows", "tm", None),
    )
    out_specs = (
        P("rows", "tm", None),
        P("rows", "tm", None),
        P("rows"),
        P("rows", None),
        P("rows", None),
        P("rows"),
        P("rows", None),
        P("rows", None),
        P("rows", None),
        P("rows", None),
        P(),
        P("rows"),
        P("rows", None),
        P(),
        P(),
        P(),
        P("rows", None),
        P("rows"),
        P("rows", None),
        P("rows", None),
        P("rows"),
    )
    return jax.shard_map(shards, mesh=mesh, in_specs=in_specs, out_specs=out_specs, check_vma=False)
```

profile of v0, /device:TPU:0, one launch (start us, length us, event | category | flops | bytes accessed | tf_op | source)
XLA Modules:
  0.0 2858.8 jit_solution(9737575555265240702)
XLA Ops:
  11.0 7.2 fusion.105
  30.3 10.4 tile.4
  40.7 16.6 slice.477
  57.3 17.6 reshape.1166
  75.0 39.5 %reshape.1122 = f32[8,384,1921]{2,1,0:T(8,128)} reshape(f32[5901312]{0:T(1024)} %reshape.1166) | data formatting | bytes 47210496 | tf_op jit(solution)/shard_map/reshape | solution.py:82
  114.5 13.7 fusion.120
  132.3 6.3 copy.230
  138.6 38.4 %slice.438 = f32[8,384,384]{1,2,0:T(8,128)} reverse(f32[8,384,384]{1,2,0:T(8,128)} %copy.230), dimensions={1} | reverse | bytes 9437184 | tf_op jit(solution)/shard_map/slice | solution.py:169
  177.1 6.0 copy.234
  183.1 38.4 %slice.444 = f32[8,384,384]{1,2,0:T(8,128)} reverse(f32[8,384,384]{1,2,0:T(8,128)} %copy.234), dimensions={1} | reverse | bytes 9437184 | tf_op jit(solution)/shard_map/slice | solution.py:169
  221.6 6.1 copy.232
  227.6 38.4 %slice.441 = f32[8,384,384]{1,2,0:T(8,128)} reverse(f32[8,384,384]{1,2,0:T(8,128)} %copy.232), dimensions={1} | reverse | bytes 9437184 | tf_op jit(solution)/shard_map/slice | solution.py:169
  266.0 6.1 copy.236
  272.1 38.9 %slice.447 = f32[8,384,384]{1,2,0:T(8,128)} reverse(f32[8,384,384]{1,2,0:T(8,128)} %copy.236), dimensions={1} | reverse | bytes 9437184 | tf_op jit(solution)/shard_map/slice | solution.py:169
  314.1 4.5 fusion.129
  330.3 4.9 copy.226
  335.2 4.0 fusion.57
  360.8 41.5 %all-reduce.13 = (f32[1024]{0:T(1024)S(1)}, f32[]{:T(128)}) all-reduce(f32[1024]{0:T(1024)S(1)} %get-tuple-element.228, f32[]{:T(128)} %fusion.95), channel_id=1, replica_groups=mesh['rows'=8,'tm'=4] {'rows','tm'}, use_global_device_ids=true, to_apply=%region_15.16 | all-reduce | flops 1025 | bytes 8200 | tf_op jit(solution)/shard_map/psum | solution.py:220
  404.6 40.8 %psum.156 = f32[1024]{0:T(1024)S(1)} all-reduce(f32[1024]{0:T(1024)S(1)} %multiply_reduce_fusion.12), channel_id=1, replica_groups=mesh['rows'=8,'tm'=4] {'rows','tm'}, use_global_device_ids=true, to_apply=%region_19.20 | all-reduce | flops 1024 | bytes 8192 | tf_op jit(solution)/shard_map/psum | solution.py:225
  449.7 6.2 fusion.109
  462.7 11.1 multiply_convert_fusion.1
  473.8 8.1 multiply_reduce_fusion.4
  486.9 39.7 %all-reduce.12 = (f32[1024]{0:T(1024)S(1)}, f32[1024]{0:T(1024)S(1)}) all-reduce(f32[1024]{0:T(1024)S(1)} %get-tuple-element.185, f32[1024]{0:T(1024)S(1)} %get-tuple-element.184), channel_id=1, replica_groups=mesh['rows'=8,'tm'=4] {'rows','tm'}, use_global_device_ids=true, to_apply=%region_31.32 | all-reduce | flops 2048 | bytes 16384 | tf_op jit(solution)/shard_map/psum | solution.py:246
  527.3 7.9 fusion.42
  538.0 4.1 collective-permute-done.3
  576.4 15.7 copy.224
  592.1 5.7 copy.263
  597.8 16.6 multiply_reduce_fusion.2
  614.5 5.7 multiply_convert_fusion.7
  623.0 7.7 pad_convert_fusion
  630.7 5.0 convert_dynamic-update-slice_fusion
  638.3 5.5 fusion.1
  646.2 4.9 fusion
  653.5 15.8 copy.222
  669.3 5.7 copy.264
  676.4 4.8 fusion.88
  709.1 4.1 reduce-scatter.37.cloned.1.call-done
  725.0 7.2 fusion.63
  733.6 14.1 fusion.91
  749.1 10.4 fusion.108
  769.0 8.3 fusion.92
  777.4 9.7 multiply_convert_fusion
  788.7 8.5 fusion.103
  797.3 7.4 reduce-scatter.31.cloned.1.call-done
  806.4 90.0 %reduce-scatter.27.cloned.1.call-done = f32[128,1024]{1,0:T(8,128)} async-done(((f32[1024,1024]{1,0:T(8,128)}), f32[128,1024]{1,0:T(8,128)}) %reduce-scatter.27.cloned.1.call-update) | async-done | bytes 524304 | tf_op jit(solution)/shard_map/reduce_scatter | solution.py:417
  898.2 89.6 %reduce-scatter.21.cloned.1.call-done = f32[128,1024]{1,0:T(8,128)} async-done(((f32[1024,1024]{1,0:T(8,128)}), f32[128,1024]{1,0:T(8,128)}) %reduce-scatter.21.cloned.1.call-update) | async-done | bytes 524304 | tf_op jit(solution)/shard_map/reduce_scatter | solution.py:414
  989.5 90.0 %reduce-scatter.25.cloned.1.call-done = f32[128,1024]{1,0:T(8,128)} async-done(((f32[1024,1024]{1,0:T(8,128)}), f32[128,1024]{1,0:T(8,128)}) %reduce-scatter.25.cloned.1.call-update) | async-done | bytes 524304 | tf_op jit(solution)/shard_map/reduce_scatter | solution.py:416
  1081.3 89.6 %reduce-scatter.23.cloned.1.call-done = f32[128,1024]{1,0:T(8,128)} async-done(((f32[1024,1024]{1,0:T(8,128)}), f32[128,1024]{1,0:T(8,128)}) %reduce-scatter.23.cloned.1.call-update) | async-done | bytes 524304 | tf_op jit(solution)/shard_map/reduce_scatter | solution.py:415
  1172.6 150.9 %reduce-scatter.29.cloned.1.call-done = f32[128,2048]{1,0:T(8,128)} async-done(((f32[1024,2048]{1,0:T(8,128)}), f32[128,2048]{1,0:T(8,128)}) %reduce-scatter.29.cloned.1.call-update) | async-done | bytes 1048592 | tf_op jit(solution)/shard_map/reduce_scatter | solution.py:408
  1325.6 283.0 %reduce-scatter.35.cloned.1.call-done = f32[512,1024]{1,0:T(8,128)} async-done(((f32[4096,1024]{1,0:T(8,128)}), f32[512,1024]{1,0:T(8,128)}) %reduce-scatter.35.cloned.1.call-update) | async-done | bytes 2097168 | tf_op jit(solution)/shard_map/reduce_scatter | solution.py:405
  1611.4 282.6 %reduce-scatter.33.cloned.1.call-done = f32[128,4096]{1,0:T(8,128)} async-done(((f32[1024,4096]{1,0:T(8,128)}), f32[128,4096]{1,0:T(8,128)}) %reduce-scatter.33.cloned.1.call-update) | async-done | bytes 2097168 | tf_op jit(solution)/shard_map/reduce_scatter | solution.py:404
  1896.7 282.4 %reduce-scatter.19.cloned.1.call-done = f32[512,1024]{1,0:T(8,128)} async-done(((f32[4096,1024]{1,0:T(8,128)}), f32[512,1024]{1,0:T(8,128)}) %reduce-scatter.19.cloned.1.call-update) | async-done | bytes 2097168 | tf_op jit(solution)/shard_map/reduce_scatter | solution.py:412
  2181.8 282.6 %reduce-scatter.17.cloned.1.call-done = f32[128,4096]{1,0:T(8,128)} async-done(((f32[1024,4096]{1,0:T(8,128)}), f32[128,4096]{1,0:T(8,128)}) %reduce-scatter.17.cloned.1.call-update) | async-done | bytes 2097168 | tf_op jit(solution)/shard_map/reduce_scatter | solution.py:411
  2469.1 151.2 %rev.4 = f32[8,384,1536]{1,2,0:T(8,128)} reverse(f32[8,384,1536]{1,2,0:T(8,128)} %get-tuple-element.218), dimensions={1} | reverse | bytes 37748736 | tf_op jit(solution)/shard_map/rev | solution.py:89
  2620.3 18.7 copy.237
  2639.0 15.6 pad.41.clone
  2654.6 37.3 %reshape.1168 = f32[5901312]{0:T(1024)} reshape(f32[8,384,1921]{2,1,0:T(8,128)} %pad.41.clone) | data formatting | bytes 47210496
  2691.9 22.3 reshape.1144
  2714.2 16.2 pad.42
  2730.4 9.2 reduce_sum.447
  2740.2 39.8 %all-reduce.11 = (f32[8,64]{1,0:T(8,128)}, f32[5,1024]{1,0:T(8,128)}) all-reduce(f32[8,64]{1,0:T(8,128)S(1)} %fusion.65, f32[5,1024]{1,0:T(8,128)S(1)} %stack.23), channel_id=1, replica_groups=mesh['rows'=8,'tm'=4] {'rows','tm'}, use_global_device_ids=true, to_apply=%region_63.64 | all-reduce | flops 5632 | bytes 45056 | tf_op jit(solution)/shard_map/psum | solution.py:452
  2780.0 9.1 fusion.18
  2789.2 36.9 %all-reduce.14 = (bf16[1024]{0:T(1024)(128)(2,1)S(1)}, bf16[1024]{0:T(1024)(128)(2,1)S(1)}, bf16[1024]{0:T(1024)(128)(2,1)S(1)}, bf16[1024]{0:T(1024)(128)(2,1)S(1)}, bf16[1024]{0:T(1024)(128)(2,1)S(1)}) all-reduce(f32[1024]{0:T(1024)S(1)} %get-tuple-element.178, ...), channel_id=6, replica_groups=mesh['rows'=8,'tm'=4] {'rows'}, use_global_device_ids=true, to_apply=%region_45.46.clone | all-reduce | flops 5120 | bytes 30720
  2826.4 5.9 all-reduce.15
  (518 shorter events, 219.2 us)
Async XLA Ops:
  7.2 438.9 %copy-start = (bf16[1024,1024]{1,0:T(8,128)(2,1)S(1)}, bf16[1024,1024]{1,0:T(8,128)(2,1)}, u32[]{:S(2)}) copy-start(bf16[1024,1024]{1,0:T(8,128)(2,1)} %param.64) | copy-start | bytes 6291460
  7.2 303.9 %all-gather.7.cloned.1.call-start = ((), (), s32[]{:S(2)}) async-start(), calls=%async_computation.23 | async-start | bytes 3932160 | tf_op jit(solution)/shard_map/all_gather | solution.py:149
  8.7 9.4 slice-start.28
  11.0 7.2 copy-start.35
  11.0 7.2 slice-start.29
  24.0 104.2 %copy-start.13 = (bf16[384,1024]{1,0:T(8,128)(2,1)}, bf16[384,1024]{1,0:T(8,128)(2,1)S(1)}, u32[]{:S(2)}) copy-start(bf16[384,1024]{1,0:T(8,128)(2,1)S(1)} %multiply_convert_fusion.18) | copy-start | bytes 2359300
  25.9 304.4 %all-gather.5.cloned.1.call-start = ((), (), s32[]{:S(2)}) async-start(), calls=%async_computation.22 | async-start | bytes 3932160 | tf_op jit(solution)/shard_map/all_gather | solution.py:150
  29.4 669.6 %reduce-scatter.39.cloned.1.call-start = ((), (), s32[]{:S(2)}) async-start(), calls=%async_computation.25 | async-start | bytes 3932160
  29.6 11.1 copy-start.107
  114.5 13.7 copy-start.117
  132.3 193.0 %copy-start.3 = (bf16[384,1024]{0,1:T(8,128)(2,1)}, bf16[384,1024]{0,1:T(8,128)(2,1)S(1)}, u32[]{:S(2)}) copy-start(bf16[384,1024]{0,1:T(8,128)(2,1)S(1)} %copy.238) | copy-start | bytes 2359300
  314.0 11.3 copy-start.39
  318.6 8.2 copy-start.8
  320.0 7.7 copy-start.6
  330.3 8.9 slice-start.4
  351.1 4.3 collective-permute-start
  353.4 5.0 collective-permute-start.1
  360.8 84.6 %copy-start.114 = (f32[1024]{0:T(1024)S(1)}, f32[1024]{0:T(1024)}, u32[]{:S(2)}) copy-start(f32[1024]{0:T(1024)} %param.62) | copy-start | bytes 12292
  360.8 85.3 %copy-start.121 = (f32[1024]{0:T(1024)S(1)}, f32[1024]{0:T(1024)}, u32[]{:S(2)}) copy-start(f32[1024]{0:T(1024)} %param.63) | copy-start | bytes 12292
  446.1 9.9 slice-start.26
  449.4 32.6 %copy-start.26 = (f32[384,1024]{1,0:T(8,128)}, f32[384,1024]{1,0:T(8,128)S(1)}, u32[]{:S(2)}) copy-start(f32[384,1024]{1,0:T(8,128)S(1)} %get-tuple-element.266) | copy-start | bytes 4718596
  449.4 32.6 %copy-start.78 = (f32[384]{0:T(512)}, f32[384]{0:T(512)S(1)}, u32[]{:S(2)}) copy-start(f32[384]{0:T(512)S(1)} %broadcast_multiply_fusion.11) | copy-start | bytes 4612
  449.7 32.2 %copy-start.82 = (f32[384]{0:T(512)}, f32[384]{0:T(512)S(1)}, u32[]{:S(2)}) copy-start(f32[384]{0:T(512)S(1)} %add_rsqrt_fusion.2) | copy-start | bytes 4612
  459.7 22.3 copy-start.28
  459.7 22.3 copy-start.90
  461.4 20.6 copy-start.92
  462.7 19.3 copy-start.103
  462.7 19.3 copy-start.105
  473.8 8.2 copy-start.52
  526.6 8.5 copy-start.110
  526.6 8.5 copy-start.113
  527.3 15.0 copy-start.25
  535.2 2.8 collective-permute-start.2
  536.5 5.6 collective-permute-start.3
  597.8 115.4 %reduce-scatter.37.cloned.1.call-start = ((), (), s32[]{:S(2)}) async-start(), calls=%async_computation.24 | async-start | bytes 3932160
  620.2 10.5 slice-start.10
  623.0 7.7 slice-start.11
  623.0 15.1 slice-start.8
  623.0 15.1 slice-start.18
  630.7 7.4 slice-start.9
  630.7 7.6 slice-start.19
  635.7 10.5 slice-start.2
  635.7 10.5 slice-start.16
  638.2 7.9 slice-start.3
  638.3 7.9 slice-start.17
  675.0 129.7 %reduce-scatter.31.cloned.1.call-start = ((), (), s32[]{:S(2)}) async-start(), calls=%async_computation.19 | async-start | bytes 4718592 | tf_op jit(solution)/shard_map/reduce_scatter | solution.py:407
  681.2 215.2 %reduce-scatter.27.cloned.1.call-start = ((), (), s32[]{:S(2)}) async-start(), calls=%async_computation.17 | async-start | bytes 4718592 | tf_op jit(solution)/shard_map/reduce_scatter | solution.py:417
  686.2 301.5 %reduce-scatter.21.cloned.1.call-start = ((), (), s32[]{:S(2)}) async-start(), calls=%async_computation.14 | async-start | bytes 4718592 | tf_op jit(solution)/shard_map/reduce_scatter | solution.py:414
  699.0 380.5 %reduce-scatter.25.cloned.1.call-start = ((), (), s32[]{:S(2)}) async-start(), calls=%async_computation.16 | async-start | bytes 4718592 | tf_op jit(solution)/shard_map/reduce_scatter | solution.py:416
  709.0 461.8 %reduce-scatter.23.cloned.1.call-start = ((), (), s32[]{:S(2)}) async-start(), calls=%async_computation.15 | async-start | bytes 4718592 | tf_op jit(solution)/shard_map/reduce_scatter | solution.py:415
  723.6 600.0 %reduce-scatter.29.cloned.1.call-start = ((), (), s32[]{:S(2)}) async-start(), calls=%async_computation.18 | async-start | bytes 9437184 | tf_op jit(solution)/shard_map/reduce_scatter | solution.py:408
  732.2 876.4 %reduce-scatter.35.cloned.1.call-start = ((), (), s32[]{:S(2)}) async-start(), calls=%async_computation.21 | async-start | bytes 18874368 | tf_op jit(solution)/shard_map/reduce_scatter | solution.py:405
  747.7 1146.3 %reduce-scatter.33.cloned.1.call-start = ((), (), s32[]{:S(2)}) async-start(), calls=%async_computation.20 | async-start | bytes 18874368 | tf_op jit(solution)/shard_map/reduce_scatter | solution.py:404
  759.5 1419.6 %reduce-scatter.19.cloned.1.call-start = ((), (), s32[]{:S(2)}) async-start(), calls=%async_computation.13 | async-start | bytes 18874368 | tf_op jit(solution)/shard_map/reduce_scatter | solution.py:412
  777.3 11.4 copy-start.36
  777.3 11.4 copy-start.71
  777.3 11.4 copy-start.77
  777.3 11.4 copy-start.81
  777.3 1687.2 %reduce-scatter.17.cloned.1.call-start = ((), (), s32[]{:S(2)}) async-start(), calls=%async_computation.12 | async-start | bytes 18874368 | tf_op jit(solution)/shard_map/reduce_scatter | solution.py:411
  797.2 2041.0 %all-reduce.19.cloned.1.call-start = ((), (), s32[]{:S(2)}) async-start(), calls=%async_computation.26 | async-start | bytes 12058624 | tf_op jit(solution)/shard_map/psum | solution.py:444
  2730.4 9.2 copy-start.108
  2780.0 9.2 copy-start.96
  2780.0 9.2 copy-start.111
  2780.0 9.2 copy-start.112
  (112 other events, 294.1 us)
Sparse Core Ops, SparseCore 0:
  26.0 31.2 all-gather.6
  59.4 28.5 all-gather.4
  597.9 38.2 reduce-scatter.38
  675.1 38.0 reduce-scatter.36
  716.7 87.9 reduce-scatter.30
  808.6 87.8 reduce-scatter.26
  900.0 87.6 reduce-scatter.20
  991.8 87.6 reduce-scatter.24
  1083.2 87.6 reduce-scatter.22
  1174.8 148.7 reduce-scatter.28
  1327.3 281.2 reduce-scatter.34
  1612.8 281.1 reduce-scatter.32
  1897.8 281.2 reduce-scatter.18
  2183.2 281.1 reduce-scatter.16
  2469.1 116.0 all-reduce.18
where the time goes:
time: 2890 us; the launch traced here: 2860 us
  waiting for transfers between devices  1660 us (57%)
  local copies, waits for them, and re-layouts  650 us (22%)
  matrix products  212 us (7%)
  blocking collectives  205 us (7%)
  other arithmetic  109 us (4%)
    reduce_scatter x1, waiting for transfers between devices, shards(): lax.psum_scatter(grad_second_out, 'rows', scatter_dimension=0, tiled=True)  283 us
    reduce_scatter x1, waiting for transfers between devices, shards(): lax.psum_scatter(grad_first_in, 'rows', scatter_dimension=0, tiled=True)  283 us
    reduce_scatter x1, waiting for transfers between devices, shards(): lax.psum_scatter(grad_second_in, 'rows', scatter_dimension=0, tiled=True)  283 us
    reduce_scatter x1, waiting for transfers between devices, shards(): lax.psum_scatter(grad_first_out, 'rows', scatter_dimension=0, tiled=True)  282 us
    unnamed x336, local copies, waits for them, and re-layouts  193 us
    slice x5, local copies, waits for them, and re-layouts, scores_at(): scores = scores + bias[None, :, :, begin:begin + width]  168 us
    rev x1, local copies, waits for them, and re-layouts, diagonal_sums(): hankel = matrix[:, ::-1, :]  151 us
    reduce_scatter x1, waiting for transfers between devices, shards(): lax.psum_scatter(grad_point_in, 'rows', scatter_dimension=0, tiled=True)  151 us
  transfers between devices with their start and end apart: 19, of which 13 were waited for; matrix products, arithmetic and copies ran while one was open for 27% of the time, Pallas kernels for 0%

commit v1 on v0

v1 whole, which is shorter than its diff:
```python
import functools

import jax
import jax.numpy as jnp
from jax import lax
from jax.experimental import pallas as pl
from jax.experimental.pallas import tpu as pltpu
from jax.sharding import PartitionSpec as P

EPS = 1e-05
NEGATIVE = -1e30
LANES = 128
QUERY_TILE = 256
VMEM_LIMIT = 56 * 1024 * 1024


def swap(value, axis, bit):
    count = lax.axis_size(axis)
    return lax.ppermute(value, axis, [(i, i ^ bit) for i in range(count)])


def matmul(left, right):
    return jnp.dot(left, right, preferred_element_type=jnp.float32)


def back_prop(grad, weight):
    return lax.dot_general(
        grad, weight, (((1,), (1,)), ((), ())), preferred_element_type=jnp.float32
    )


def weight_grad(inputs, grad):
    return lax.dot_general(
        inputs, grad, (((0,), (0,)), ((), ())), preferred_element_type=jnp.float32
    ).astype(jnp.bfloat16)


def norm_forward(values, gain):
    mean = jnp.mean(values, axis=-1, keepdims=True)
    centered = values - mean
    rstd = lax.rsqrt(jnp.mean(centered * centered, axis=-1, keepdims=True) + EPS)
    scaled = centered * rstd
    return (scaled * gain, scaled, rstd)


def norm_backward(grad, scaled, rstd, gain):
    weighted = grad * gain
    inner = weighted - jnp.mean(weighted, axis=-1, keepdims=True)
    inner = inner - scaled * jnp.mean(weighted * scaled, axis=-1, keepdims=True)
    return (rstd * inner, jnp.sum(grad * scaled, axis=0))


def silu_slope(hidden):
    sigma = jax.nn.sigmoid(hidden)
    return sigma * (1.0 + hidden * (1.0 - sigma))


def ordered(first_is_lower, mine, other):
    low = jnp.where(first_is_lower, mine, other)
    high = jnp.where(first_is_lower, other, mine)
    return jnp.concatenate([low, high], axis=0)


def mesh_sum(value):
    for axis in ("tm", "rows"):
        bit = 1
        while bit < lax.axis_size(axis):
            value = value + swap(value, axis, bit)
            bit *= 2
    return value


def mesh_moments(count, mean, spread):
    for axis in ("tm", "rows"):
        bit = 1
        while bit < lax.axis_size(axis):
            sent = jnp.concatenate([mean[None], spread[None], jnp.broadcast_to(count, (1, mean.shape[0]))])
            got = swap(sent, axis, bit)
            other_mean, other_spread, other_count = got[0], got[1], got[2]
            total = count + other_count
            safe = jnp.maximum(total, 1.0)
            gap = other_mean - mean
            spread = spread + other_spread + gap * gap * (count * other_count / safe)
            mean = (count * mean + other_count * other_mean) / safe
            count = total
            bit *= 2
    return (count, mean, spread)


def reduce_rows(partial):
    size = lax.axis_size("rows")
    place = lax.axis_index("rows")
    left = partial.reshape(size, partial.shape[0] // size, partial.shape[1])
    bit = 1
    while left.shape[0] > 1:
        pairs = left.reshape(left.shape[0] // 2, 2, left.shape[1], left.shape[2])
        mine = (place // bit) % 2
        keep = lax.dynamic_index_in_dim(pairs, mine, 1, keepdims=False)
        send = lax.dynamic_index_in_dim(pairs, 1 - mine, 1, keepdims=False)
        got = swap(send, "rows", bit)
        left = (keep.astype(jnp.float32) + got.astype(jnp.float32)).astype(jnp.bfloat16)
        bit *= 2
    return left[0]


def spread_tm(piece):
    near = swap(piece, "tm", 1)
    far = swap(piece, "tm", 2)
    return [piece, near, far, swap(far, "tm", 1)]


def take_kernel(place, source, target):
    target[...] = source[...]


def take_columns(weight, groups, place, parts):
    model, total = weight.shape
    block = total // groups // parts
    if block % LANES:
        cut = weight.reshape(model, groups, parts, block)
        return lax.dynamic_index_in_dim(cut, place, 2, keepdims=False).reshape(model, -1)
    return pl.pallas_call(
        take_kernel,
        out_shape=jax.ShapeDtypeStruct((model, total // parts), weight.dtype),
        grid_spec=pltpu.PrefetchScalarGridSpec(
            num_scalar_prefetch=1,
            grid=(groups,),
            in_specs=[pl.BlockSpec((model, block), lambda g, at: (0, g * parts + at[0]))],
            out_specs=pl.BlockSpec((model, block), lambda g, at: (0, g)),
        ),
        name="take_columns",
    )(place.reshape(1), weight)


def take_rows(weight, groups, place, parts):
    total, model = weight.shape
    cut = weight.reshape(groups, parts, total // groups // parts, model)
    return lax.dynamic_index_in_dim(cut, place, 1, keepdims=False).reshape(-1, model)


def lay_kernel(widths, groups, places, *refs):
    parts = 4
    pieces, targets = refs[:parts], refs[parts:]
    for k in range(parts):
        begin = 0
        for width, target in zip(widths, targets, strict=True):
            block = width // groups
            for g in range(groups):
                at = pl.multiple_of((g * parts + places[k]) * block, LANES)
                source = pieces[k][:, begin + g * block : begin + (g + 1) * block]
                target[:, pl.ds(at, block)] = source.astype(jnp.float32)
            begin += width


def lay_columns(pieces, widths, groups, places):
    rows = pieces[0].shape[0]
    parts = len(pieces)
    if any((width // groups) % LANES for width in widths):
        outs, begin = [], 0
        stacked = jnp.zeros((parts, *pieces[0].shape), pieces[0].dtype)
        for k in range(parts):
            stacked = lax.dynamic_update_index_in_dim(stacked, pieces[k], places[k], 0)
        for width in widths:
            cut = stacked[:, :, begin : begin + width].reshape(parts, rows, groups, width // groups)
            outs.append(cut.transpose(1, 2, 0, 3).reshape(rows, parts * width).astype(jnp.float32))
            begin += width
        return outs
    return pl.pallas_call(
        functools.partial(lay_kernel, widths, groups),
        out_shape=[jax.ShapeDtypeStruct((rows, parts * width), jnp.float32) for width in widths],
        grid_spec=pltpu.PrefetchScalarGridSpec(
            num_scalar_prefetch=1,
            grid=(1,),
            in_specs=[pl.BlockSpec(p.shape, lambda i, at: (0, 0)) for p in pieces],
            out_specs=[pl.BlockSpec((rows, parts * width), lambda i, at: (0, 0)) for width in widths],
        ),
        compiler_params=pltpu.CompilerParams(vmem_limit_bytes=VMEM_LIMIT),
        name="lay_columns",
    )(places, *pieces)


def skew_kernel(line, out):
    length = line.shape[-1]
    width = out.shape[-1]
    spread = jnp.broadcast_to(line[0], (LANES, length))
    rolled = pltpu.roll(spread, length - (LANES - 1), 1, stride=1, stride_axis=0)
    out[0] = rolled[:, :width]


def skewed(lines):
    heads, _, length = lines.shape
    width = length - LANES
    return pl.pallas_call(
        skew_kernel,
        out_shape=jax.ShapeDtypeStruct((heads, LANES, width), jnp.float32),
        grid=(heads,),
        in_specs=[pl.BlockSpec((1, 1, length), lambda h: (h, 0, 0))],
        out_specs=pl.BlockSpec((1, LANES, width), lambda h: (h, 0, 0)),
        name="bias_rows",
    )(lines)


def attend_kernel(scale, at, q_ref, k_ref, v_ref, bias_ref, out_ref, lse_ref, vt_ref, s_ref, p_ref):
    tile = q_ref.shape[0]
    blocks = k_ref.shape[0] // LANES
    length = at[blocks * 2]

    @pl.when(pl.program_id(1) == 0)
    def _():
        vt_ref[...] = v_ref[...].T

    begin = pl.program_id(1) * tile
    s_ref[...] = lax.dot_general(
        k_ref[...], q_ref[...], (((1,), (1,)), ((), ())), preferred_element_type=jnp.float32
    )
    frame = lax.broadcasted_iota(jnp.int32, (LANES, tile), 0)
    top = jnp.full((1, tile), NEGATIVE, jnp.float32)
    for b in range(blocks):
        lanes = pl.ds(pl.multiple_of(at[b] + begin, LANES), tile)
        s = s_ref[b * LANES : (b + 1) * LANES] * scale + bias_ref[0, :, lanes]
        s = jnp.where(frame < length - at[blocks + b], s, NEGATIVE)
        s_ref[b * LANES : (b + 1) * LANES] = s
        top = jnp.maximum(top, jnp.max(s, axis=0, keepdims=True))
    total = jnp.zeros((1, tile), jnp.float32)
    for b in range(blocks):
        p = jnp.exp(s_ref[b * LANES : (b + 1) * LANES] - top)
        total = total + jnp.sum(p, axis=0, keepdims=True)
        p_ref[b * LANES : (b + 1) * LANES] = p.astype(jnp.bfloat16)
    mixed = jnp.dot(vt_ref[...], p_ref[...], preferred_element_type=jnp.float32) / total
    out_ref[...] = mixed.T.astype(jnp.bfloat16)
    lse_ref[0] = top + jnp.log(total)


def attend(at, query, keyval, bias, heads, head_dim):
    queries, keys = query.shape[0], keyval.shape[0]
    tile = QUERY_TILE
    width = bias.shape[-1]
    grid_spec = pltpu.PrefetchScalarGridSpec(
        num_scalar_prefetch=1,
        grid=(heads, queries // tile),
        in_specs=[
            pl.BlockSpec((tile, head_dim), lambda h, i, at: (i, h)),
            pl.BlockSpec((keys, head_dim), lambda h, i, at: (0, h)),
            pl.BlockSpec((keys, head_dim), lambda h, i, at: (0, heads + h)),
            pl.BlockSpec((1, LANES, width), lambda h, i, at: (h, 0, 0)),
        ],
        out_specs=[
            pl.BlockSpec((tile, head_dim), lambda h, i, at: (i, h)),
            pl.BlockSpec((1, 1, tile), lambda h, i, at: (h, 0, i)),
        ],
        scratch_shapes=[
            pltpu.VMEM((head_dim, keys), jnp.bfloat16),
            pltpu.VMEM((keys, tile), jnp.float32),
            pltpu.VMEM((keys, tile), jnp.bfloat16),
        ],
    )
    return pl.pallas_call(
        functools.partial(attend_kernel, head_dim ** (-0.5)),
        out_shape=[
            jax.ShapeDtypeStruct((queries, heads * head_dim), jnp.bfloat16),
            jax.ShapeDtypeStruct((heads, 1, queries), jnp.float32),
        ],
        grid_spec=grid_spec,
        compiler_params=pltpu.CompilerParams(vmem_limit_bytes=VMEM_LIMIT),
        cost_estimate=pl.CostEstimate(
            flops=4 * heads * queries * keys * head_dim,
            transcendentals=heads * queries * keys,
            bytes_accessed=4 * heads * LANES * width + 4 * heads * head_dim * (queries + keys),
        ),
        name="attend",
    )(at, query, keyval, keyval, bias)


def attend_back_kernel(
    scale, at, q_ref, k_ref, v_ref, do_ref, lse_ref, bias_ref,
    dq_ref, dk_ref, dv_ref, line_ref,
    kt_ref, s_ref, dp_ref, p_ref, ds_ref, dk_sum, dv_sum, skew_ref,
):
    tile = q_ref.shape[0]
    blocks = k_ref.shape[0] // LANES
    length = at[blocks * 2]

    @pl.when(pl.program_id(1) == 0)
    def _():
        kt_ref[...] = k_ref[...].T
        dk_sum[...] = jnp.zeros_like(dk_sum)
        dv_sum[...] = jnp.zeros_like(dv_sum)
        skew_ref[...] = jnp.zeros_like(skew_ref)

    begin = pl.program_id(1) * tile
    s_ref[...] = lax.dot_general(
        k_ref[...], q_ref[...], (((1,), (1,)), ((), ())), preferred_element_type=jnp.float32
    )
    dp_ref[...] = lax.dot_general(
        v_ref[...], do_ref[...], (((1,), (1,)), ((), ())), preferred_element_type=jnp.float32
    )
    frame = lax.broadcasted_iota(jnp.int32, (LANES, tile), 0)
    lse = lse_ref[0]
    delta = jnp.zeros((1, tile), jnp.float32)
    for b in range(blocks):
        rows = slice(b * LANES, (b + 1) * LANES)
        lanes = pl.ds(pl.multiple_of(at[b] + begin, LANES), tile)
        s = s_ref[rows] * scale + bias_ref[0, :, lanes]
        s = jnp.where(frame < length - at[blocks + b], s, NEGATIVE)
        p = jnp.exp(s - lse)
        s_ref[rows] = p
        p_ref[rows] = p.astype(jnp.bfloat16)
        delta = delta + jnp.sum(p * dp_ref[rows], axis=0, keepdims=True)
    for b in range(blocks):
        rows = slice(b * LANES, (b + 1) * LANES)
        lanes = pl.ds(pl.multiple_of(at[b] + begin, LANES), tile)
        ds = (s_ref[rows] * (dp_ref[rows] - delta)).astype(jnp.bfloat16)
        ds_ref[rows] = ds
        skew_ref[:, lanes] += ds.astype(jnp.float32)
    dv_sum[...] += jnp.dot(p_ref[...], do_ref[...], preferred_element_type=jnp.float32)
    dk_sum[...] += jnp.dot(ds_ref[...], q_ref[...], preferred_element_type=jnp.float32)
    dq = jnp.dot(kt_ref[...], ds_ref[...], preferred_element_type=jnp.float32) * scale
    dq_ref[...] = dq.T.astype(jnp.bfloat16)

    @pl.when(pl.program_id(1) == pl.num_programs(1) - 1)
    def _():
        dk_ref[...] = (dk_sum[...] * scale).astype(jnp.bfloat16)
        dv_ref[...] = dv_sum[...].astype(jnp.bfloat16)
        lines = jnp.concatenate([skew_ref[...], jnp.zeros((LANES, LANES), jnp.float32)], axis=1)
        count = LANES // 2
        while count >= 8:
            lines = lines[count:] + pltpu.roll(lines[:count], count, 1)
            count //= 2
        line_ref[0] = lines


def attend_back(at, query, keyval, grad, lse, bias, heads, head_dim):
    queries, keys = query.shape[0], keyval.shape[0]
    tile = QUERY_TILE
    width = bias.shape[-1]
    grid_spec = pltpu.PrefetchScalarGridSpec(
        num_scalar_prefetch=1,
        grid=(heads, queries // tile),
        in_specs=[
            pl.BlockSpec((tile, head_dim), lambda h, i, at: (i, h)),
            pl.BlockSpec((keys, head_dim), lambda h, i, at: (0, h)),
            pl.BlockSpec((keys, head_dim), lambda h, i, at: (0, heads + h)),
            pl.BlockSpec((tile, head_dim), lambda h, i, at: (i, h)),
            pl.BlockSpec((1, 1, tile), lambda h, i, at: (h, 0, i)),
            pl.BlockSpec((1, LANES, width), lambda h, i, at: (h, 0, 0)),
        ],
        out_specs=[
            pl.BlockSpec((tile, head_dim), lambda h, i, at: (i, h)),
            pl.BlockSpec((keys, head_dim), lambda h, i, at: (0, h)),
            pl.BlockSpec((keys, head_dim), lambda h, i, at: (0, h)),
            pl.BlockSpec((1, 8, width + LANES), lambda h, i, at: (h, 0, 0)),
        ],
        scratch_shapes=[
            pltpu.VMEM((head_dim, keys), jnp.bfloat16),
            pltpu.VMEM((keys, tile), jnp.float32),
            pltpu.VMEM((keys, tile), jnp.float32),
            pltpu.VMEM((keys, tile), jnp.bfloat16),
            pltpu.VMEM((keys, tile), jnp.bfloat16),
            pltpu.VMEM((keys, head_dim), jnp.float32),
            pltpu.VMEM((keys, head_dim), jnp.float32),
            pltpu.VMEM((LANES, width), jnp.float32),
        ],
    )
    return pl.pallas_call(
        functools.partial(attend_back_kernel, head_dim ** (-0.5)),
        out_shape=[
            jax.ShapeDtypeStruct((queries, heads * head_dim), jnp.bfloat16),
            jax.ShapeDtypeStruct((keys, heads * head_dim), jnp.bfloat16),
            jax.ShapeDtypeStruct((keys, heads * head_dim), jnp.bfloat16),
            jax.ShapeDtypeStruct((heads, 8, width + LANES), jnp.float32),
        ],
        grid_spec=grid_spec,
        compiler_params=pltpu.CompilerParams(vmem_limit_bytes=VMEM_LIMIT),
        cost_estimate=pl.CostEstimate(
            flops=10 * heads * queries * keys * head_dim,
            transcendentals=heads * queries * keys,
            bytes_accessed=4 * heads * LANES * width + 8 * heads * head_dim * (queries + keys),
        ),
        name="attend_back",
    )(at, query, keyval, keyval, grad, lse, bias)


def ffn_forward(values, gain, weight_in, weight_out):
    normed, scaled, rstd = norm_forward(values, gain)
    act_in = normed.astype(jnp.bfloat16)
    hidden = matmul(act_in, weight_in)
    act_mid = jax.nn.silu(hidden).astype(jnp.bfloat16)
    slope = silu_slope(hidden).astype(jnp.bfloat16)
    return (values + 0.5 * matmul(act_mid, weight_out), (act_in, slope, scaled, rstd))


def ffn_backward(grad, kept, gain, weight_in, weight_out):
    act_in, slope, scaled, rstd = kept
    d_branch = (0.5 * grad).astype(jnp.bfloat16)
    d_hidden = (back_prop(d_branch, weight_out) * slope.astype(jnp.float32)).astype(jnp.bfloat16)
    d_values, grad_gain = norm_backward(back_prop(d_hidden, weight_in), scaled, rstd, gain)
    return (grad + d_values, grad_gain, d_branch)


def ffn_again(act_all, part_in):
    hidden = matmul(act_all, part_in)
    return (jax.nn.silu(hidden).astype(jnp.bfloat16), silu_slope(hidden).astype(jnp.bfloat16))


def ffn_weight_grads(act_all, again, branch_all, part_out):
    act_mid, slope = again
    grad_out = reduce_rows(weight_grad(act_mid, branch_all))
    d_hidden = (back_prop(branch_all, part_out) * slope.astype(jnp.float32)).astype(jnp.bfloat16)
    grad_in = reduce_rows(weight_grad(act_all, d_hidden))
    return (spread_tm(grad_in), spread_tm(grad_out))


def shards(
    features,
    lengths,
    buckets,
    gain_first,
    first_in,
    first_out,
    gain_attend,
    query_weight,
    key_weight,
    value_weight,
    output_weight,
    bias_table,
    gain_conv,
    point_in,
    depth_weight,
    batch_scale,
    batch_shift,
    point_out,
    gain_second,
    second_in,
    second_out,
    gain_final,
    cotangent,
):
    row_count, width, model = features.shape
    tokens = row_count * width
    heads, bucket_count = bias_table.shape
    head_dim = model // heads
    parts = lax.axis_size("tm")
    groups = lax.axis_size("rows")
    frames = width * parts
    half = depth_weight.shape[0] // 2
    taps = depth_weight.shape[0]
    place = lax.axis_index("tm")
    row_place = lax.axis_index("rows")
    side = place % 2
    far = place // 2
    is_low = side == 0
    offset = place * width
    near_heads = heads // 2
    near_width = near_heads * head_dim
    pair = 2 * width
    valid_flat = ((offset + jnp.arange(width)) < lengths[0]).astype(jnp.float32).reshape(tokens, 1)

    def near_half(array, axis, index):
        size = array.shape[axis] // 2
        return lax.dynamic_slice_in_dim(array, index * size, size, axis)

    near_table = lax.dynamic_slice_in_dim(bias_table, side * near_heads, near_heads, 0)
    span = pair + frames
    turned = jnp.pad(buckets[::-1], (0, 1), constant_values=-1)
    window = lax.dynamic_slice_in_dim(turned, far * pair, span, 0)
    one_hot = (window[:, None] == jnp.arange(bucket_count)[None, :]).astype(jnp.float32)
    bias_lines = lax.dot_general(
        near_table, one_hot, (((1,), (1,)), ((), ())), precision=lax.Precision.HIGHEST
    )
    bias = skewed(bias_lines[:, None, :])
    key_blocks = frames // LANES
    block = jnp.arange(key_blocks)
    block = (block + far * (key_blocks // 2)) % key_blocks
    at = jnp.concatenate(
        [frames - LANES - LANES * block, LANES * block, lengths[:1]]
    ).astype(jnp.int32)

    state = features.astype(jnp.float32).reshape(tokens, model)
    state, kept_first = ffn_forward(state, gain_first, first_in, first_out)

    normed, scaled_attend, rstd_attend = norm_forward(state, gain_attend)
    act_attend = normed.astype(jnp.bfloat16)
    act_near, act_far = swap(act_attend, "tm", 1), swap(act_attend, "tm", 2)
    act_pair = ordered(is_low, act_attend, act_near)
    act_all = jnp.concatenate([act_pair, ordered(is_low, act_far, swap(act_far, "tm", 1))], axis=0)
    near_query = near_half(query_weight, 1, side)
    near_keyval = jnp.concatenate(
        [near_half(key_weight, 1, side), near_half(value_weight, 1, side)], axis=1
    )
    query = matmul(act_pair, near_query).astype(jnp.bfloat16)
    keyval = matmul(act_all, near_keyval).astype(jnp.bfloat16)
    mixed, lse = attend(at, query, keyval, bias, near_heads, head_dim)
    own_mixed = near_half(mixed, 0, side)
    other_mixed = swap(near_half(mixed, 0, 1 - side), "tm", 1)
    attended = jnp.concatenate(
        [jnp.where(is_low, own_mixed, other_mixed), jnp.where(is_low, other_mixed, own_mixed)], axis=1
    )
    state = state + matmul(attended, output_weight)

    normed, scaled_conv, rstd_conv = norm_forward(state, gain_conv)
    act_conv = normed.astype(jnp.bfloat16)
    joined = matmul(act_conv, point_in)
    joined_value = joined[:, :model]
    gate_sig = jax.nn.sigmoid(joined[:, model:])
    gated = joined_value * gate_sig * valid_flat
    up = [(i, i + 1) for i in range(parts - 1)]
    down = [(j, i) for i, j in up]

    def rimmed_of(value):
        low = value.astype(jnp.bfloat16)
        before = lax.ppermute(low[width - half :], "tm", up).astype(jnp.float32)
        after = lax.ppermute(low[:half], "tm", down).astype(jnp.float32)
        return jnp.concatenate([before, value, after], axis=0)

    rimmed = rimmed_of(gated)
    filtered = jnp.zeros_like(gated)
    for tap in range(taps):
        filtered = filtered + depth_weight[tap] * rimmed[tap : tap + width]
    local_count = jnp.sum(valid_flat)
    local_mean = jnp.sum(filtered * valid_flat, axis=0) / jnp.maximum(local_count, 1.0)
    local_gap = (filtered - local_mean) * valid_flat
    count, batch_mean, spread = mesh_moments(local_count, local_mean, jnp.sum(local_gap * local_gap, axis=0))
    count = count[0]
    rstd_batch = lax.rsqrt(spread / count + EPS)
    scaled_batch = (filtered - batch_mean) * rstd_batch
    normalized = scaled_batch * batch_scale + batch_shift
    act_batch = jax.nn.silu(normalized).astype(jnp.bfloat16)
    state = state + matmul(act_batch, point_out)
    state, kept_second = ffn_forward(state, gain_second, second_in, second_out)
    normed, scaled_final, rstd_final = norm_forward(state, gain_final)
    output = (normed * valid_flat).astype(jnp.bfloat16).reshape(row_count, width, model)

    act_first_all = jnp.concatenate(spread_tm(kept_first[0]), axis=0)
    act_second_all = jnp.concatenate(spread_tm(kept_second[0]), axis=0)
    part_first_in = take_columns(first_in, groups, place, parts)
    part_second_in = take_columns(second_in, groups, place, parts)
    part_first_out = take_rows(first_out, groups, place, parts)
    part_second_out = take_rows(second_out, groups, place, parts)
    again_first = ffn_again(act_first_all, part_first_in)
    again_second = ffn_again(act_second_all, part_second_in)

    grad, grad_gain_final = norm_backward(
        cotangent.astype(jnp.float32).reshape(tokens, model) * valid_flat,
        scaled_final,
        rstd_final,
        gain_final,
    )
    grad, grad_gain_second, branch_second = ffn_backward(
        grad, kept_second, gain_second, second_in, second_out
    )
    second_pieces = ffn_weight_grads(
        act_second_all,
        again_second,
        jnp.concatenate(spread_tm(branch_second), axis=0),
        part_second_out,
    )

    d_branch = grad.astype(jnp.bfloat16)
    d_normal = back_prop(d_branch, point_out) * silu_slope(normalized) * valid_flat
    batch_grads = mesh_sum(
        jnp.stack([jnp.sum(d_normal, axis=0), jnp.sum(d_normal * scaled_batch, axis=0)])
    )
    grad_batch_shift, grad_batch_scale = batch_grads[0], batch_grads[1]
    d_filtered = (
        valid_flat
        * (batch_scale * rstd_batch)
        * (d_normal - grad_batch_shift / count - scaled_batch * grad_batch_scale / count)
    )
    rimmed_grad = rimmed_of(d_filtered)
    d_gated = jnp.zeros_like(gated)
    tap_grads = []
    for tap in range(taps):
        d_gated = d_gated + depth_weight[tap] * rimmed_grad[2 * half - tap : 2 * half - tap + width]
        tap_grads.append(jnp.sum(d_filtered * rimmed[tap : tap + width], axis=0))
    d_gated = d_gated * valid_flat
    d_value = (d_gated * gate_sig).astype(jnp.bfloat16)
    d_gate = (d_gated * joined_value * gate_sig * (1.0 - gate_sig)).astype(jnp.bfloat16)
    d_joined = jnp.concatenate([d_value, d_gate], axis=1)

    def near_pair(array):
        return jnp.concatenate([array, swap(array, "tm", 1)], axis=0)

    def near_pair_half(array):
        got = swap(near_half(array, 1, 1 - side), "tm", 1)
        return jnp.concatenate([near_half(array, 1, side), got], axis=0)

    def far_sum(make):
        got = swap(make(1 - far), "tm", 2)
        return (make(far).astype(jnp.float32) + got.astype(jnp.float32)).astype(jnp.bfloat16)

    act_conv_pair, act_batch_pair = near_pair(act_conv), near_pair(act_batch)
    d_joined_pair, d_branch_pair = near_pair_half(d_joined), near_pair_half(d_branch)

    def conv_grads(which):
        return jnp.concatenate(
            [
                weight_grad(act_conv_pair, near_half(d_joined_pair, 1, which)),
                weight_grad(act_batch_pair, near_half(d_branch_pair, 1, which)),
            ],
            axis=1,
        )

    conv_pieces = spread_tm(reduce_rows(far_sum(conv_grads)))

    d_values, grad_gain_conv = norm_backward(
        back_prop(d_joined, point_in), scaled_conv, rstd_conv, gain_conv
    )
    grad = grad + d_values
    d_attend = grad.astype(jnp.bfloat16)
    d_attend_pair = ordered(is_low, d_attend, swap(d_attend, "tm", 1))
    attended_pair = ordered(is_low, attended, swap(attended, "tm", 1))
    d_mixed = back_prop(d_attend_pair, near_half(output_weight, 0, side)).astype(jnp.bfloat16)
    d_query, d_key, d_val, skew_lines = attend_back(
        at, query, keyval, d_mixed, lse, bias, near_heads, head_dim
    )

    far_input = back_prop(d_key[pair:], near_keyval[:, :near_width]) + back_prop(
        d_val[pair:], near_keyval[:, near_width:]
    )
    pair_input = (
        back_prop(d_query, near_query)
        + back_prop(d_key[:pair], near_keyval[:, :near_width])
        + back_prop(d_val[:pair], near_keyval[:, near_width:])
    )
    far_got = swap(near_half(far_input, 0, 1 - side).astype(jnp.bfloat16), "tm", 1)
    far_mine = near_half(far_input, 0, side) + far_got.astype(jnp.float32)
    far_back = swap(far_mine.astype(jnp.bfloat16), "tm", 2)
    pair_got = swap(near_half(pair_input, 0, 1 - side).astype(jnp.bfloat16), "tm", 1)
    d_input = near_half(pair_input, 0, side) + pair_got.astype(jnp.float32) + far_back.astype(jnp.float32)

    d_values, grad_gain_attend = norm_backward(d_input, scaled_attend, rstd_attend, gain_attend)
    grad = grad + d_values
    grad, grad_gain_first, branch_first = ffn_backward(
        grad, kept_first, gain_first, first_in, first_out
    )
    grad_features = grad.astype(jnp.bfloat16).reshape(row_count, width, model)
    first_pieces = ffn_weight_grads(
        act_first_all,
        again_first,
        jnp.concatenate(spread_tm(branch_first), axis=0),
        part_first_out,
    )

    d_attend_side = near_half(d_attend_pair, 1, side)

    def attend_grads(which):
        return jnp.concatenate(
            [
                weight_grad(act_pair, near_half(d_query, 1, which)),
                weight_grad(act_all, near_half(d_key, 1, which)),
                weight_grad(act_all, near_half(d_val, 1, which)),
                weight_grad(attended_pair, near_half(d_attend_side, 1, which)),
            ],
            axis=1,
        )

    attend_pieces = spread_tm(reduce_rows(far_sum(attend_grads)))

    table_lines = sum(
        jnp.pad(skew_lines[:, r], ((0, 0), (7 - r, 0)))[:, :span] for r in range(8)
    )
    near_grad = lax.dot_general(
        table_lines, one_hot, (((1,), (0,)), ((), ())), precision=lax.Precision.HIGHEST
    )
    grad_table = lax.dynamic_update_slice_in_dim(
        jnp.zeros((heads, bucket_count), jnp.float32), near_grad, side * near_heads, 0
    )
    small = jnp.concatenate(
        [
            grad_gain_first[None],
            grad_gain_attend[None],
            grad_gain_conv[None],
            grad_gain_second[None],
            grad_gain_final[None],
            jnp.stack(tap_grads),
            jnp.pad(grad_table.reshape(1, -1), ((0, 0), (0, model - heads * bucket_count))),
        ],
        axis=0,
    )
    small = mesh_sum(small)
    share = model // groups
    gains = lax.dynamic_slice_in_dim(small[:5], row_place * share, share, 1)
    grad_depth = small[5 : 5 + taps]
    grad_table = small[5 + taps, : heads * bucket_count].reshape(heads, bucket_count)

    relative = jnp.arange(parts) ^ place
    crossed = (relative % 2) * 2 + relative // 2
    (grad_first_in,) = lay_columns(first_pieces[0], (model,), groups, relative)
    (grad_second_in,) = lay_columns(second_pieces[0], (model,), groups, relative)

    def lay_rows(pieces):
        size = pieces[0].shape[0]
        out = jnp.zeros((parts, size, model), jnp.float32)
        for k in range(parts):
            out = lax.dynamic_update_index_in_dim(out, pieces[k].astype(jnp.float32), place ^ k, 0)
        return out.reshape(parts * size, model)

    grad_first_out = lay_rows(first_pieces[1])
    grad_second_out = lay_rows(second_pieces[1])
    quarter = model // parts
    grad_query, grad_key, grad_value, grad_output = lay_columns(
        attend_pieces, (quarter,) * 4, 1, crossed
    )
    grad_point_in, grad_point_out = lay_columns(conv_pieces, (2 * quarter, quarter), 1, crossed)
    return (
        output,
        grad_features,
        gains[0],
        grad_first_in,
        grad_first_out,
        gains[1],
        grad_query,
        grad_key,
        grad_value,
        grad_output,
        grad_table,
        gains[2],
        grad_point_in,
        grad_depth,
        grad_batch_scale,
        grad_batch_shift,
        grad_point_out,
        gains[3],
        grad_second_in,
        grad_second_out,
        gains[4],
    )


def solution(mesh):
    rows3, rows2, rows1 = P("rows", "tm", None), P("rows", None), P("rows")
    in_specs = (rows3, rows1) + (P(),) * 20 + (rows3,)
    out_specs = (
        rows3, rows3, rows1, rows2, rows2, rows1, rows2, rows2, rows2, rows2, P(),
        rows1, rows2, P(), P(), P(), rows2, rows1, rows2, rows2, rows1,
    )
    return jax.shard_map(shards, mesh=mesh, in_specs=in_specs, out_specs=out_specs, check_vma=False)
```

time: 2890 us -> 683 us (0.24)
  waiting for transfers between devices: 1660 us -> 179 us
  local copies, waits for them, and re-layouts: 650 us -> 78.9 us
  blocking collectives: 205 us -> 0 us
  starting transfers between devices: 7.16 us -> 85.2 us
  Pallas kernels: 0 us -> 75.2 us
  matrix products: 212 us -> 158 us
    reduce_scatter x10 -> x0, waiting for transfers between devices: 1650 us -> none  [the longest x1 283 us: shards(): lax.psum_scatter(grad_second_out, 'rows', scatter_dimension=0, tiled=True)]
    slice x10 -> x8, local copies, waits for them, and re-layouts: 185 us -> 2.42 us  [the longest x1 0.62 us: shards(): grad_depth = small[5:5 + taps]]
    ppermute x4 -> x82, waiting for transfers between devices: 7.17 us -> 179 us  [the longest x78 179 us: swap(): return lax.ppermute(value, axis, [(i, i ^ bit) for i in range(count)])]
    psum x5 -> x0, blocking collectives: 168 us -> none  [the longest x1 41.5 us: shards(): lax.psum((jnp.sum(filtered * valid_three, axis=(0, 1)), local_count), ('r...]
    unnamed x336 -> x364, local copies, waits for them, and re-layouts: 193 us -> 38.8 us
    rev x1 -> x0, local copies, waits for them, and re-layouts: 151 us -> none  [diagonal_sums(): hankel = matrix[:, ::-1, :]]
    ppermute x4 -> x82, starting transfers between devices: 6.36 us -> 85.2 us  [the longest x78 78.1 us: swap(): return lax.ppermute(value, axis, [(i, i ^ bit) for i in range(count)])]
    pallas_call x0 -> x9, Pallas kernels: none -> 75.2 us  [the longest x1 27.3 us: attend_back(): pl.pallas_call(functools.partial(attend_back_kernel, head_dim ** (-0.5)),...]
  transfers between devices with their start and end apart: 19 -> 82, of which waited for: 13 -> 24; matrix products, arithmetic and copies ran while one was open for 27% -> 38% of each run, Pallas kernels for 0% -> 8%
where the time goes in v1:
time: 683 us; the launch traced here: 672 us
  waiting for transfers between devices  179 us (26%)
  matrix products  158 us (23%)
  other arithmetic  90.3 us (13%)
  starting transfers between devices  85.2 us (12%)
  local copies, waits for them, and re-layouts  78.9 us (12%)
  Pallas kernels  75.2 us (11%)
    ppermute x78, waiting for transfers between devices, swap(): return lax.ppermute(value, axis, [(i, i ^ bit) for i in range(count)])  179 us
    ppermute x78, starting transfers between devices, swap(): return lax.ppermute(value, axis, [(i, i ^ bit) for i in range(count)])  78.1 us
    dot_general x16, matrix products, weight_grad(): lax.dot_general(inputs, grad, (((0,), (0,)), ((), ())), preferred_element...  60.2 us
    dot_general x11, matrix products, matmul(): return jnp.dot(left, right, preferred_element_type=jnp.float32)  52.3 us
    dot_general x10, matrix products, back_prop(): lax.dot_general(grad, weight, (((1,), (1,)), ((), ())), preferred_element...  42.8 us
    unnamed x364, local copies, waits for them, and re-layouts  38.8 us
    pallas_call x1, Pallas kernels, attend_back(): pl.pallas_call(functools.partial(attend_back_kernel, head_dim ** (-0.5)),...  27.3 us
    pallas_call x1, Pallas kernels, attend(): pl.pallas_call(functools.partial(attend_kernel, head_dim ** (-0.5)), out_...  19.2 us
  transfers between devices with their start and end apart: 82, of which 24 were waited for; matrix products, arithmetic and copies ran while one was open for 38% of the time, Pallas kernels for 8%

profile of v1, /device:TPU:0, one launch (start us, length us, event | category | flops | bytes accessed | tf_op | source)
XLA Modules:
  0.0 671.6 jit_solution(11403159649275258595)
XLA Ops:
  6.3 6.2 fusion.185
  12.5 3.6 fusion.181
  18.4 3.0 collective-permute-start.1
  23.3 16.0 %collective-permute-done.1 = bf16[384,1024]{1,0:T(8,128)(2,1)} collective-permute-done((bf16[384,1024]{1,0:T(8,128)(2,1)}, bf16[384,1024]{1,0:T(8,128)(2,1)}, u32[]{:S(2)}, u32[]{:S(2)}) %collective-permute-start.1) | collective-permute-done | bytes 786464 | tf_op jit(solution)/shard_map/ppermute | solution.py:19
  40.6 4.2 bias_rows.1.bias_ref
  53.7 7.7 %convolution_convert_fusion.k_ref.v_ref = bf16[1536,1024]{1,0:T(8,128)(2,1)} fusion(bf16[1024,512]{1,0:T(8,128)(2,1)S(1)} %get-tuple-element.171, bf16[1024,512]{1,0:T(8,128)(2,1)S(1)} %get-tuple-element.172, bf16[384,1024]{1,0:T(8,128)(2,1)S(1)} %get-tuple-element.103, bf16[384,1024]{1,0:T(8,128)(2,1)S(1)} %get-tuple-element.102, ...), kind=kOutput, calls=%fused_computation.17 | convolution fusion | flops 3239575552 | bytes 8388608 | tf_op jit(solution)/shard_map/dot_general | solution.py:23
  61.4 19.2 %attend.1 = (bf16[768,512]{1,0:T(8,128)(2,1)}, f32[4,1,768]{2,1,0:T(1,128)}) custom-call(s32[25]{0:T(128)} %pad_add_fusion.at, bf16[768,512]{1,0:T(8,128)(2,1)} %convolution_convert_fusion.5.q_ref, bf16[1536,1024]{1,0:T(8,128)(2,1)} %convolution_convert_fusion.k_ref.v_ref, bf16[1536,1024]{1,0:T(8,128)(2,1)} %convolution_convert_fusion.k_ref.v_ref, ...), custom_call_target="tpu_custom_call" | custom-call | flops 2415919104 | bytes 9175040 | tf_op jit(solution)/shard_map/attend/pallas_call | solution.py:257
  85.0 3.3 fusion.182
  97.1 3.0 collective-permute-start.4
  102.7 5.3 multiply_reduce_fusion.15
  115.7 2.7 collective-permute-done.7
  131.1 2.9 collective-permute-start.10
  134.0 3.2 constant_dynamic-slice_fusion.13
  145.9 6.3 fusion.187
  152.3 3.7 fusion.184
  161.7 15.2 %multiply_reduce_fusion.5 = (f32[1024]{0:T(1024)}, f32[384]{0:T(512)}, f32[384]{0:T(512)}, f32[384,1024]{1,0:T(8,128)}) fusion(f32[384,1024]{1,0:T(8,128)} %copy-done.16, f32[384]{0:T(512)} %copy-done.132, f32[384]{0:T(512)} %copy-done.126, f32[1024]{0:T(1024)} %param.41, bf16[1024,4096]{1,0:T(8,128)(2,1)} %source.3, ...), kind=kOutput, calls=%fused_computation.135 | convolution fusion | flops 6462896128 | bytes 27015168 | tf_op jit(solution)/shard_map/dot_general | solution.py:27
  178.3 4.6 fusion.173
  183.0 2.8 fusion.170
  186.4 3.1 constant_dynamic-slice_fusion.2
  190.8 2.4 collective-permute-done.12
  194.7 5.6 take_columns.2
  200.4 5.6 take_columns.3
  208.8 8.7 %fusion.95 = f32[1536,1024]{1,0:T(8,128)} fusion(bf16[1024,1024]{1,0:T(8,128)(2,1)} %take_columns.2, bf16[384,1024]{1,0:T(8,128)(2,1)} %collective-permute-done.29, bf16[384,1024]{1,0:T(8,128)(2,1)} %collective-permute-done.28, bf16[384,1024]{1,0:T(8,128)(2,1)} %collective-permute-done.27, bf16[384,1024]{1,0:T(8,128)(2,1)} %fusion.35), kind=kOutput, calls=%fused_computation.252 | convolution fusion | flops 3233808384 | bytes 11534336 | tf_op jit(solution)/shard_map/dot_general | solution.py:23
  217.5 2.7 collective-permute-start.15
  224.0 3.6 multiply_reduce_fusion
  233.4 2.4 multiply_convert_fusion.22
  255.2 27.3 %attend_back.1 = (bf16[768,512]{1,0:T(8,128)(2,1)}, bf16[1536,512]{1,0:T(8,128)(2,1)}, bf16[1536,512]{1,0:T(8,128)(2,1)}, f32[4,8,2304]{2,1,0:T(8,128)}) custom-call(s32[25]{0:T(128)} %pad_add_fusion.at, bf16[768,512]{1,0:T(8,128)(2,1)} %convolution_convert_fusion.5.q_ref, bf16[1536,1024]{1,0:T(8,128)(2,1)} %convolution_convert_fusion.k_ref.v_ref, ...), custom_call_target="tpu_custom_call" | custom-call | flops 6039797760 | bytes 13893632 | tf_op jit(solution)/shard_map/attend_back/pallas_call | solution.py:364
  298.8 2.3 convolution_convert_fusion.3
  305.8 3.2 convolution_convert_fusion.4
  315.7 7.9 %fusion.94 = f32[1536,1024]{1,0:T(8,128)} fusion(bf16[1024,1024]{1,0:T(8,128)(2,1)S(1)} %copy-done.45, bf16[384,1024]{1,0:T(8,128)(2,1)} %collective-permute-done.66, bf16[384,1024]{1,0:T(8,128)(2,1)} %collective-permute-done.65, bf16[384,1024]{1,0:T(8,128)(2,1)} %collective-permute-done.64, bf16[384,1024]{1,0:T(8,128)(2,1)} %multiply_convert_fusion.25), kind=kOutput, calls=%fused_computation.251 | convolution fusion | flops 3233808384 | bytes 11534336 | tf_op jit(solution)/shard_map/dot_general | solution.py:23
  325.3 12.9 %convolution_convert_fusion.1 = bf16[1024,1024]{1,0:T(8,128)(2,1)S(1)} fusion(bf16[1024,1024]{1,0:T(8,128)(2,1)} %bitcast.299, f32[1536,1024]{1,0:T(8,128)} %fusion.94, bf16[384,1024]{1,0:T(8,128)(2,1)} %collective-permute-done.69, bf16[384,1024]{1,0:T(8,128)(2,1)} %collective-permute-done.68, bf16[384,1024]{1,0:T(8,128)(2,1)} %collective-permute-done.67, ...), kind=kOutput, calls=%fused_computation.61 | convolution fusion | flops 6485966848 | bytes 16777216 | tf_op jit(solution)/shard_map/dot_general | solution.py:33
  343.2 7.8 %fusion.16 = bf16[1024,1024]{1,0:T(8,128)(2,1)S(1)} fusion(f32[1536,1024]{1,0:T(8,128)} %fusion.94, bf16[384,1024]{1,0:T(8,128)(2,1)} %collective-permute-done.69, bf16[384,1024]{1,0:T(8,128)(2,1)} %collective-permute-done.68, bf16[384,1024]{1,0:T(8,128)(2,1)} %collective-permute-done.67, bf16[384,1024]{1,0:T(8,128)(2,1)} %multiply_convert_fusion.23), kind=kOutput, calls=%fused_computation.59 | convolution fusion | flops 3242721280 | bytes 11534336 | tf_op jit(solution)/shard_map/dot_general | solution.py:33
  352.7 61.4 %collective-permute-done.21 = bf16[384,1024]{1,0:T(8,128)(2,1)S(1)} collective-permute-done((bf16[384,1024]{1,0:T(8,128)(2,1)S(1)}, bf16[384,1024]{1,0:T(8,128)(2,1)S(1)}, u32[]{:S(2)}, u32[]{:S(2)}) %collective-permute-start.21) | collective-permute-done | bytes 786464 | tf_op jit(solution)/shard_map/ppermute | solution.py:19
  417.2 14.3 %fusion.41 = (f32[1024]{0:T(1024)S(1)}, f32[384]{0:T(512)S(1)}, f32[384]{0:T(512)S(1)}, f32[384,1024]{1,0:T(8,128)}) fusion(bf16[1,384,1024]{2,1,0:T(8,128)(2,1)S(1)} %copy-done.18, f32[384]{0:T(512)S(1)} %copy-done.129, f32[384]{0:T(512)S(1)} %copy-done.123, f32[1024]{0:T(1024)S(1)} %copy-done.157, bf16[1024,4096]{1,0:T(8,128)(2,1)} %source.2, ...), kind=kOutput, calls=%fused_computation.99 | convolution fusion | flops 6463289344 | bytes 26228736 | tf_op jit(solution)/shard_map/dot_general | solution.py:27
  433.4 3.0 fusion.74
  439.6 3.3 add_convert_fusion.1
  442.9 3.0 reshape_reshape.21
  446.7 4.9 constant_dynamic-slice_fusion.5
  451.6 4.8 copy.80
  456.3 2.9 copy.79
  462.8 2.6 collective-permute-start.26
  473.3 4.1 add_convert_fusion
  477.5 3.2 reshape_reshape.20
  480.7 6.3 constant_dynamic-slice_fusion.10
  487.0 6.0 copy.77
  493.0 2.8 copy.76
  505.5 17.9 %collective-permute-done.78 = bf16[1,128,1024]{2,1,0:T(8,128)(2,1)S(1)} collective-permute-done((bf16[1,128,1024]{2,1,0:T(8,128)(2,1)S(1)}, bf16[1,128,1024]{2,1,0:T(8,128)(2,1)S(1)}, u32[]{:S(2)}, u32[]{:S(2)}) %collective-permute-start.78) | collective-permute-done | bytes 262176 | tf_op jit(solution)/shard_map/ppermute | solution.py:19
  530.8 12.9 %convolution_convert_fusion.2 = bf16[1024,1024]{1,0:T(8,128)(2,1)S(1)} fusion(bf16[1024,1024]{1,0:T(8,128)(2,1)} %bitcast.298, f32[1536,1024]{1,0:T(8,128)} %fusion.95, bf16[384,1024]{1,0:T(8,128)(2,1)} %copy-done.170, bf16[384,1024]{1,0:T(8,128)(2,1)} %collective-permute-done.31, bf16[384,1024]{1,0:T(8,128)(2,1)} %collective-permute-done.30, ...), kind=kOutput, calls=%fused_computation.62 | convolution fusion | flops 6485966848 | bytes 16777216 | tf_op jit(solution)/shard_map/dot_general | solution.py:33
  545.5 7.3 %fusion.17 = bf16[1024,1024]{1,0:T(8,128)(2,1)S(1)} fusion(f32[1536,1024]{1,0:T(8,128)} %fusion.95, bf16[384,1024]{1,0:T(8,128)(2,1)S(1)} %copy-done.171, bf16[384,1024]{1,0:T(8,128)(2,1)} %collective-permute-done.31, bf16[384,1024]{1,0:T(8,128)(2,1)} %collective-permute-done.30, bf16[384,1024]{1,0:T(8,128)(2,1)} %get-tuple-element.70), kind=kOutput, calls=%fused_computation.60 | convolution fusion | flops 3242721280 | bytes 11534336 | tf_op jit(solution)/shard_map/dot_general | solution.py:33
  557.1 13.0 %collective-permute-done.33 = bf16[4,128,1024]{2,1,0:T(8,128)(2,1)S(1)} collective-permute-done((bf16[4,128,1024]{2,1,0:T(8,128)(2,1)S(1)}, bf16[4,128,1024]{2,1,0:T(8,128)(2,1)S(1)}, u32[]{:S(2)}, u32[]{:S(2)}) %collective-permute-start.33) | collective-permute-done | bytes 1048608 | tf_op jit(solution)/shard_map/ppermute | solution.py:19
  570.1 2.9 collective-permute-start.48
  573.4 17.5 %collective-permute-done.39 = bf16[4,128,1024]{2,1,0:T(8,128)(2,1)S(1)} collective-permute-done((bf16[4,128,1024]{2,1,0:T(8,128)(2,1)S(1)}, bf16[4,128,1024]{2,1,0:T(8,128)(2,1)S(1)}, u32[]{:S(2)}, u32[]{:S(2)}) %collective-permute-start.39) | collective-permute-done | bytes 1048608 | tf_op jit(solution)/shard_map/ppermute | solution.py:19
  590.9 2.6 collective-permute-start.34
  594.3 14.8 %collective-permute-done.34 = bf16[2,128,1024]{2,1,0:T(8,128)(2,1)S(1)} collective-permute-done((bf16[2,128,1024]{2,1,0:T(8,128)(2,1)S(1)}, bf16[2,128,1024]{2,1,0:T(8,128)(2,1)S(1)}, u32[]{:S(2)}, u32[]{:S(2)}) %collective-permute-start.34) | collective-permute-done | bytes 524320 | tf_op jit(solution)/shard_map/ppermute | solution.py:19
  610.5 10.2 %collective-permute-done.40 = bf16[2,128,1024]{2,1,0:T(8,128)(2,1)S(1)} collective-permute-done((bf16[2,128,1024]{2,1,0:T(8,128)(2,1)S(1)}, bf16[2,128,1024]{2,1,0:T(8,128)(2,1)S(1)}, u32[]{:S(2)}, u32[]{:S(2)}) %collective-permute-start.40) | collective-permute-done | bytes 524320 | tf_op jit(solution)/shard_map/ppermute | solution.py:19
  621.8 3.4 collective-permute-start.41
  625.4 6.6 collective-permute-start.62
  632.0 4.1 collective-permute-done.35
  636.1 4.1 collective-permute-start.51
  640.4 4.1 collective-permute-done.41
  651.2 3.5 lay_columns.7
  655.5 3.1 lay_columns.6
  660.0 3.3 lay_columns.5
  666.3 3.5 lay_columns.4
  (683 shorter events, 200.4 us)
Async XLA Ops:
  18.4 20.8 %collective-permute-start.1 = (bf16[384,1024]{1,0:T(8,128)(2,1)}, bf16[384,1024]{1,0:T(8,128)(2,1)}, u32[]{:S(2)}, u32[]{:S(2)}) collective-permute-start(bf16[384,1024]{1,0:T(8,128)(2,1)} %multiply_convert_fusion.28), channel_id=1, source_target_pairs={{0,2},{1,3},{2,0},{3,1},{4,6},{5,7},{6,4},{7,5},{8,10},{9,11},{10,... | collective-permute-start | bytes 2359304 | tf_op jit(solution)/shard_map/ppermute | solution.py:19
  21.4 25.8 %collective-permute-start = (bf16[384,1024]{1,0:T(8,128)(2,1)}, bf16[384,1024]{1,0:T(8,128)(2,1)}, u32[]{:S(2)}, u32[]{:S(2)}) collective-permute-start(bf16[384,1024]{1,0:T(8,128)(2,1)} %multiply_convert_fusion.28), channel_id=1, source_target_pairs={{0,1},{1,0},{2,3},{3,2},{4,5},{5,4},{6,7},{7,6},{8,9},{9,8},{10,11... | collective-permute-start | bytes 2359304 | tf_op jit(solution)/shard_map/ppermute | solution.py:19
  39.3 11.8 %collective-permute-start.2 = (bf16[384,1024]{1,0:T(8,128)(2,1)}, bf16[384,1024]{1,0:T(8,128)(2,1)}, u32[]{:S(2)}, u32[]{:S(2)}) collective-permute-start(bf16[384,1024]{1,0:T(8,128)(2,1)} %collective-permute-done.1), channel_id=1, source_target_pairs={{0,1},{1,0},{2,3},{3,2},{4,5},{5,4},{6,7},{7,6},{8,9},{9,8},{10,11... | collective-permute-start | bytes 2359304 | tf_op jit(solution)/shard_map/ppermute | solution.py:19
  95.8 6.2 collective-permute-start.5
  120.9 18.7 %collective-permute-start.28 = (bf16[384,1024]{1,0:T(8,128)(2,1)}, bf16[384,1024]{1,0:T(8,128)(2,1)}, u32[]{:S(2)}, u32[]{:S(2)}) collective-permute-start(bf16[384,1024]{1,0:T(8,128)(2,1)} %fusion.35), channel_id=1, source_target_pairs={{0,2},{1,3},{2,0},{3,1},{4,6},{5,7},{6,4},{7,5},{8,10},{9,11},{10,... | collective-permute-start | bytes 2359304 | tf_op jit(solution)/shard_map/ppermute | solution.py:19
  126.5 82.3 %collective-permute-start.27 = (bf16[384,1024]{1,0:T(8,128)(2,1)}, bf16[384,1024]{1,0:T(8,128)(2,1)}, u32[]{:S(2)}, u32[]{:S(2)}) collective-permute-start(bf16[384,1024]{1,0:T(8,128)(2,1)} %fusion.35), channel_id=1, source_target_pairs={{0,1},{1,0},{2,3},{3,2},{4,5},{5,4},{6,7},{7,6},{8,9},{9,8},{10,11... | collective-permute-start | bytes 2359304 | tf_op jit(solution)/shard_map/ppermute | solution.py:19
  131.1 8.4 %collective-permute-start.10 = (f32[3,1024]{1,0:T(4,128)S(1)}, f32[3,1024]{1,0:T(4,128)S(1)}, u32[]{:S(2)}, u32[]{:S(2)}) collective-permute-start(f32[3,1024]{1,0:T(4,128)S(1)} %pad_maximum_fusion.47), channel_id=1, source_target_pairs={{0,16},{4,20},{8,24},{12,28},{16,0},{20,4},{24,8},{28,12},{1,17},{... | collective-permute-start | bytes 36872 | tf_op jit(solution)/shard_map/ppermute | solution.py:19
  139.5 69.3 %collective-permute-start.29 = (bf16[384,1024]{1,0:T(8,128)(2,1)}, bf16[384,1024]{1,0:T(8,128)(2,1)}, u32[]{:S(2)}, u32[]{:S(2)}) collective-permute-start(bf16[384,1024]{1,0:T(8,128)(2,1)} %collective-permute-done.28), channel_id=1, source_target_pairs={{0,1},{1,0},{2,3},{3,2},{4,5},{5,4},{6,7},{7,6},{8,9},{9,8},{10,11... | collective-permute-start | bytes 2359304 | tf_op jit(solution)/shard_map/ppermute | solution.py:19
  193.8 12.2 %collective-permute-start.13 = (f32[2,1024]{1,0:T(2,128)}, f32[2,1024]{1,0:T(2,128)}, u32[]{:S(2)}, u32[]{:S(2)}) collective-permute-start(f32[2,1024]{1,0:T(2,128)} %fusion.217), channel_id=1, source_target_pairs={{0,4},{4,0},{8,12},{12,8},{16,20},{20,16},{24,28},{28,24},{1,5},{5... | collective-permute-start | bytes 24584 | tf_op jit(solution)/shard_map/ppermute | solution.py:19
  207.0 10.5 %collective-permute-start.14 = (f32[2,1024]{1,0:T(2,128)S(1)}, f32[2,1024]{1,0:T(2,128)S(1)}, u32[]{:S(2)}, u32[]{:S(2)}) collective-permute-start(f32[2,1024]{1,0:T(2,128)S(1)} %add.776), channel_id=1, source_target_pairs={{0,8},{4,12},{8,0},{12,4},{16,24},{20,28},{24,16},{28,20},{1,9},{5... | collective-permute-start | bytes 24584 | tf_op jit(solution)/shard_map/ppermute | solution.py:19
  230.7 67.0 %collective-permute-start.53 = (bf16[384,1024]{1,0:T(8,128)(2,1)S(1)}, bf16[384,1024]{1,0:T(8,128)(2,1)}, u32[]{:S(2)}, u32[]{:S(2)}) collective-permute-start(bf16[384,1024]{1,0:T(8,128)(2,1)S(1)} %copy-done.58), channel_id=1, source_target_pairs={{0,1},{1,0},{2,3},{3,2},{4,5},{5,4},{6,7},{7,6},{8,9},{9,8},{10,11... | collective-permute-start | bytes 2359304 | tf_op jit(solution)/shard_map/ppermute | solution.py:19
  232.8 11.8 %collective-permute-start.45 = (bf16[384,1024]{1,0:T(8,128)(2,1)S(1)}, bf16[384,1024]{1,0:T(8,128)(2,1)S(1)}, u32[]{:S(2)}, u32[]{:S(2)}) collective-permute-start(bf16[384,1024]{1,0:T(8,128)(2,1)S(1)} %pad_maximum_fusion.27), channel_id=1, source_target_pairs={{0,1},{1,0},{2,3},{3,2},{4,5},{5,4},{6,7},{7,6},{8,9},{9,8},{10,11... | collective-permute-start | bytes 2359304 | tf_op jit(solution)/shard_map/ppermute | solution.py:19
  232.9 13.5 %collective-permute-start.55 = (bf16[384,1024]{1,0:T(8,128)(2,1)S(1)}, bf16[384,1024]{1,0:T(8,128)(2,1)S(1)}, u32[]{:S(2)}, u32[]{:S(2)}) collective-permute-start(bf16[384,1024]{1,0:T(8,128)(2,1)S(1)} %copy-done.60), channel_id=1, source_target_pairs={{0,1},{1,0},{2,3},{3,2},{4,5},{5,4},{6,7},{7,6},{8,9},{9,8},{10,11... | collective-permute-start | bytes 2359304 | tf_op jit(solution)/shard_map/ppermute | solution.py:19
  241.2 9.8 %collective-permute-start.18 = (bf16[384,1024]{1,0:T(8,128)(2,1)S(1)}, bf16[384,1024]{1,0:T(8,128)(2,1)S(1)}, u32[]{:S(2)}, u32[]{:S(2)}) collective-permute-start(bf16[384,1024]{1,0:T(8,128)(2,1)S(1)} %get-tuple-element.73), channel_id=1, source_target_pairs={{0,1},{1,0},{2,3},{3,2},{4,5},{5,4},{6,7},{7,6},{8,9},{9,8},{10,11... | collective-permute-start | bytes 2359304 | tf_op jit(solution)/shard_map/ppermute | solution.py:19
  244.6 53.2 %collective-permute-start.65 = (bf16[384,1024]{1,0:T(8,128)(2,1)}, bf16[384,1024]{1,0:T(8,128)(2,1)}, u32[]{:S(2)}, u32[]{:S(2)}) collective-permute-start(bf16[384,1024]{1,0:T(8,128)(2,1)} %multiply_convert_fusion.25), channel_id=1, source_target_pairs={{0,2},{1,3},{2,0},{3,1},{4,6},{5,7},{6,4},{7,5},{8,10},{9,11},{10,... | collective-permute-start | bytes 2359304 | tf_op jit(solution)/shard_map/ppermute | solution.py:19
  246.4 68.8 %collective-permute-start.64 = (bf16[384,1024]{1,0:T(8,128)(2,1)}, bf16[384,1024]{1,0:T(8,128)(2,1)}, u32[]{:S(2)}, u32[]{:S(2)}) collective-permute-start(bf16[384,1024]{1,0:T(8,128)(2,1)} %multiply_convert_fusion.25), channel_id=1, source_target_pairs={{0,1},{1,0},{2,3},{3,2},{4,5},{5,4},{6,7},{7,6},{8,9},{9,8},{10,11... | collective-permute-start | bytes 2359304 | tf_op jit(solution)/shard_map/ppermute | solution.py:19
  246.5 51.8 %collective-permute-start.68 = (bf16[384,1024]{1,0:T(8,128)(2,1)}, bf16[384,1024]{1,0:T(8,128)(2,1)}, u32[]{:S(2)}, u32[]{:S(2)}) collective-permute-start(bf16[384,1024]{1,0:T(8,128)(2,1)} %multiply_convert_fusion.23), channel_id=1, source_target_pairs={{0,2},{1,3},{2,0},{3,1},{4,6},{5,7},{6,4},{7,5},{8,10},{9,11},{10,... | collective-permute-start | bytes 2359304 | tf_op jit(solution)/shard_map/ppermute | solution.py:19
  251.1 47.3 %collective-permute-start.54 = (bf16[384,1024]{1,0:T(8,128)(2,1)S(1)}, bf16[384,1024]{1,0:T(8,128)(2,1)}, u32[]{:S(2)}, u32[]{:S(2)}) collective-permute-start(bf16[384,1024]{1,0:T(8,128)(2,1)S(1)} %get-tuple-element.96), channel_id=1, source_target_pairs={{0,1},{1,0},{2,3},{3,2},{4,5},{5,4},{6,7},{7,6},{8,9},{9,8},{10,11... | collective-permute-start | bytes 2359304 | tf_op jit(solution)/shard_map/ppermute | solution.py:19
  297.7 25.9 %collective-permute-start.67 = (bf16[384,1024]{1,0:T(8,128)(2,1)}, bf16[384,1024]{1,0:T(8,128)(2,1)}, u32[]{:S(2)}, u32[]{:S(2)}) collective-permute-start(bf16[384,1024]{1,0:T(8,128)(2,1)} %multiply_convert_fusion.23), channel_id=1, source_target_pairs={{0,1},{1,0},{2,3},{3,2},{4,5},{5,4},{6,7},{7,6},{8,9},{9,8},{10,11... | collective-permute-start | bytes 2359304 | tf_op jit(solution)/shard_map/ppermute | solution.py:19
  297.8 17.6 %collective-permute-start.66 = (bf16[384,1024]{1,0:T(8,128)(2,1)}, bf16[384,1024]{1,0:T(8,128)(2,1)}, u32[]{:S(2)}, u32[]{:S(2)}) collective-permute-start(bf16[384,1024]{1,0:T(8,128)(2,1)} %collective-permute-done.65), channel_id=1, source_target_pairs={{0,1},{1,0},{2,3},{3,2},{4,5},{5,4},{6,7},{7,6},{8,9},{9,8},{10,11... | collective-permute-start | bytes 2359304 | tf_op jit(solution)/shard_map/ppermute | solution.py:19
  298.3 27.0 %collective-permute-start.69 = (bf16[384,1024]{1,0:T(8,128)(2,1)}, bf16[384,1024]{1,0:T(8,128)(2,1)}, u32[]{:S(2)}, u32[]{:S(2)}) collective-permute-start(bf16[384,1024]{1,0:T(8,128)(2,1)} %collective-permute-done.68), channel_id=1, source_target_pairs={{0,1},{1,0},{2,3},{3,2},{4,5},{5,4},{6,7},{7,6},{8,9},{9,8},{10,11... | collective-permute-start | bytes 2359304 | tf_op jit(solution)/shard_map/ppermute | solution.py:19
  298.4 42.5 %collective-permute-start.20 = (bf16[384,1024]{1,0:T(8,128)(2,1)}, bf16[384,1024]{1,0:T(8,128)(2,1)}, u32[]{:S(2)}, u32[]{:S(2)}) collective-permute-start(bf16[384,1024]{1,0:T(8,128)(2,1)} %dynamic-slice_convert_fusion), channel_id=1, source_target_pairs={{0,1},{1,0},{2,3},{3,2},{4,5},{5,4},{6,7},{7,6},{8,9},{9,8},{10,11... | collective-permute-start | bytes 2359304 | tf_op jit(solution)/shard_map/ppermute | solution.py:19
  315.2 37.0 %collective-permute-start.19 = (bf16[384,1024]{1,0:T(8,128)(2,1)}, bf16[384,1024]{1,0:T(8,128)(2,1)S(1)}, u32[]{:S(2)}, u32[]{:S(2)}) collective-permute-start(bf16[384,1024]{1,0:T(8,128)(2,1)} %dynamic-slice_convert_fusion.1), channel_id=1, source_target_pairs={{0,1},{1,0},{2,3},{3,2},{4,5},{5,4},{6,7},{7,6},{8,9},{9,8},{10,11... | collective-permute-start | bytes 2359304 | tf_op jit(solution)/shard_map/ppermute | solution.py:19
  315.4 156.5 %collective-permute-start.46 = (bf16[1024,1024]{0,1:T(8,128)(2,1)}, bf16[1024,1024]{0,1:T(8,128)(2,1)}, u32[]{:S(2)}, u32[]{:S(2)}) collective-permute-start(bf16[1024,1024]{0,1:T(8,128)(2,1)} %pad_maximum_fusion.5), channel_id=1, source_target_pairs={{0,2},{1,3},{2,0},{3,1},{4,6},{5,7},{6,4},{7,5},{8,10},{9,11},{10,... | collective-permute-start | bytes 6291464 | tf_op jit(solution)/shard_map/ppermute | solution.py:19
  323.6 114.4 %collective-permute-start.57 = (bf16[1024,768]{0,1:T(8,128)(2,1)}, bf16[1024,768]{0,1:T(8,128)(2,1)}, u32[]{:S(2)}, u32[]{:S(2)}) collective-permute-start(bf16[1024,768]{0,1:T(8,128)(2,1)} %pad_maximum_fusion.18), channel_id=1, source_target_pairs={{0,2},{1,3},{2,0},{3,1},{4,6},{5,7},{6,4},{7,5},{8,10},{9,11},{10,... | collective-permute-start | bytes 4718600 | tf_op jit(solution)/shard_map/ppermute | solution.py:19
  339.4 119.9 %collective-permute-start.70 = (bf16[4,128,1024]{2,1,0:T(8,128)(2,1)}, bf16[4,128,1024]{2,1,0:T(8,128)(2,1)}, u32[]{:S(2)}, u32[]{:S(2)}) collective-permute-start(bf16[4,128,1024]{2,1,0:T(8,128)(2,1)} %dynamic-slice_bitcast_fusion.1), channel_id=1, source_target_pairs={{0,4},{4,0},{8,12},{12,8},{16,20},{20,16},{24,28},{28,24},{1,5},{5... | collective-permute-start | bytes 3145736 | tf_op jit(solution)/shard_map/ppermute | solution.py:19
  342.8 71.3 %collective-permute-start.21 = (bf16[384,1024]{1,0:T(8,128)(2,1)S(1)}, bf16[384,1024]{1,0:T(8,128)(2,1)S(1)}, u32[]{:S(2)}, u32[]{:S(2)}) collective-permute-start(bf16[384,1024]{1,0:T(8,128)(2,1)S(1)} %add_convert_fusion.2), channel_id=1, source_target_pairs={{0,2},{1,3},{2,0},{3,1},{4,6},{5,7},{6,4},{7,5},{8,10},{9,11},{10,... | collective-permute-start | bytes 2359304 | tf_op jit(solution)/shard_map/ppermute | solution.py:19
  352.2 110.6 %collective-permute-start.76 = (bf16[4,128,1024]{2,1,0:T(8,128)(2,1)}, bf16[4,128,1024]{2,1,0:T(8,128)(2,1)}, u32[]{:S(2)}, u32[]{:S(2)}) collective-permute-start(bf16[4,128,1024]{2,1,0:T(8,128)(2,1)} %dynamic-slice_bitcast_fusion), channel_id=1, source_target_pairs={{0,4},{4,0},{8,12},{12,8},{16,20},{20,16},{24,28},{28,24},{1,5},{5... | collective-permute-start | bytes 3145736 | tf_op jit(solution)/shard_map/ppermute | solution.py:19
  437.3 67.2 %collective-permute-start.31 = (bf16[384,1024]{1,0:T(8,128)(2,1)}, bf16[384,1024]{1,0:T(8,128)(2,1)}, u32[]{:S(2)}, u32[]{:S(2)}) collective-permute-start(bf16[384,1024]{1,0:T(8,128)(2,1)} %get-tuple-element.70), channel_id=1, source_target_pairs={{0,2},{1,3},{2,0},{3,1},{4,6},{5,7},{6,4},{7,5},{8,10},{9,11},{10,... | collective-permute-start | bytes 2359304 | tf_op jit(solution)/shard_map/ppermute | solution.py:19
  438.0 7.8 %collective-permute-start.24 = (f32[11,1024]{1,0:T(8,128)S(1)}, f32[11,1024]{1,0:T(8,128)S(1)}, u32[]{:S(2)}, u32[]{:S(2)}) collective-permute-start(f32[11,1024]{1,0:T(8,128)S(1)} %add.801), channel_id=1, source_target_pairs={{0,4},{4,0},{8,12},{12,8},{16,20},{20,16},{24,28},{28,24},{1,5},{5... | collective-permute-start | bytes 135176 | tf_op jit(solution)/shard_map/ppermute | solution.py:19
  445.9 13.4 %collective-permute-start.25 = (f32[11,1024]{1,0:T(8,128)S(1)}, f32[11,1024]{1,0:T(8,128)S(1)}, u32[]{:S(2)}, u32[]{:S(2)}) collective-permute-start(f32[11,1024]{1,0:T(8,128)S(1)} %add.802), channel_id=1, source_target_pairs={{0,8},{4,12},{8,0},{12,4},{16,24},{20,28},{24,16},{28,20},{1,9},{5... | collective-permute-start | bytes 135176 | tf_op jit(solution)/shard_map/ppermute | solution.py:19
  459.2 69.4 %collective-permute-start.30 = (bf16[384,1024]{1,0:T(8,128)(2,1)}, bf16[384,1024]{1,0:T(8,128)(2,1)}, u32[]{:S(2)}, u32[]{:S(2)}) collective-permute-start(bf16[384,1024]{1,0:T(8,128)(2,1)} %get-tuple-element.70), channel_id=1, source_target_pairs={{0,1},{1,0},{2,3},{3,2},{4,5},{5,4},{6,7},{7,6},{8,9},{9,8},{10,11... | collective-permute-start | bytes 2359304 | tf_op jit(solution)/shard_map/ppermute | solution.py:19
  459.3 42.7 %collective-permute-start.58 = (bf16[4,128,768]{2,1,0:T(8,128)(2,1)}, bf16[4,128,768]{2,1,0:T(8,128)(2,1)}, u32[]{:S(2)}, u32[]{:S(2)}) collective-permute-start(bf16[4,128,768]{2,1,0:T(8,128)(2,1)} %bitcast.82), channel_id=1, source_target_pairs={{0,4},{4,0},{8,12},{12,8},{16,20},{20,16},{24,28},{28,24},{1,5},{5... | collective-permute-start | bytes 2359304 | tf_op jit(solution)/shard_map/ppermute | solution.py:19
  462.8 6.6 collective-permute-start.26
  469.4 26.4 %collective-permute-start.71 = (bf16[2,128,1024]{2,1,0:T(8,128)(2,1)}, bf16[2,128,1024]{2,1,0:T(8,128)(2,1)}, u32[]{:S(2)}, u32[]{:S(2)}) collective-permute-start(bf16[2,128,1024]{2,1,0:T(8,128)(2,1)} %dynamic-slice_bitcast_fusion.5), channel_id=1, source_target_pairs={{0,8},{4,12},{8,0},{12,4},{16,24},{20,28},{24,16},{28,20},{1,9},{5... | collective-permute-start | bytes 1572872 | tf_op jit(solution)/shard_map/ppermute | solution.py:19
  471.9 26.9 %collective-permute-start.77 = (bf16[2,128,1024]{2,1,0:T(8,128)(2,1)}, bf16[2,128,1024]{2,1,0:T(8,128)(2,1)}, u32[]{:S(2)}, u32[]{:S(2)}) collective-permute-start(bf16[2,128,1024]{2,1,0:T(8,128)(2,1)} %dynamic-slice_bitcast_fusion.4), channel_id=1, source_target_pairs={{0,8},{4,12},{8,0},{12,4},{16,24},{20,28},{24,16},{28,20},{1,9},{5... | collective-permute-start | bytes 1572872 | tf_op jit(solution)/shard_map/ppermute | solution.py:19
  495.9 59.4 %collective-permute-start.47 = (bf16[4,128,1024]{2,1,0:T(8,128)(2,1)}, bf16[4,128,1024]{2,1,0:T(8,128)(2,1)}, u32[]{:S(2)}, u32[]{:S(2)}) collective-permute-start(bf16[4,128,1024]{2,1,0:T(8,128)(2,1)} %bitcast.300), channel_id=1, source_target_pairs={{0,4},{4,0},{8,12},{12,8},{16,20},{20,16},{24,28},{28,24},{1,5},{5... | collective-permute-start | bytes 3145736 | tf_op jit(solution)/shard_map/ppermute | solution.py:19
  498.8 25.7 %collective-permute-start.72 = (bf16[1,128,1024]{2,1,0:T(8,128)(2,1)S(1)}, bf16[1,128,1024]{2,1,0:T(8,128)(2,1)S(1)}, u32[]{:S(2)}, u32[]{:S(2)}) collective-permute-start(bf16[1,128,1024]{2,1,0:T(8,128)(2,1)S(1)} %constant_dynamic-slice_fusion.1), channel_id=1, source_target_pairs={{0,16},{4,20},{8,24},{12,28},{16,0},{20,4},{24,8},{28,12},{1,17},{... | collective-permute-start | bytes 786440 | tf_op jit(solution)/shard_map/ppermute | solution.py:19
  502.0 21.4 %collective-permute-start.78 = (bf16[1,128,1024]{2,1,0:T(8,128)(2,1)S(1)}, bf16[1,128,1024]{2,1,0:T(8,128)(2,1)S(1)}, u32[]{:S(2)}, u32[]{:S(2)}) collective-permute-start(bf16[1,128,1024]{2,1,0:T(8,128)(2,1)S(1)} %constant_dynamic-slice_fusion), channel_id=1, source_target_pairs={{0,16},{4,20},{8,24},{12,28},{16,0},{20,4},{24,8},{28,12},{1,17},{... | collective-permute-start | bytes 786440 | tf_op jit(solution)/shard_map/ppermute | solution.py:19
  504.5 21.3 %collective-permute-start.59 = (bf16[2,128,768]{2,1,0:T(8,128)(2,1)S(1)}, bf16[2,128,768]{2,1,0:T(8,128)(2,1)S(1)}, u32[]{:S(2)}, u32[]{:S(2)}) collective-permute-start(bf16[2,128,768]{2,1,0:T(8,128)(2,1)S(1)} %dynamic-slice_bitcast_fusion.9), channel_id=1, source_target_pairs={{0,8},{4,12},{8,0},{12,4},{16,24},{20,28},{24,16},{28,20},{1,9},{5... | collective-permute-start | bytes 1179656 | tf_op jit(solution)/shard_map/ppermute | solution.py:19
  523.4 6.1 collective-permute-start.32
  525.8 29.1 %collective-permute-start.80 = (bf16[128,1024]{1,0:T(8,128)(2,1)}, bf16[128,1024]{1,0:T(8,128)(2,1)}, u32[]{:S(2)}, u32[]{:S(2)}) collective-permute-start(bf16[128,1024]{1,0:T(8,128)(2,1)} %get-tuple-element.108), channel_id=1, source_target_pairs={{0,2},{1,3},{2,0},{3,1},{4,6},{5,7},{6,4},{7,5},{8,10},{9,11},{10,... | collective-permute-start | bytes 786440 | tf_op jit(solution)/shard_map/ppermute | solution.py:19
  527.8 26.9 %collective-permute-start.74 = (bf16[128,1024]{1,0:T(8,128)(2,1)}, bf16[128,1024]{1,0:T(8,128)(2,1)}, u32[]{:S(2)}, u32[]{:S(2)}) collective-permute-start(bf16[128,1024]{1,0:T(8,128)(2,1)} %fusion.108.refs_0_), channel_id=1, source_target_pairs={{0,2},{1,3},{2,0},{3,1},{4,6},{5,7},{6,4},{7,5},{8,10},{9,11},{10,... | collective-permute-start | bytes 786440 | tf_op jit(solution)/shard_map/ppermute | solution.py:19
  528.7 24.2 %collective-permute-start.60 = (bf16[1,128,768]{2,1,0:T(8,128)(2,1)}, bf16[1,128,768]{2,1,0:T(8,128)(2,1)}, u32[]{:S(2)}, u32[]{:S(2)}) collective-permute-start(bf16[1,128,768]{2,1,0:T(8,128)(2,1)} %constant_dynamic-slice_fusion.3), channel_id=1, source_target_pairs={{0,16},{4,20},{8,24},{12,28},{16,0},{20,4},{24,8},{28,12},{1,17},{... | collective-permute-start | bytes 589832 | tf_op jit(solution)/shard_map/ppermute | solution.py:19
  543.9 26.2 %collective-permute-start.33 = (bf16[4,128,1024]{2,1,0:T(8,128)(2,1)S(1)}, bf16[4,128,1024]{2,1,0:T(8,128)(2,1)S(1)}, u32[]{:S(2)}, u32[]{:S(2)}) collective-permute-start(bf16[4,128,1024]{2,1,0:T(8,128)(2,1)S(1)} %dynamic-slice_bitcast_fusion.3), channel_id=1, source_target_pairs={{0,4},{4,0},{8,12},{12,8},{16,20},{20,16},{24,28},{28,24},{1,5},{5... | collective-permute-start | bytes 3145736 | tf_op jit(solution)/shard_map/ppermute | solution.py:19
  552.9 38.1 %collective-permute-start.39 = (bf16[4,128,1024]{2,1,0:T(8,128)(2,1)S(1)}, bf16[4,128,1024]{2,1,0:T(8,128)(2,1)S(1)}, u32[]{:S(2)}, u32[]{:S(2)}) collective-permute-start(bf16[4,128,1024]{2,1,0:T(8,128)(2,1)S(1)} %dynamic-slice_bitcast_fusion.2), channel_id=1, source_target_pairs={{0,4},{4,0},{8,12},{12,8},{16,20},{20,16},{24,28},{28,24},{1,5},{5... | collective-permute-start | bytes 3145736 | tf_op jit(solution)/shard_map/ppermute | solution.py:19
  554.7 70.6 %collective-permute-start.73 = (bf16[128,1024]{1,0:T(8,128)(2,1)}, bf16[128,1024]{1,0:T(8,128)(2,1)S(1)}, u32[]{:S(2)}, u32[]{:S(2)}) collective-permute-start(bf16[128,1024]{1,0:T(8,128)(2,1)} %fusion.108.refs_0_), channel_id=1, source_target_pairs={{0,1},{1,0},{2,3},{3,2},{4,5},{5,4},{6,7},{7,6},{8,9},{9,8},{10,11... | collective-permute-start | bytes 786440 | tf_op jit(solution)/shard_map/ppermute | solution.py:19
  554.8 90.2 %collective-permute-start.75 = (bf16[128,1024]{1,0:T(8,128)(2,1)}, bf16[128,1024]{1,0:T(8,128)(2,1)S(1)}, u32[]{:S(2)}, u32[]{:S(2)}) collective-permute-start(bf16[128,1024]{1,0:T(8,128)(2,1)} %collective-permute-done.74.refs_2_), channel_id=1, source_target_pairs={{0,1},{1,0},{2,3},{3,2},{4,5},{5,4},{6,7},{7,6},{8,9},{9,8},{10,11... | collective-permute-start | bytes 786440 | tf_op jit(solution)/shard_map/ppermute | solution.py:19
  555.3 91.5 %collective-permute-start.81 = (bf16[128,1024]{1,0:T(8,128)(2,1)}, bf16[128,1024]{1,0:T(8,128)(2,1)S(1)}, u32[]{:S(2)}, u32[]{:S(2)}) collective-permute-start(bf16[128,1024]{1,0:T(8,128)(2,1)} %collective-permute-done.80), channel_id=1, source_target_pairs={{0,1},{1,0},{2,3},{3,2},{4,5},{5,4},{6,7},{7,6},{8,9},{9,8},{10,11... | collective-permute-start | bytes 786440 | tf_op jit(solution)/shard_map/ppermute | solution.py:19
  570.1 23.9 %collective-permute-start.48 = (bf16[2,128,1024]{2,1,0:T(8,128)(2,1)S(1)}, bf16[2,128,1024]{2,1,0:T(8,128)(2,1)S(1)}, u32[]{:S(2)}, u32[]{:S(2)}) collective-permute-start(bf16[2,128,1024]{2,1,0:T(8,128)(2,1)S(1)} %dynamic-slice_bitcast_fusion.6), channel_id=1, source_target_pairs={{0,8},{4,12},{8,0},{12,4},{16,24},{20,28},{24,16},{28,20},{1,9},{5... | collective-permute-start | bytes 1572872 | tf_op jit(solution)/shard_map/ppermute | solution.py:19
  590.9 18.2 %collective-permute-start.34 = (bf16[2,128,1024]{2,1,0:T(8,128)(2,1)S(1)}, bf16[2,128,1024]{2,1,0:T(8,128)(2,1)S(1)}, u32[]{:S(2)}, u32[]{:S(2)}) collective-permute-start(bf16[2,128,1024]{2,1,0:T(8,128)(2,1)S(1)} %dynamic-slice_bitcast_fusion.8), channel_id=1, source_target_pairs={{0,8},{4,12},{8,0},{12,4},{16,24},{20,28},{24,16},{28,20},{1,9},{5... | collective-permute-start | bytes 1572872 | tf_op jit(solution)/shard_map/ppermute | solution.py:19
  594.0 26.7 %collective-permute-start.40 = (bf16[2,128,1024]{2,1,0:T(8,128)(2,1)S(1)}, bf16[2,128,1024]{2,1,0:T(8,128)(2,1)S(1)}, u32[]{:S(2)}, u32[]{:S(2)}) collective-permute-start(bf16[2,128,1024]{2,1,0:T(8,128)(2,1)S(1)} %dynamic-slice_bitcast_fusion.7), channel_id=1, source_target_pairs={{0,8},{4,12},{8,0},{12,4},{16,24},{20,28},{24,16},{28,20},{1,9},{5... | collective-permute-start | bytes 1572872 | tf_op jit(solution)/shard_map/ppermute | solution.py:19
  609.2 12.6 %collective-permute-start.49 = (bf16[1,128,1024]{2,1,0:T(8,128)(2,1)S(1)}, bf16[1,128,1024]{2,1,0:T(8,128)(2,1)S(1)}, u32[]{:S(2)}, u32[]{:S(2)}) collective-permute-start(bf16[1,128,1024]{2,1,0:T(8,128)(2,1)S(1)} %constant_dynamic-slice_fusion.8), channel_id=1, source_target_pairs={{0,16},{4,20},{8,24},{12,28},{16,0},{20,4},{24,8},{28,12},{1,17},{... | collective-permute-start | bytes 786440 | tf_op jit(solution)/shard_map/ppermute | solution.py:19
  620.7 15.4 %collective-permute-start.35 = (bf16[1,128,1024]{2,1,0:T(8,128)(2,1)S(1)}, bf16[1,128,1024]{2,1,0:T(8,128)(2,1)S(1)}, u32[]{:S(2)}, u32[]{:S(2)}) collective-permute-start(bf16[1,128,1024]{2,1,0:T(8,128)(2,1)S(1)} %constant_dynamic-slice_fusion.12), channel_id=1, source_target_pairs={{0,16},{4,20},{8,24},{12,28},{16,0},{20,4},{24,8},{28,12},{1,17},{... | collective-permute-start | bytes 786440 | tf_op jit(solution)/shard_map/ppermute | solution.py:19
  621.8 22.7 %collective-permute-start.41 = (bf16[1,128,1024]{2,1,0:T(8,128)(2,1)S(1)}, bf16[1,128,1024]{2,1,0:T(8,128)(2,1)S(1)}, u32[]{:S(2)}, u32[]{:S(2)}) collective-permute-start(bf16[1,128,1024]{2,1,0:T(8,128)(2,1)S(1)} %constant_dynamic-slice_fusion.11), channel_id=1, source_target_pairs={{0,16},{4,20},{8,24},{12,28},{16,0},{20,4},{24,8},{28,12},{1,17},{... | collective-permute-start | bytes 786440 | tf_op jit(solution)/shard_map/ppermute | solution.py:19
  625.4 15.0 %collective-permute-start.62 = (bf16[128,768]{1,0:T(8,128)(2,1)S(1)}, bf16[128,768]{1,0:T(8,128)(2,1)S(1)}, u32[]{:S(2)}, u32[]{:S(2)}) collective-permute-start(bf16[128,768]{1,0:T(8,128)(2,1)S(1)} %fusion.109.refs_0_), channel_id=1, source_target_pairs={{0,2},{1,3},{2,0},{3,1},{4,6},{5,7},{6,4},{7,5},{8,10},{9,11},{10,... | collective-permute-start | bytes 589832 | tf_op jit(solution)/shard_map/ppermute | solution.py:19
  636.1 10.7 %collective-permute-start.51 = (bf16[128,1024]{1,0:T(8,128)(2,1)S(1)}, bf16[128,1024]{1,0:T(8,128)(2,1)S(1)}, u32[]{:S(2)}, u32[]{:S(2)}) collective-permute-start(bf16[128,1024]{1,0:T(8,128)(2,1)S(1)} %fusion.107.refs_0_), channel_id=1, source_target_pairs={{0,2},{1,3},{2,0},{3,1},{4,6},{5,7},{6,4},{7,5},{8,10},{9,11},{10,... | collective-permute-start | bytes 786440 | tf_op jit(solution)/shard_map/ppermute | solution.py:19
  640.3 7.0 %collective-permute-start.61 = (bf16[128,768]{1,0:T(8,128)(2,1)S(1)}, bf16[128,768]{1,0:T(8,128)(2,1)S(1)}, u32[]{:S(2)}, u32[]{:S(2)}) collective-permute-start(bf16[128,768]{1,0:T(8,128)(2,1)S(1)} %fusion.109.refs_0_), channel_id=1, source_target_pairs={{0,1},{1,0},{2,3},{3,2},{4,5},{5,4},{6,7},{7,6},{8,9},{9,8},{10,11... | collective-permute-start | bytes 589832 | tf_op jit(solution)/shard_map/ppermute | solution.py:19
  645.0 13.6 %collective-permute-start.50 = (bf16[128,1024]{1,0:T(8,128)(2,1)S(1)}, bf16[128,1024]{1,0:T(8,128)(2,1)S(1)}, u32[]{:S(2)}, u32[]{:S(2)}) collective-permute-start(bf16[128,1024]{1,0:T(8,128)(2,1)S(1)} %fusion.107.refs_0_), channel_id=1, source_target_pairs={{0,1},{1,0},{2,3},{3,2},{4,5},{5,4},{6,7},{7,6},{8,9},{9,8},{10,11... | collective-permute-start | bytes 786440 | tf_op jit(solution)/shard_map/ppermute | solution.py:19
  646.8 11.8 %collective-permute-start.52 = (bf16[128,1024]{1,0:T(8,128)(2,1)S(1)}, bf16[128,1024]{1,0:T(8,128)(2,1)S(1)}, u32[]{:S(2)}, u32[]{:S(2)}) collective-permute-start(bf16[128,1024]{1,0:T(8,128)(2,1)S(1)} %collective-permute-done.51.refs_2_), channel_id=1, source_target_pairs={{0,1},{1,0},{2,3},{3,2},{4,5},{5,4},{6,7},{7,6},{8,9},{9,8},{10,11... | collective-permute-start | bytes 786440 | tf_op jit(solution)/shard_map/ppermute | solution.py:19
  646.8 17.1 %collective-permute-start.42 = (bf16[128,1024]{1,0:T(8,128)(2,1)S(1)}, bf16[128,1024]{1,0:T(8,128)(2,1)S(1)}, u32[]{:S(2)}, u32[]{:S(2)}) collective-permute-start(bf16[128,1024]{1,0:T(8,128)(2,1)S(1)} %get-tuple-element.112), channel_id=1, source_target_pairs={{0,1},{1,0},{2,3},{3,2},{4,5},{5,4},{6,7},{7,6},{8,9},{9,8},{10,11... | collective-permute-start | bytes 786440 | tf_op jit(solution)/shard_map/ppermute | solution.py:19
  647.4 16.5 %collective-permute-start.43 = (bf16[128,1024]{1,0:T(8,128)(2,1)S(1)}, bf16[128,1024]{1,0:T(8,128)(2,1)S(1)}, u32[]{:S(2)}, u32[]{:S(2)}) collective-permute-start(bf16[128,1024]{1,0:T(8,128)(2,1)S(1)} %get-tuple-element.112), channel_id=1, source_target_pairs={{0,2},{1,3},{2,0},{3,1},{4,6},{5,7},{6,4},{7,5},{8,10},{9,11},{10,... | collective-permute-start | bytes 786440 | tf_op jit(solution)/shard_map/ppermute | solution.py:19
  649.1 14.2 %collective-permute-start.37 = (bf16[128,1024]{1,0:T(8,128)(2,1)S(1)}, bf16[128,1024]{1,0:T(8,128)(2,1)S(1)}, u32[]{:S(2)}, u32[]{:S(2)}) collective-permute-start(bf16[128,1024]{1,0:T(8,128)(2,1)S(1)} %fusion.106.refs_0_), channel_id=1, source_target_pairs={{0,2},{1,3},{2,0},{3,1},{4,6},{5,7},{6,4},{7,5},{8,10},{9,11},{10,... | collective-permute-start | bytes 786440 | tf_op jit(solution)/shard_map/ppermute | solution.py:19
  663.9 5.9 collective-permute-start.44
  (197 other events, 1767.1 us)

commit v2 on v1

v2 whole, which is shorter than its diff:
```python
import functools

import jax
import jax.numpy as jnp
from jax import lax
from jax.experimental import pallas as pl
from jax.experimental.pallas import tpu as pltpu
from jax.sharding import PartitionSpec as P

EPS = 1e-05
NEGATIVE = -1e30
LANES = 128
QUERY_TILE = 768
MIB = 1024 * 1024
BLOCK = 1024
EFFORT = 0.5


def swap(value, axis, bit):
    count = lax.axis_size(axis)
    return lax.ppermute(value, axis, [(i, i ^ bit) for i in range(count)])


def mesh_sum(value):
    for axis in ("tm", "rows"):
        bit = 1
        while bit < lax.axis_size(axis):
            value = value + swap(value, axis, bit)
            bit *= 2
    return value


def mesh_moments(count, mean, spread):
    for axis in ("tm", "rows"):
        bit = 1
        while bit < lax.axis_size(axis):
            sent = jnp.concatenate([mean[None], spread[None], jnp.broadcast_to(count, (1, mean.shape[0]))])
            got = swap(sent, axis, bit)
            other_mean, other_spread, other_count = got[0], got[1], got[2]
            total = count + other_count
            safe = jnp.maximum(total, 1.0)
            gap = other_mean - mean
            spread = spread + other_spread + gap * gap * (count * other_count / safe)
            mean = (count * mean + other_count * other_mean) / safe
            count = total
            bit *= 2
    return (count, mean, spread)


def after(value, *earlier):
    return lax.optimization_barrier((value, *earlier))[0]


def reduce_rows(partial, far_first=False):
    size = lax.axis_size("rows")
    place = lax.axis_index("rows")
    bits = size.bit_length() - 1
    order = list(range(bits))
    if far_first:
        order = order[1:] + order[:1]
    inner = (partial.shape[0] // size, partial.shape[1])
    left = partial.reshape((2,) * bits + inner)
    held = list(range(bits))[::-1]
    for bit in order:
        axis = held.index(bit)
        mine = (place >> bit) & 1
        front = left.shape[:axis]
        rows = 1
        for n in left.shape[axis + 1 : -2]:
            rows *= n
        lead = 1
        for n in front:
            lead *= n
        cut = left.reshape((lead, 2, rows) + inner)
        keep = lax.dynamic_index_in_dim(cut, mine, 1, keepdims=False)
        send = lax.dynamic_index_in_dim(cut, 1 - mine, 1, keepdims=False)
        got = swap(send, "rows", 1 << bit)
        left = (keep.astype(jnp.float32) + got.astype(jnp.float32)).astype(jnp.bfloat16)
        held.remove(bit)
        left = left.reshape((2,) * len(held) + inner)
    return left


def spread_tm(piece, *earlier):
    near = swap(piece, "tm", 1)
    far = swap(after(piece, *earlier) if earlier else piece, "tm", 2)
    return [piece, near, far, swap(far, "tm", 1)]


def silu_pair(hidden):
    sigma = 0.5 * jnp.tanh(0.5 * hidden) + 0.5
    act = hidden * sigma
    return (act, sigma + act * (1.0 - sigma))


def normed_of(values, gain):
    mean = jnp.mean(values, axis=-1, keepdims=True)
    centered = values - mean
    rstd = lax.rsqrt(jnp.mean(centered * centered, axis=-1, keepdims=True) + EPS)
    scaled = centered * rstd
    return (scaled * gain, scaled, rstd)


def normed_back(grad, values, gain):
    _, scaled, rstd = normed_of(values, gain)
    weighted = grad * gain
    inner = weighted - jnp.mean(weighted, axis=-1, keepdims=True)
    inner = inner - scaled * jnp.mean(weighted * scaled, axis=-1, keepdims=True)
    return (rstd * inner, jnp.sum(grad * scaled, axis=0, keepdims=True))


def dot(left, right):
    return jnp.dot(left, right, preferred_element_type=jnp.float32)


def dot_turned(left, right):
    return lax.dot_general(left, right, (((1,), (1,)), ((), ())), preferred_element_type=jnp.float32)


def scalars():
    return [pl.BlockSpec(memory_space=pltpu.SMEM)]


def struct(*shape, kind=jnp.bfloat16):
    return jax.ShapeDtypeStruct(shape, kind)


class Arriving:
    def __init__(self, source, target, sem):
        self.copy = pltpu.make_async_copy(source, target, sem)
        self.target = target
        self.started = self.here = False

    def start(self):
        if not self.started:
            self.copy.start()
            self.started = True

    def get(self):
        self.start()
        if not self.here:
            self.copy.wait()
            self.here = True
        return self.target


class Leaving:
    def __init__(self, source, target, sem):
        self.copy = pltpu.make_async_copy(source, target, sem)
        self.ref = source
        self.sent = False

    def send(self):
        self.copy.start()
        self.sent = True


def flow_call(body, name, outs, scratch, info, operands, flops, mib=24, raw=()):
    ins, results = len(operands), len(outs)

    def kernel(info, *refs):
        sources, targets = refs[:ins], refs[ins : ins + results]
        rest = refs[ins + results :]
        held, made = rest[:ins], rest[ins : ins + results]
        extra, sem_in, sem_out = rest[ins + results : -2], rest[-2], rest[-1]
        arriving = [
            (sources[k], held[k]) if k in raw else Arriving(sources[k], held[k], sem_in.at[k])
            for k in range(ins)
        ]
        for k in range(ins):
            if k not in raw:
                arriving[k].start()
        leaving = [Leaving(made[k], targets[k], sem_out.at[k]) for k in range(results)]
        body(info, arriving, leaving, *extra)
        for item in leaving:
            if not item.sent:
                item.send()
        for k in range(ins):
            if k not in raw:
                arriving[k].get()
        for item in leaving:
            item.copy.wait()

    moved = sum(o.size * o.dtype.itemsize for o in (*operands, *outs))
    return pl.pallas_call(
        kernel,
        in_specs=scalars() + [pl.BlockSpec(memory_space=pl.ANY)] * ins,
        out_specs=[pl.BlockSpec(memory_space=pl.ANY)] * results,
        out_shape=outs,
        scratch_shapes=[pltpu.VMEM(o.shape, o.dtype) for o in (*operands, *outs)]
        + list(scratch)
        + [pltpu.SemaphoreType.DMA((ins,)), pltpu.SemaphoreType.DMA((results,))],
        compiler_params=pltpu.CompilerParams(vmem_limit_bytes=mib * MIB),
        cost_estimate=cost(flops, 0, moved),
        name=name,
    )(info, *operands)


def cost(flops, transcendentals, moved):
    return pl.CostEstimate(
        flops=int(flops * EFFORT), transcendentals=int(transcendentals * EFFORT), bytes_accessed=int(moved * EFFORT)
    )


SIDE, FAR, OFFSET, LENGTH = range(4)


def project_kernel(info, ins, outs, sem, rows):
    mine, other, *weights = ins
    side = info[SIDE]
    half = outs[0].ref.shape[1]
    lanes = pl.ds(pl.multiple_of(side * half, half), half)
    copies = [
        pltpu.make_async_copy(source.at[:, lanes], held.at[:, :half], sem.at[k])
        for k, (source, held) in enumerate(weights)
    ]
    for copy in copies:
        copy.start()
    tokens = mine.target.shape[0]
    rows[pl.ds(pl.multiple_of(side * tokens, tokens), tokens)] = mine.get()[...]
    rows[pl.ds(pl.multiple_of((1 - side) * tokens, tokens), tokens)] = other.get()[...]
    for copy, (_, held), out in zip(copies, weights, outs, strict=True):
        copy.wait()
        out.ref[...] = dot(rows[...], held[:, :half]).astype(jnp.bfloat16)
        out.send()


def project(info, mine, other, weights):
    tokens, model = mine.shape
    pair = 2 * tokens
    return flow_call(
        project_kernel, "project",
        [struct(pair, model // 2)] * len(weights),
        [pltpu.SemaphoreType.DMA((len(weights),)), pltpu.VMEM((pair, model), jnp.bfloat16)],
        info, (mine, other, *weights), pair * model * model * len(weights),
        raw=tuple(range(2, 2 + len(weights))),
    )


def rows_of(length, first, count):
    frame = lax.broadcasted_iota(jnp.int32, (count, 1), 0) + first
    return ((frame >= 0) & (frame < length)).astype(jnp.float32)


def mix_kernel(
    info, own_ref, other_ref, weight, state_ref, gain_ref, value_w, gate_w,
    attended_ref, after_ref, act_ref, value_ref, gate_ref, gated_ref,
):
    side = info[SIDE]
    tokens, half = own_ref.shape

    @pl.when(pl.program_id(0) == 0)
    def _():
        attended_ref[:, pl.ds(pl.multiple_of(side * half, half), half)] = own_ref[...]
        attended_ref[:, pl.ds(pl.multiple_of((1 - side) * half, half), half)] = other_ref[...]
        values = state_ref[...] + dot(attended_ref[...], weight[...])
        after_ref[...] = values
        act_ref[...] = normed_of(values, gain_ref[...])[0].astype(jnp.bfloat16)

    value = dot(act_ref[...], value_w[...])
    gate = 0.5 * jnp.tanh(0.5 * dot(act_ref[...], gate_w[...])) + 0.5
    value_ref[...] = value.astype(jnp.bfloat16)
    gate_ref[...] = gate.astype(jnp.bfloat16)
    gated_ref[...] = value * gate * rows_of(info[LENGTH], info[OFFSET], tokens)


def mix(info, own, other, weight, state, gain, point_in):
    tokens, model = state.shape
    step = 512
    steps = model // step
    flat = (tokens, model)
    column = pl.BlockSpec((tokens, step), lambda i: (0, i))
    return pl.pallas_call(
        mix_kernel,
        grid=(steps,),
        in_specs=scalars() + [
            whole(own.shape), whole(own.shape), whole(weight.shape), whole(flat), whole((1, model)),
            pl.BlockSpec((model, step), lambda i: (0, i)),
            pl.BlockSpec((model, step), lambda i: (0, steps + i)),
        ],
        out_specs=[whole(flat)] * 3 + [column] * 3,
        out_shape=[
            struct(*flat), struct(*flat, kind=jnp.float32), struct(*flat),
            struct(*flat), struct(*flat), struct(*flat, kind=jnp.float32),
        ],
        compiler_params=pltpu.CompilerParams(vmem_limit_bytes=32 * MIB),
        cost_estimate=cost(
            6 * tokens * model * model,
            tokens * model,
            6 * model * model + 20 * tokens * model,
        ),
        name="mix",
    )(info, own, other, weight, state, gain[None], point_in, point_in)


def filter_kernel(info, ins, outs, wide):
    gated_ref, before_ref, after_ref, taps_ref = [item.get() for item in ins]
    filtered_ref, moments_ref = [item.ref for item in outs]
    tokens = gated_ref.shape[0]
    half = before_ref.shape[0]
    wide[8 : 8 + tokens] = gated_ref[...]
    wide[8 - half : 8] = before_ref[...].astype(jnp.float32)
    wide[8 + tokens : 8 + tokens + half] = after_ref[...].astype(jnp.float32)
    filtered = taps_ref[0:1] * wide[8 - half : 8 - half + tokens]
    for tap in range(1, taps_ref.shape[0]):
        filtered = filtered + taps_ref[tap : tap + 1] * wide[8 - half + tap : 8 - half + tap + tokens]
    filtered_ref[...] = filtered
    outs[0].send()
    valid = rows_of(info[LENGTH], info[OFFSET], tokens)
    count = jnp.clip(info[LENGTH] - info[OFFSET], 1, tokens).astype(jnp.float32)
    mean = jnp.sum(filtered * valid, axis=0, keepdims=True) / count
    gap = (filtered - mean) * valid
    moments_ref[0:1] = mean
    moments_ref[1:2] = jnp.sum(gap * gap, axis=0, keepdims=True)


def filter_frames(info, gated, before, later, depth):
    tokens, model = gated.shape
    return flow_call(
        filter_kernel, "filter_frames",
        [struct(tokens, model, kind=jnp.float32), struct(2, model, kind=jnp.float32)],
        [pltpu.VMEM((tokens + 16, model), jnp.float32)],
        info, (gated, before, later, depth), 10 * tokens * model,
    )


def weight_copies(pair_in, pair_out, sem, block):
    def at(i):
        lanes = pl.ds(pl.multiple_of(i * block, block), block)
        return (
            pltpu.make_async_copy(pair_in[0].at[:, lanes], pair_in[1].at[:, lanes], sem.at[0, i]),
            pltpu.make_async_copy(pair_out[0].at[lanes, :], pair_out[1].at[lanes, :], sem.at[1, i]),
        )

    return at


def second_kernel(info, ins, outs, sem, state, grad, total, slopes):
    filtered, stats, state_in, cot, gain, final_gain, point, pair_in, pair_out = ins
    w_in, w_out = pair_in[1], pair_out[1]
    act_batch, act_out, output, branch_out, grad_out, conv_out, d_norm_out, sums = outs
    tokens = filtered.target.shape[0]
    steps = w_in.shape[1] // BLOCK
    valid = rows_of(info[LENGTH], info[OFFSET], tokens)
    copies = weight_copies(pair_in, pair_out, sem, BLOCK)
    for i in range(steps):
        for copy in copies(i):
            copy.start()

    filtered_ref, stats_ref = filtered.get(), stats.get()

    def normalized():
        scaled = (filtered_ref[...] - stats_ref[0:1]) * stats_ref[1:2]
        return (scaled, scaled * stats_ref[2:3] + stats_ref[3:4])

    act = silu_pair(normalized()[1])[0].astype(jnp.bfloat16)
    act_batch.ref[...] = act
    act_batch.send()
    values = state_in.get()[...] + dot(act, point.get()[...])
    state[...] = values
    act_ref = act_out.ref
    act_ref[...] = normed_of(values, gain.get()[...])[0].astype(jnp.bfloat16)
    act_out.send()
    total[...] = jnp.zeros_like(total)

    def forward(i, carry):
        lanes = pl.ds(pl.multiple_of(i * BLOCK, BLOCK), BLOCK)
        for copy in copies(i):
            copy.wait()
        mid, slope = silu_pair(dot(act_ref[...], w_in[:, lanes]))
        slopes[:, lanes] = slope.astype(jnp.bfloat16)
        total[...] += dot(mid.astype(jnp.bfloat16), w_out[lanes, :])
        return carry

    lax.fori_loop(0, steps, forward, 0)
    values = state[...] + 0.5 * total[...]
    final = final_gain.get()[...]
    normed, _, _ = normed_of(values, final)
    output.ref[...] = (normed * valid).astype(jnp.bfloat16)
    output.send()
    begin, sums.ref[0:1] = normed_back(cot.get()[...].astype(jnp.float32) * valid, values, final)
    grad[...] = begin
    branch_ref = branch_out.ref
    branch_ref[...] = (0.5 * begin).astype(jnp.bfloat16)
    branch_out.send()
    total[...] = jnp.zeros_like(total)

    def backward(i, carry):
        lanes = pl.ds(pl.multiple_of(i * BLOCK, BLOCK), BLOCK)
        part = dot_turned(branch_ref[...], w_out[lanes, :])
        part = (part * slopes[:, lanes].astype(jnp.float32)).astype(jnp.bfloat16)
        total[...] += dot_turned(part, w_in[:, lanes])
        return carry

    lax.fori_loop(0, steps, backward, 0)
    d_values, sums.ref[1:2] = normed_back(total[...], state[...], gain.get()[...])
    later = grad[...] + d_values
    grad_out.ref[...] = later
    grad_out.send()
    low = later.astype(jnp.bfloat16)
    conv_out.ref[...] = low
    conv_out.send()
    scaled, normal = normalized()
    d_norm = dot_turned(low, point.get()[...]) * silu_pair(normal)[1] * valid
    d_norm_out.ref[...] = d_norm
    d_norm_out.send()
    sums.ref[2:3] = jnp.sum(d_norm, axis=0, keepdims=True)
    sums.ref[3:4] = jnp.sum(d_norm * scaled, axis=0, keepdims=True)


def second_both(info, filtered, stats, state, cotangent, gain, final_gain, point_out, w_in, w_out):
    tokens, model = state.shape
    inner = w_in.shape[1]
    flat = (tokens, model)
    low, high = struct(*flat), struct(*flat, kind=jnp.float32)
    return flow_call(
        second_kernel, "second_both",
        [low, low, low, low, high, low, high, struct(4, model, kind=jnp.float32)],
        [
            pltpu.SemaphoreType.DMA((2, inner // BLOCK)),
            pltpu.VMEM(flat, jnp.float32), pltpu.VMEM(flat, jnp.float32), pltpu.VMEM(flat, jnp.float32),
            pltpu.VMEM((tokens, inner), jnp.bfloat16),
        ],
        info,
        (filtered, stats, state, cotangent, gain[None], final_gain[None], point_out, w_in, w_out),
        8 * tokens * model * inner + 4 * tokens * model * model,
        mib=48,
        raw=(7, 8),
    )


def conv_back_kernel(info, ins, outs, wide, gated_wide):
    d_norm_ref, filtered_ref, before_ref, after_ref, stats_ref, sums_ref, taps_ref = [i.get() for i in ins[:7]]
    gated_ref, gated_before, gated_after = [i.get() for i in ins[7:10]]
    value, gate, point, state, gain, grad = ins[10:]
    joined_ref, out_ref, low_ref, small_ref = [item.ref for item in outs]
    tokens, model = d_norm_ref.shape
    half = gated_before.shape[0]

    def d_filtered(d_norm, filtered, first):
        valid = rows_of(info[LENGTH], first, d_norm.shape[0])
        scaled = (filtered - stats_ref[0:1]) * stats_ref[1:2]
        inner = d_norm - sums_ref[0:1] - scaled * sums_ref[1:2]
        return valid * (stats_ref[2:3] * stats_ref[1:2]) * inner

    offset = info[OFFSET]
    wide[8 : 8 + tokens] = d_filtered(d_norm_ref[...], filtered_ref[...], offset)
    wide[8 - half : 8] = d_filtered(before_ref[:half], before_ref[half:], offset - half)
    wide[8 + tokens : 8 + tokens + half] = d_filtered(after_ref[:half], after_ref[half:], offset + tokens)
    gated_wide[8 : 8 + tokens] = gated_ref[...]
    gated_wide[8 - half : 8] = gated_before[...].astype(jnp.float32)
    gated_wide[8 + tokens : 8 + tokens + half] = gated_after[...].astype(jnp.float32)
    d_gated = jnp.zeros((tokens, model), jnp.float32)
    for tap in range(taps_ref.shape[0]):
        begin = 8 + half - tap
        d_gated = d_gated + taps_ref[tap : tap + 1] * wide[begin : begin + tokens]
        begin = 8 - half + tap
        small_ref[1 + tap : 2 + tap] = jnp.sum(
            wide[8 : 8 + tokens] * gated_wide[begin : begin + tokens], axis=0, keepdims=True
        )
    d_gated = d_gated * rows_of(info[LENGTH], offset, tokens)
    gate = gate.get()[...].astype(jnp.float32)
    d_value = d_gated * gate
    joined_ref[:, :model] = d_value.astype(jnp.bfloat16)
    joined_ref[:, model:] = (d_value * value.get()[...].astype(jnp.float32) * (1.0 - gate)).astype(jnp.bfloat16)
    outs[0].send()
    d_values, small_ref[0:1] = normed_back(
        dot_turned(joined_ref[...], point.get()[...]), state.get()[...], gain.get()[...]
    )
    later = grad.get()[...] + d_values
    low_ref[...] = later.astype(jnp.bfloat16)
    outs[2].send()
    out_ref[...] = later


def conv_back(info, d_norm, filtered, before, later, stats, sums, depth, gated, gated_before, gated_after,
              value, gate, point_in, state, gain, grad):
    tokens, model = d_norm.shape
    return flow_call(
        conv_back_kernel, "conv_back",
        [
            struct(tokens, 2 * model), struct(tokens, model, kind=jnp.float32), struct(tokens, model),
            struct(1 + depth.shape[0], model, kind=jnp.float32),
        ],
        [pltpu.VMEM((tokens + 16, model), jnp.float32)] * 2,
        info,
        (d_norm, filtered, before, later, stats, sums, depth, gated, gated_before, gated_after, value,
         gate, point_in, state, gain[None], grad),
        4 * tokens * model * model,
        mib=32,
    )


def mixed_back_kernel(info, ins, outs, sem):
    own, near, (source, held) = ins
    half = source.shape[0] // 2
    side = info[SIDE]
    copy = pltpu.make_async_copy(source.at[pl.ds(pl.multiple_of(side * half, half), half), :], held.at[:half], sem.at[0])
    copy.start()
    own_ref, near_ref, out_ref = own.get(), near.get(), outs[0].ref
    tokens = own_ref.shape[0]
    copy.wait()
    part = held[:half]
    mine = pl.ds(pl.multiple_of(side * tokens, tokens), tokens)
    other = pl.ds(pl.multiple_of((1 - side) * tokens, tokens), tokens)
    out_ref[mine] = dot_turned(own_ref[...], part).astype(jnp.bfloat16)
    out_ref[other] = dot_turned(near_ref[...], part).astype(jnp.bfloat16)


def mixed_back(info, own, near, weight):
    tokens, model = own.shape
    return flow_call(
        mixed_back_kernel, "mixed_back", [struct(2 * tokens, model // 2)], [pltpu.SemaphoreType.DMA((1,))],
        info, (own, near, weight), 2 * tokens * model * model, raw=(2,),
    )[0]


def input_back_kernel(count, base, info, ins, outs, sem):
    grads, weights = ins[:count], ins[count:]
    send_ref, keep_ref = outs[0].ref, outs[1].ref
    tokens = send_ref.shape[0]
    side = info[SIDE]
    half = weights[0][0].shape[1] // 2
    lanes = pl.ds(pl.multiple_of(side * half, half), half)
    copies = [
        pltpu.make_async_copy(source.at[:, lanes], held.at[:, :half], sem.at[k])
        for k, (source, held) in enumerate(weights)
    ]
    for copy in copies:
        copy.start()
    grads = [grad.get() for grad in grads]
    for copy in copies:
        copy.wait()

    def total(which):
        out = None
        for first, grad, (_, held) in zip(base, grads, weights, strict=True):
            rows = pl.ds(pl.multiple_of(first + which * tokens, LANES), tokens)
            part = dot_turned(grad[rows], held[:, :half])
            out = part if out is None else out + part
        return out

    send_ref[...] = total(1 - side).astype(jnp.bfloat16)
    outs[0].send()
    keep_ref[...] = total(side)


def input_back(info, grads, base, weights, tokens):
    model = weights[0].shape[0]
    count = len(grads)
    return flow_call(
        functools.partial(input_back_kernel, count, base), "input_back",
        [struct(tokens, model), struct(tokens, model, kind=jnp.float32)],
        [pltpu.SemaphoreType.DMA((count,))],
        info, (*grads, *weights), 2 * tokens * model * model * count,
        mib=32, raw=tuple(range(count, 2 * count)),
    )


def cross_kernel(layout, info, refs, outs, left_rows, right_rows):
    send_ref, keep_ref = outs[0].ref, outs[1].ref
    far, side = info[FAR], info[SIDE]
    at = 0
    begin = 0
    for pieces, width in layout:
        lefts, right = refs[at : at + pieces], refs[at + pieces : at + pieces + (2 if width < 0 else 1)]
        at += pieces + len(right)
        tokens = lefts[0].target.shape[0]
        for k, left in enumerate(lefts):
            spot = (k // 2 * 2 + (side if k % 2 == 0 else 1 - side)) * tokens
            left_rows[pl.ds(pl.multiple_of(spot, tokens), tokens)] = left.get()[...]
        size = abs(width)
        half = size // 2
        if len(right) == 2:
            for k, piece in enumerate(right):
                spot = (side if k == 0 else 1 - side) * tokens
                right_rows[pl.ds(pl.multiple_of(spot, tokens), tokens), :size] = piece.get()[...]
            source = right_rows
        else:
            source = right[0].get()
        count = pieces * tokens
        for which, target in ((1 - far, send_ref), (far, keep_ref)):
            lanes = pl.ds(pl.multiple_of(which * half, half), half)
            target[:, begin : begin + half] = lax.dot_general(
                left_rows[:count], source[:count, lanes], (((0,), (0,)), ((), ())),
                preferred_element_type=jnp.float32,
            ).astype(jnp.bfloat16)
        begin += half


def cross_grads(info, terms):
    operands, layout = [], []
    total = flops = 0
    for lefts, rights in terms:
        operands += [*lefts, *rights]
        width = rights[0].shape[1]
        layout.append((len(lefts), -width if len(rights) == 2 else width))
        total += width // 2
        tokens, model = lefts[0].shape
        flops += 2 * len(lefts) * tokens * model * width
    deepest = max(len(lefts) for lefts, _ in terms) * tokens
    widest = max(rights[0].shape[1] for _, rights in terms)
    return flow_call(
        functools.partial(cross_kernel, layout), "cross_grads", [struct(model, total)] * 2,
        [pltpu.VMEM((deepest, model), jnp.bfloat16), pltpu.VMEM((deepest, widest), jnp.bfloat16)],
        info, tuple(operands), flops, mib=40,
    )


def first_back_kernel(info, ins, outs, sem, branch, total):
    grad, x, gain, slope, pair_in, pair_out = ins
    w_in, w_out = pair_in[1], pair_out[1]
    steps = w_in.shape[1] // BLOCK
    copies = weight_copies(pair_in, pair_out, sem, BLOCK)
    for i in range(steps):
        for copy in copies(i):
            copy.start()
    grad_ref = grad.get()
    branch[...] = (0.5 * grad_ref[...]).astype(jnp.bfloat16)
    total[...] = jnp.zeros_like(total)
    slope_ref = slope.get()

    def backward(i, carry):
        lanes = pl.ds(pl.multiple_of(i * BLOCK, BLOCK), BLOCK)
        for copy in copies(i):
            copy.wait()
        part = dot_turned(branch[...], w_out[lanes, :])
        part = (part * slope_ref[:, lanes].astype(jnp.float32)).astype(jnp.bfloat16)
        total[...] += dot_turned(part, w_in[:, lanes])
        return carry

    lax.fori_loop(0, steps, backward, 0)
    d_values, outs[1].ref[...] = normed_back(total[...], x.get()[...].astype(jnp.float32), gain.get()[...])
    outs[0].ref[...] = (grad_ref[...] + d_values).astype(jnp.bfloat16)


def first_backward(info, grad, features, gain, slope, w_in, w_out):
    tokens, model = features.shape
    inner = w_in.shape[1]
    return flow_call(
        first_back_kernel, "first_backward",
        [struct(tokens, model), struct(1, model, kind=jnp.float32)],
        [pltpu.SemaphoreType.DMA((2, inner // BLOCK)), pltpu.VMEM((tokens, model), jnp.bfloat16), pltpu.VMEM((tokens, model), jnp.float32)],
        info, (grad, features, gain[None], slope, w_in, w_out), 4 * tokens * model * inner,
        mib=40, raw=(4, 5),
    )


def norm_backward(grad, scaled, rstd, gain):
    weighted = grad * gain
    inner = weighted - jnp.mean(weighted, axis=-1, keepdims=True)
    inner = inner - scaled * jnp.mean(weighted * scaled, axis=-1, keepdims=True)
    return (rstd * inner, jnp.sum(grad * scaled, axis=0))


def first_kernel(x_ref, gain_ref, next_gain_ref, w_in, w_out, state_ref, act_ref, slope_ref, next_ref, total):
    step = pl.program_id(0)

    @pl.when(step == 0)
    def _():
        values = x_ref[...].astype(jnp.float32)
        act_ref[...] = normed_of(values, gain_ref[...])[0].astype(jnp.bfloat16)
        total[...] = jnp.zeros_like(total)

    mid, slope = silu_pair(dot(act_ref[...], w_in[...]))
    slope_ref[...] = slope.astype(jnp.bfloat16)
    total[...] += dot(mid.astype(jnp.bfloat16), w_out[...])

    @pl.when(step == pl.num_programs(0) - 1)
    def _():
        values = x_ref[...].astype(jnp.float32) + 0.5 * total[...]
        state_ref[...] = values
        next_ref[...] = normed_of(values, next_gain_ref[...])[0].astype(jnp.bfloat16)


def whole(shape):
    return pl.BlockSpec(shape, lambda *_: (0,) * len(shape))


def first_forward(features, gain, next_gain, w_in, w_out):
    tokens, model = features.shape
    inner = w_in.shape[1]
    return pl.pallas_call(
        first_kernel,
        grid=(inner // BLOCK,),
        in_specs=[
            whole((tokens, model)),
            whole((1, model)),
            whole((1, model)),
            pl.BlockSpec((model, BLOCK), lambda i: (0, i)),
            pl.BlockSpec((BLOCK, model), lambda i: (i, 0)),
        ],
        out_specs=[
            whole((tokens, model)),
            whole((tokens, model)),
            pl.BlockSpec((tokens, BLOCK), lambda i: (0, i)),
            whole((tokens, model)),
        ],
        out_shape=[
            jax.ShapeDtypeStruct((tokens, model), jnp.float32),
            jax.ShapeDtypeStruct((tokens, model), jnp.bfloat16),
            jax.ShapeDtypeStruct((tokens, inner), jnp.bfloat16),
            jax.ShapeDtypeStruct((tokens, model), jnp.bfloat16),
        ],
        scratch_shapes=[pltpu.VMEM((tokens, model), jnp.float32)],
        compiler_params=pltpu.CompilerParams(vmem_limit_bytes=40 * MIB),
        cost_estimate=cost(
            4 * tokens * model * inner,
            2 * tokens * inner,
            4 * model * inner + 2 * tokens * inner,
        ),
        name="first_forward",
    )(features, gain[None], next_gain[None], w_in, w_out)


def take_kernel(place, source, target):
    target[...] = source[...]


def take_columns(weight, groups, place, parts):
    model, total = weight.shape
    block = total // groups // parts
    if block % LANES:
        cut = weight.reshape(model, groups, parts, block)
        return lax.dynamic_index_in_dim(cut, place, 2, keepdims=False).reshape(model, -1)
    return pl.pallas_call(
        take_kernel,
        out_shape=jax.ShapeDtypeStruct((model, total // parts), weight.dtype),
        grid_spec=pltpu.PrefetchScalarGridSpec(
            num_scalar_prefetch=1,
            grid=(groups,),
            in_specs=[pl.BlockSpec((model, block), lambda g, at: (0, g * parts + at[0]))],
            out_specs=pl.BlockSpec((model, block), lambda g, at: (0, g)),
        ),
        name="take_columns",
    )(place.reshape(1), weight)


def take_rows(weight, groups, place, parts):
    total, model = weight.shape
    cut = weight.reshape(groups, parts, total // groups // parts, model)
    return lax.dynamic_index_in_dim(cut, place, 1, keepdims=False).reshape(-1, model)


def lay_kernel(widths, groups, places, *refs):
    parts = 4
    pieces, targets = refs[:parts], refs[parts:]
    for k in range(parts):
        begin = 0
        for width, target in zip(widths, targets, strict=True):
            block = width // groups
            for g in range(groups):
                at = pl.multiple_of((g * parts + places[k]) * block, LANES)
                source = pieces[k][:, begin + g * block : begin + (g + 1) * block]
                target[:, pl.ds(at, block)] = source.astype(jnp.float32)
            begin += width


def lay_columns(pieces, widths, groups, places):
    rows = pieces[0].shape[0]
    parts = len(pieces)
    if any((width // groups) % LANES for width in widths):
        outs, begin = [], 0
        stacked = jnp.zeros((parts, *pieces[0].shape), pieces[0].dtype)
        for k in range(parts):
            stacked = lax.dynamic_update_index_in_dim(stacked, pieces[k], places[k], 0)
        for width in widths:
            cut = stacked[:, :, begin : begin + width].reshape(parts, rows, groups, width // groups)
            outs.append(cut.transpose(1, 2, 0, 3).reshape(rows, parts * width).astype(jnp.float32))
            begin += width
        return outs
    return pl.pallas_call(
        functools.partial(lay_kernel, widths, groups),
        out_shape=[jax.ShapeDtypeStruct((rows, parts * width), jnp.float32) for width in widths],
        grid_spec=pltpu.PrefetchScalarGridSpec(
            num_scalar_prefetch=1,
            grid=(1,),
            in_specs=[pl.BlockSpec(p.shape, lambda i, at: (0, 0)) for p in pieces],
            out_specs=[pl.BlockSpec((rows, parts * width), lambda i, at: (0, 0)) for width in widths],
        ),
        compiler_params=pltpu.CompilerParams(vmem_limit_bytes=24 * MIB),
        name="lay_columns",
    )(places, *pieces)


def skew_kernel(line, out):
    length = line.shape[-1]
    width = out.shape[-1]
    spread = jnp.broadcast_to(line[0], (LANES, length))
    rolled = pltpu.roll(spread, length - (LANES - 1), 1, stride=1, stride_axis=0)
    out[0] = rolled[:, :width]


def skewed(lines):
    heads, _, length = lines.shape
    width = length - LANES
    return pl.pallas_call(
        skew_kernel,
        out_shape=jax.ShapeDtypeStruct((heads, LANES, width), jnp.float32),
        grid=(heads,),
        in_specs=[pl.BlockSpec((1, 1, length), lambda h: (h, 0, 0))],
        out_specs=pl.BlockSpec((1, LANES, width), lambda h: (h, 0, 0)),
        name="bias_rows",
    )(lines)


def attend_kernel(
    scale, at, q_ref, k_pair, k_far, v_pair, v_far, bias_ref, out_ref, lse_ref, k_ref, vt_ref, s_ref, p_ref
):
    tile = q_ref.shape[0]
    blocks = k_ref.shape[0] // LANES
    pair = k_pair.shape[0]
    length = at[blocks * 2]

    @pl.when(pl.program_id(1) == 0)
    def _():
        k_ref[:pair] = k_pair[...]
        k_ref[pair:] = k_far[...]
        vt_ref[:, :pair] = v_pair[...].T
        vt_ref[:, pair:] = v_far[...].T

    begin = pl.program_id(1) * tile
    s_ref[...] = lax.dot_general(
        k_ref[...], q_ref[...], (((1,), (1,)), ((), ())), preferred_element_type=jnp.float32
    )
    frame = lax.broadcasted_iota(jnp.int32, (LANES, tile), 0)
    top = jnp.full((1, tile), NEGATIVE, jnp.float32)
    for b in range(blocks):
        lanes = pl.ds(pl.multiple_of(at[b] + begin, LANES), tile)
        s = s_ref[b * LANES : (b + 1) * LANES] * scale + bias_ref[0, :, lanes]
        s = jnp.where(frame < length - at[blocks + b], s, NEGATIVE)
        s_ref[b * LANES : (b + 1) * LANES] = s
        top = jnp.maximum(top, jnp.max(s, axis=0, keepdims=True))
    total = jnp.zeros((1, tile), jnp.float32)
    for b in range(blocks):
        p = jnp.exp(s_ref[b * LANES : (b + 1) * LANES] - top)
        total = total + jnp.sum(p, axis=0, keepdims=True)
        p_ref[b * LANES : (b + 1) * LANES] = p.astype(jnp.bfloat16)
    mixed = jnp.dot(vt_ref[...], p_ref[...], preferred_element_type=jnp.float32) / total
    out_ref[...] = mixed.T.astype(jnp.bfloat16)
    lse_ref[0] = top + jnp.log(total)


def attend(at, query, key, key_far, value, value_far, bias, heads, head_dim):
    queries, keys = query.shape[0], 2 * key.shape[0]
    tile = QUERY_TILE
    width = bias.shape[-1]
    grid_spec = pltpu.PrefetchScalarGridSpec(
        num_scalar_prefetch=1,
        grid=(heads, queries // tile),
        in_specs=[
            pl.BlockSpec((tile, head_dim), lambda h, i, at: (i, h)),
            pl.BlockSpec((keys // 2, head_dim), lambda h, i, at: (0, h)),
            pl.BlockSpec((keys // 2, head_dim), lambda h, i, at: (0, h)),
            pl.BlockSpec((keys // 2, head_dim), lambda h, i, at: (0, h)),
            pl.BlockSpec((keys // 2, head_dim), lambda h, i, at: (0, h)),
            pl.BlockSpec((1, LANES, width), lambda h, i, at: (h, 0, 0)),
        ],
        out_specs=[
            pl.BlockSpec((tile, head_dim), lambda h, i, at: (i, h)),
            pl.BlockSpec((1, 1, tile), lambda h, i, at: (h, 0, i)),
        ],
        scratch_shapes=[
            pltpu.VMEM((keys, head_dim), jnp.bfloat16),
            pltpu.VMEM((head_dim, keys), jnp.bfloat16),
            pltpu.VMEM((keys, tile), jnp.float32),
            pltpu.VMEM((keys, tile), jnp.bfloat16),
        ],
    )
    return pl.pallas_call(
        functools.partial(attend_kernel, head_dim ** (-0.5)),
        out_shape=[
            jax.ShapeDtypeStruct((queries, heads * head_dim), jnp.bfloat16),
            jax.ShapeDtypeStruct((heads, 1, queries), jnp.float32),
        ],
        grid_spec=grid_spec,
        compiler_params=pltpu.CompilerParams(vmem_limit_bytes=24 * MIB),
        cost_estimate=cost(
            4 * heads * queries * keys * head_dim,
            heads * queries * keys,
            4 * heads * LANES * width + 4 * heads * head_dim * (queries + keys),
        ),
        name="attend",
    )(at, query, key, key_far, value, value_far, bias)


def attend_back_kernel(
    scale, at, q_ref, k_pair, k_far, v_pair, v_far, do_ref, lse_ref, bias_ref,
    dq_ref, dk_ref, dv_ref, line_ref,
    k_ref, v_ref, kt_ref, s_ref, dp_ref, p_ref, ds_ref, dk_sum, dv_sum, skew_ref,
):
    tile = q_ref.shape[0]
    blocks = k_ref.shape[0] // LANES
    length = at[blocks * 2]
    pair = k_pair.shape[0]

    @pl.when(pl.program_id(1) == 0)
    def _():
        k_ref[:pair] = k_pair[...]
        k_ref[pair:] = k_far[...]
        v_ref[:pair] = v_pair[...]
        v_ref[pair:] = v_far[...]
        kt_ref[...] = k_ref[...].T
        dk_sum[...] = jnp.zeros_like(dk_sum)
        dv_sum[...] = jnp.zeros_like(dv_sum)
        skew_ref[...] = jnp.zeros_like(skew_ref)

    begin = pl.program_id(1) * tile
    s_ref[...] = lax.dot_general(
        k_ref[...], q_ref[...], (((1,), (1,)), ((), ())), preferred_element_type=jnp.float32
    )
    dp_ref[...] = lax.dot_general(
        v_ref[...], do_ref[...], (((1,), (1,)), ((), ())), preferred_element_type=jnp.float32
    )
    frame = lax.broadcasted_iota(jnp.int32, (LANES, tile), 0)
    lse = lse_ref[0]
    delta = jnp.zeros((1, tile), jnp.float32)
    for b in range(blocks):
        rows = slice(b * LANES, (b + 1) * LANES)
        lanes = pl.ds(pl.multiple_of(at[b] + begin, LANES), tile)
        s = s_ref[rows] * scale + bias_ref[0, :, lanes]
        s = jnp.where(frame < length - at[blocks + b], s, NEGATIVE)
        p = jnp.exp(s - lse)
        s_ref[rows] = p
        p_ref[rows] = p.astype(jnp.bfloat16)
        delta = delta + jnp.sum(p * dp_ref[rows], axis=0, keepdims=True)
    for b in range(blocks):
        rows = slice(b * LANES, (b + 1) * LANES)
        lanes = pl.ds(pl.multiple_of(at[b] + begin, LANES), tile)
        ds = (s_ref[rows] * (dp_ref[rows] - delta)).astype(jnp.bfloat16)
        ds_ref[rows] = ds
        skew_ref[:, lanes] += ds.astype(jnp.float32)
    dv_sum[...] += jnp.dot(p_ref[...], do_ref[...], preferred_element_type=jnp.float32)
    dk_sum[...] += jnp.dot(ds_ref[...], q_ref[...], preferred_element_type=jnp.float32)
    dq = jnp.dot(kt_ref[...], ds_ref[...], preferred_element_type=jnp.float32) * scale
    dq_ref[...] = dq.T.astype(jnp.bfloat16)

    @pl.when(pl.program_id(1) == pl.num_programs(1) - 1)
    def _():
        dk_ref[...] = (dk_sum[...] * scale).astype(jnp.bfloat16)
        dv_ref[...] = dv_sum[...].astype(jnp.bfloat16)
        lines = jnp.concatenate([skew_ref[...], jnp.zeros((LANES, LANES), jnp.float32)], axis=1)
        count = LANES // 2
        while count >= 8:
            lines = lines[count:] + pltpu.roll(lines[:count], count, 1)
            count //= 2
        line_ref[0] = lines


def attend_back(at, query, key, key_far, value, value_far, grad, lse, bias, heads, head_dim):
    queries, keys = query.shape[0], 2 * key.shape[0]
    tile = QUERY_TILE
    width = bias.shape[-1]
    grid_spec = pltpu.PrefetchScalarGridSpec(
        num_scalar_prefetch=1,
        grid=(heads, queries // tile),
        in_specs=[
            pl.BlockSpec((tile, head_dim), lambda h, i, at: (i, h)),
            pl.BlockSpec((keys // 2, head_dim), lambda h, i, at: (0, h)),
            pl.BlockSpec((keys // 2, head_dim), lambda h, i, at: (0, h)),
            pl.BlockSpec((keys // 2, head_dim), lambda h, i, at: (0, h)),
            pl.BlockSpec((keys // 2, head_dim), lambda h, i, at: (0, h)),
            pl.BlockSpec((tile, head_dim), lambda h, i, at: (i, h)),
            pl.BlockSpec((1, 1, tile), lambda h, i, at: (h, 0, i)),
            pl.BlockSpec((1, LANES, width), lambda h, i, at: (h, 0, 0)),
        ],
        out_specs=[
            pl.BlockSpec((tile, head_dim), lambda h, i, at: (i, h)),
            pl.BlockSpec((keys, head_dim), lambda h, i, at: (0, h)),
            pl.BlockSpec((keys, head_dim), lambda h, i, at: (0, h)),
            pl.BlockSpec((1, 8, width + LANES), lambda h, i, at: (h, 0, 0)),
        ],
        scratch_shapes=[
            pltpu.VMEM((keys, head_dim), jnp.bfloat16),
            pltpu.VMEM((keys, head_dim), jnp.bfloat16),
            pltpu.VMEM((head_dim, keys), jnp.bfloat16),
            pltpu.VMEM((keys, tile), jnp.float32),
            pltpu.VMEM((keys, tile), jnp.float32),
            pltpu.VMEM((keys, tile), jnp.bfloat16),
            pltpu.VMEM((keys, tile), jnp.bfloat16),
            pltpu.VMEM((keys, head_dim), jnp.float32),
            pltpu.VMEM((keys, head_dim), jnp.float32),
            pltpu.VMEM((LANES, width), jnp.float32),
        ],
    )
    return pl.pallas_call(
        functools.partial(attend_back_kernel, head_dim ** (-0.5)),
        out_shape=[
            jax.ShapeDtypeStruct((queries, heads * head_dim), jnp.bfloat16),
            jax.ShapeDtypeStruct((keys, heads * head_dim), jnp.bfloat16),
            jax.ShapeDtypeStruct((keys, heads * head_dim), jnp.bfloat16),
            jax.ShapeDtypeStruct((heads, 8, width + LANES), jnp.float32),
        ],
        grid_spec=grid_spec,
        compiler_params=pltpu.CompilerParams(vmem_limit_bytes=24 * MIB),
        cost_estimate=cost(
            10 * heads * queries * keys * head_dim,
            heads * queries * keys,
            4 * heads * LANES * width + 8 * heads * head_dim * (queries + keys),
        ),
        name="attend_back",
    )(at, query, key, key_far, value, value_far, grad, lse, bias)


def again_kernel(count, at, *refs):
    pieces, cuts = refs[:4], refs[4 : 4 + count]
    act_ref, slope_ref, rows = refs[4 + count :]
    tokens = pieces[0].shape[0]

    @pl.when(pl.program_id(0) == 0)
    def _():
        for k in range(4):
            rows[k * tokens : (k + 1) * tokens] = pieces[k][...]

    for k in range(count):
        block = cuts[k].shape[1]
        mid, slope = silu_pair(dot_turned(cuts[k][...].T, rows[...]))
        act_ref[k * block : (k + 1) * block] = mid.astype(jnp.bfloat16)
        slope_ref[k * block : (k + 1) * block] = slope.astype(jnp.bfloat16)


def column_cuts(weight, groups, parts, width):
    block = weight.shape[1] // groups // parts
    if block == width:
        return weight, lambda g, at: (0, g * parts + at[0])
    return None, lambda g, at: (0, g)


def again(place, pieces, weight, groups):
    parts = len(pieces)
    tokens, model = pieces[0].shape
    inner = weight.shape[1] // parts
    width = LANES
    source, where = column_cuts(weight, groups, parts, width)
    if source is None:
        source = take_columns(weight, groups, place, parts)
    count = 2
    cut = inner // width // count
    return pl.pallas_call(
        functools.partial(again_kernel, count),
        grid_spec=pltpu.PrefetchScalarGridSpec(
            num_scalar_prefetch=1,
            grid=(cut,),
            in_specs=[whole((tokens, model))] * parts
            + [
                pl.BlockSpec((model, width), lambda i, at, k=k: where(i * count + k, at))
                for k in range(count)
            ],
            out_specs=[pl.BlockSpec((count * width, parts * tokens), lambda i, at: (i, 0))] * 2,
            scratch_shapes=[pltpu.VMEM((parts * tokens, model), jnp.bfloat16)],
        ),
        out_shape=[jax.ShapeDtypeStruct((inner, parts * tokens), jnp.bfloat16)] * 2,
        compiler_params=pltpu.CompilerParams(vmem_limit_bytes=40 * MIB),
        cost_estimate=cost(
            2 * parts * tokens * model * inner,
            2 * parts * tokens * inner,
            2 * parts * tokens * (2 * inner + model) + 2 * model * inner,
        ),
        name="again",
    )(place.reshape(1), *pieces, *([source] * count))


def grad_out_kernel(act_ref, *refs):
    pieces, out_ref, rows = refs[:4], refs[4], refs[5]
    tokens = pieces[0].shape[0]

    @pl.when(pl.program_id(0) == 0)
    def _():
        for k in range(4):
            rows[k * tokens : (k + 1) * tokens] = pieces[k][...]

    out_ref[...] = dot(act_ref[...], rows[...]).astype(jnp.bfloat16)


def grad_out_of(act, pieces):
    inner, frames = act.shape
    tokens, model = pieces[0].shape
    step = 256
    return pl.pallas_call(
        grad_out_kernel,
        grid=(inner // step,),
        in_specs=[pl.BlockSpec((step, frames), lambda i: (i, 0))]
        + [whole((tokens, model))] * len(pieces),
        out_specs=pl.BlockSpec((step, model), lambda i: (i, 0)),
        out_shape=jax.ShapeDtypeStruct((inner, model), jnp.bfloat16),
        scratch_shapes=[pltpu.VMEM((frames, model), jnp.bfloat16)],
        compiler_params=pltpu.CompilerParams(vmem_limit_bytes=40 * MIB),
        cost_estimate=cost(
            2 * frames * model * inner,
            0,
            2 * frames * (inner + model) + 2 * model * inner,
        ),
        name="grad_out",
    )(act, *pieces)


def grad_in_kernel(count, at, slope_ref, *refs):
    acts, branches, cuts = refs[:4], refs[4:8], refs[8 : 8 + count]
    out_ref, act_rows, branch_rows = refs[8 + count :]
    tokens = acts[0].shape[0]

    @pl.when(pl.program_id(0) == 0)
    def _():
        for k in range(4):
            act_rows[k * tokens : (k + 1) * tokens] = acts[k][...]
            branch_rows[k * tokens : (k + 1) * tokens] = branches[k][...]

    cut = jnp.concatenate([c[...] for c in cuts], axis=0)
    d_hidden = (dot_turned(cut, branch_rows[...]) * slope_ref[...].astype(jnp.float32)).astype(jnp.bfloat16)
    out_ref[...] = dot(d_hidden, act_rows[...]).T.astype(jnp.bfloat16)


def grad_in_of(place, slope, acts, branches, weight, groups):
    inner, frames = slope.shape
    tokens, model = acts[0].shape
    parts = len(acts)
    width = LANES
    count = 2
    if weight.shape[0] // groups // parts == width:
        source, where = weight, lambda g, at: (g * parts + at[0], 0)
    else:
        source, where = take_rows(weight, groups, place, parts), lambda g, at: (g, 0)
    return pl.pallas_call(
        functools.partial(grad_in_kernel, count),
        grid_spec=pltpu.PrefetchScalarGridSpec(
            num_scalar_prefetch=1,
            grid=(inner // width // count,),
            in_specs=[pl.BlockSpec((count * width, frames), lambda i, at: (i, 0))]
            + [whole((tokens, model))] * (2 * parts)
            + [
                pl.BlockSpec((width, model), lambda i, at, k=k: where(i * count + k, at))
                for k in range(count)
            ],
            out_specs=pl.BlockSpec((model, count * width), lambda i, at: (0, i)),
            scratch_shapes=[pltpu.VMEM((frames, model), jnp.bfloat16)] * 2,
        ),
        out_shape=jax.ShapeDtypeStruct((model, inner), jnp.bfloat16),
        compiler_params=pltpu.CompilerParams(vmem_limit_bytes=40 * MIB),
        cost_estimate=cost(
            4 * frames * model * inner,
            0,
            2 * frames * (inner + 2 * model) + 4 * model * inner,
        ),
        name="grad_in",
    )(place.reshape(1), slope, *acts, *branches, *([source] * count))


def shards(
    features,
    lengths,
    buckets,
    gain_first,
    first_in,
    first_out,
    gain_attend,
    query_weight,
    key_weight,
    value_weight,
    output_weight,
    bias_table,
    gain_conv,
    point_in,
    depth_weight,
    batch_scale,
    batch_shift,
    point_out,
    gain_second,
    second_in,
    second_out,
    gain_final,
    cotangent,
):
    row_count, width, model = features.shape
    tokens = row_count * width
    heads, bucket_count = bias_table.shape
    head_dim = model // heads
    parts = lax.axis_size("tm")
    groups = lax.axis_size("rows")
    frames = width * parts
    half = depth_weight.shape[0] // 2
    taps = depth_weight.shape[0]
    place = lax.axis_index("tm")
    row_place = lax.axis_index("rows")
    side = place % 2
    far = place // 2
    offset = place * width
    near_heads = heads // 2
    pair = 2 * width
    info = jnp.stack([side, far, offset, lengths[0]]).astype(jnp.int32)

    def near_half(array, axis, index):
        size = array.shape[axis] // 2
        return lax.dynamic_slice_in_dim(array, index * size, size, axis)

    flat_features = features.reshape(tokens, model)
    after_first, act_first, slope_first, act_attend = first_forward(
        flat_features, gain_first, gain_attend, first_in, first_out
    )
    act_near, act_far = swap(act_attend, "tm", 1), swap(act_attend, "tm", 2)
    act_cross = swap(act_far, "tm", 1)

    near_table = lax.dynamic_slice_in_dim(bias_table, side * near_heads, near_heads, 0)
    span = pair + frames
    turned = jnp.pad(buckets[::-1], (0, 1), constant_values=-1)
    window = lax.dynamic_slice_in_dim(turned, far * pair, span, 0)
    one_hot = (window[:, None] == jnp.arange(bucket_count)[None, :]).astype(jnp.float32)
    bias_lines = lax.dot_general(
        near_table, one_hot, (((1,), (1,)), ((), ())), precision=lax.Precision.HIGHEST
    )
    bias = skewed(bias_lines[:, None, :])
    key_blocks = frames // LANES
    block = jnp.arange(key_blocks)
    block = (block + far * (key_blocks // 2)) % key_blocks
    at = jnp.concatenate([frames - LANES - LANES * block, LANES * block, lengths[:1]]).astype(jnp.int32)

    query, key, value = project(info, act_attend, act_near, (query_weight, key_weight, value_weight))
    key_far, value_far = project(info, act_far, act_cross, (key_weight, value_weight))
    mixed, lse = attend(at, query, key, key_far, value, value_far, bias, near_heads, head_dim)
    own_mixed = near_half(mixed, 0, side)
    other_mixed = swap(near_half(mixed, 0, 1 - side), "tm", 1)

    attended, after_attend, act_conv, joined_value, gate, gated = mix(
        info, own_mixed, other_mixed, output_weight, after_first, gain_conv, point_in
    )
    up = [(i, i + 1) for i in range(parts - 1)]
    down = [(j, i) for i, j in up]
    gated_before = lax.ppermute(gated[width - half :].astype(jnp.bfloat16), "tm", up)
    gated_after = lax.ppermute(gated[:half].astype(jnp.bfloat16), "tm", down)
    filtered, moments = filter_frames(info, gated, gated_before, gated_after, depth_weight)
    local_count = jnp.clip(lengths[0] - offset, 0, width).astype(jnp.float32)
    count, batch_mean, spread = mesh_moments(local_count, moments[0], moments[1])
    count = count[0]
    rstd_batch = lax.rsqrt(spread / count + EPS)
    stats = jnp.stack([batch_mean, rstd_batch, batch_scale, batch_shift])
    act_batch, act_second, output, branch_second, grad, d_branch, d_normal, second_sums = second_both(
        info, filtered, stats, after_attend, cotangent.reshape(tokens, model), gain_second, gain_final,
        point_out, second_in, second_out,
    )
    output = output.reshape(row_count, width, model)

    edge_before = lax.ppermute(
        jnp.concatenate([d_normal[width - half :], filtered[width - half :]], axis=0), "tm", up
    )
    edge_after = lax.ppermute(jnp.concatenate([d_normal[:half], filtered[:half]], axis=0), "tm", down)
    batch_grads = mesh_sum(second_sums[2:])
    branch_second = after(branch_second, batch_grads)
    d_joined, grad, d_attend, conv_small = conv_back(
        info, d_normal, filtered, edge_before, edge_after, stats, batch_grads / count, depth_weight,
        gated, gated_before, gated_after, joined_value, gate, point_in, after_attend, gain_conv, grad,
    )
    d_attend_near = swap(d_attend, "tm", 1)
    d_mixed = mixed_back(info, d_attend, d_attend_near, output_weight)
    d_query, d_key, d_value, skew_lines = attend_back(
        at, query, key, key_far, value, value_far, d_mixed, lse, bias, near_heads, head_dim
    )
    far_send, far_keep = input_back(info, (d_key, d_value), (pair, pair), (key_weight, value_weight), width)
    far_mine = far_keep + swap(far_send, "tm", 1).astype(jnp.float32)
    far_back = swap(far_mine.astype(jnp.bfloat16), "tm", 2)
    pair_send, pair_keep = input_back(
        info, (d_query, d_key, d_value), (0, 0, 0), (query_weight, key_weight, value_weight), width
    )
    d_input = pair_keep + swap(pair_send, "tm", 1).astype(jnp.float32) + far_back.astype(jnp.float32)
    _, scaled_attend, rstd_attend = normed_of(after_first, gain_attend)
    d_values, grad_gain_attend = norm_backward(d_input, scaled_attend, rstd_attend, gain_attend)
    grad = grad + d_values
    branch_first = (0.5 * grad).astype(jnp.bfloat16)
    branch_first_all = spread_tm(branch_first)
    grad_features, grad_gain_first = first_backward(
        info, grad, flat_features, gain_first, slope_first, first_in, first_out
    )
    grad_features = grad_features.reshape(row_count, width, model)

    act_first_all = spread_tm(act_first, act_far)
    mid_first, slope_first_part = again(place, act_first_all, first_in, groups)
    branch_second_all = spread_tm(branch_second)
    act_second_all = spread_tm(act_second, branch_second_all[2])
    mid_second, slope_second_part = again(place, act_second_all, second_in, groups)
    second_out_piece = reduce_rows(grad_out_of(mid_second, branch_second_all))
    second_in_piece = reduce_rows(
        grad_in_of(place, slope_second_part, act_second_all, branch_second_all, second_out, groups), True
    )
    first_out_piece = reduce_rows(grad_out_of(mid_first, branch_first_all))
    first_in_piece = reduce_rows(
        grad_in_of(place, slope_first_part, act_first_all, branch_first_all, first_out, groups), True
    )

    def near_exchange(array):
        return (near_half(array, 1, side), swap(near_half(array, 1, 1 - side), "tm", 1))

    conv_send, conv_keep = cross_grads(
        info,
        [
            ((act_conv, swap(act_conv, "tm", 1)), near_exchange(d_joined)),
            ((act_batch, swap(act_batch, "tm", 1)), near_exchange(d_branch)),
        ],
    )
    attend_send, attend_keep = cross_grads(
        info,
        [
            ((act_attend, act_near), (d_query,)),
            ((act_attend, act_near, act_far, act_cross), (d_key,)),
            ((act_attend, act_near, act_far, act_cross), (d_value,)),
            (
                (attended, swap(attended, "tm", 1)),
                (near_half(d_attend, 1, side), near_half(d_attend_near, 1, side)),
            ),
        ],
    )

    def far_sum(send, keep, *earlier):
        got = swap(after(send, *earlier), "tm", 2)
        return (keep.astype(jnp.float32) + got.astype(jnp.float32)).astype(jnp.bfloat16)

    conv_piece = reduce_rows(far_sum(conv_send, conv_keep, far_back))
    attend_piece = reduce_rows(far_sum(attend_send, attend_keep, branch_first_all[2]))
    second_in_pieces = spread_tm(second_in_piece, branch_first_all[2])
    second_out_pieces = spread_tm(second_out_piece, branch_first_all[2])
    conv_pieces = spread_tm(conv_piece, branch_first_all[2])
    attend_pieces = spread_tm(attend_piece)
    first_out_pieces = spread_tm(first_out_piece)
    first_in_pieces = spread_tm(first_in_piece)

    table_lines = sum(jnp.pad(skew_lines[:, r], ((0, 0), (7 - r, 0)))[:, :span] for r in range(8))
    near_grad = lax.dot_general(
        table_lines, one_hot, (((1,), (0,)), ((), ())), precision=lax.Precision.HIGHEST
    )
    grad_table = lax.dynamic_update_slice_in_dim(
        jnp.zeros((heads, bucket_count), jnp.float32), near_grad, side * near_heads, 0
    )
    small = jnp.concatenate(
        [
            grad_gain_first,
            grad_gain_attend[None],
            second_sums[:2],
            conv_small,
            jnp.pad(grad_table.reshape(1, -1), ((0, 0), (0, model - heads * bucket_count))),
        ],
        axis=0,
    )
    small = mesh_sum(small)
    share = model // groups
    gains = lax.dynamic_slice_in_dim(small[:5], row_place * share, share, 1)
    grad_depth = small[5 : 5 + taps]
    grad_table = small[5 + taps, : heads * bucket_count].reshape(heads, bucket_count)

    relative = jnp.arange(parts) ^ place
    crossed = (relative % 2) * 2 + relative // 2
    (grad_first_in,) = lay_columns(first_in_pieces, (model,), groups, relative)
    (grad_second_in,) = lay_columns(second_in_pieces, (model,), groups, relative)

    def lay_rows(pieces):
        size = pieces[0].shape[0]
        out = jnp.zeros((parts, size, model), jnp.float32)
        for k in range(parts):
            out = lax.dynamic_update_index_in_dim(out, pieces[k].astype(jnp.float32), place ^ k, 0)
        return out.reshape(parts * size, model)

    grad_first_out = lay_rows(first_out_pieces)
    grad_second_out = lay_rows(second_out_pieces)
    quarter = model // parts
    grad_query, grad_key, grad_value, grad_output = lay_columns(attend_pieces, (quarter,) * 4, 1, crossed)
    grad_point_in, grad_point_out = lay_columns(conv_pieces, (2 * quarter, quarter), 1, crossed)
    return (
        output,
        grad_features,
        gains[0],
        grad_first_in,
        grad_first_out,
        gains[1],
        grad_query,
        grad_key,
        grad_value,
        grad_output,
        grad_table,
        gains[4],
        grad_point_in,
        grad_depth,
        batch_grads[1],
        batch_grads[0],
        grad_point_out,
        gains[3],
        grad_second_in,
        grad_second_out,
        gains[2],
    )


def solution(mesh):
    rows3, rows2, rows1 = P("rows", "tm", None), P("rows", None), P("rows")
    in_specs = (rows3, rows1) + (P(),) * 20 + (rows3,)
    out_specs = (
        rows3, rows3, rows1, rows2, rows2, rows1, rows2, rows2, rows2, rows2, P(),
        rows1, rows2, P(), P(), P(), rows2, rows1, rows2, rows2, rows1,
    )
    return jax.shard_map(shards, mesh=mesh, in_specs=in_specs, out_specs=out_specs, check_vma=False)
```

time: 683 us -> 570 us (0.83)
  matrix products: 158 us -> 2.96 us
  Pallas kernels: 75.2 us -> 214 us
  other arithmetic: 90.3 us -> 19.3 us
  local copies, waits for them, and re-layouts: 78.9 us -> 57.7 us
  starting transfers between devices: 85.2 us -> 77.2 us
    pallas_call x2 -> x19, Pallas kernels: 11.3 us -> 169 us  [the longest x11 94.8 us: flow_call(): pl.pallas_call(kernel, in_specs=scalars() + [pl.BlockSpec(memory_space=pl...]
    dot_general x37 -> x0, matrix products: 155 us -> none  [the longest x16 60.2 us: weight_grad(): lax.dot_general(inputs, grad, (((0,), (0,)), ((), ())), preferred_element...]
    convert_element_type x20 -> x3, other arithmetic: 28.1 us -> 3.46 us  [the longest x2 2.85 us: far_sum(): (keep.astype(jnp.float32) + got.astype(jnp.float32)).astype(jnp.bfloat16)]
    dynamic_slice x4 -> x0, local copies, waits for them, and re-layouts: 17.6 us -> none  [the longest x2 11.2 us: reduce_rows(): keep = lax.dynamic_index_in_dim(pairs, mine, 1, keepdims=False)]
    reduce_sum x10 -> x2, other arithmetic: 13.9 us -> 0.45 us  [the longest x1 0.3 us: normed_of(): jnp.mean(centered * centered, axis=-1, keepdims=True) + EPS]
    pallas_call x1, Pallas kernels: 19.2 us -> 11.7 us  [attend(): pl.pallas_call(functools.partial(attend_kernel, head_dim ** (-0.5)), out_...]
    ppermute x78, starting transfers between devices: 78.1 us -> 71 us  [swap(): return lax.ppermute(value, axis, [(i, i ^ bit) for i in range(count)])]
    unnamed x364 -> x198, local copies, waits for them, and re-layouts: 38.8 us -> 41.1 us
  transfers between devices with their start and end apart: 82 -> 82, of which waited for: 24 -> 33; matrix products, arithmetic and copies ran while one was open for 38% -> 7% of each run, Pallas kernels for 8% -> 26%
where the time goes in v2:
time: 570 us; the launch traced here: 560 us
  Pallas kernels  214 us (38%)
  waiting for transfers between devices  185 us (32%)
  starting transfers between devices  77.2 us (14%)
  local copies, waits for them, and re-layouts  57.7 us (10%)
  other arithmetic  19.3 us (3%)
    ppermute x78, waiting for transfers between devices, swap(): return lax.ppermute(value, axis, [(i, i ^ bit) for i in range(count)])  182 us
    pallas_call x11, Pallas kernels, flow_call(): pl.pallas_call(kernel, in_specs=scalars() + [pl.BlockSpec(memory_space=pl...  94.8 us
    ppermute x78, starting transfers between devices, swap(): return lax.ppermute(value, axis, [(i, i ^ bit) for i in range(count)])  71 us
    unnamed x198, local copies, waits for them, and re-layouts  41.1 us
    pallas_call x2, Pallas kernels, again(): pl.pallas_call(functools.partial(again_kernel, count), grid_spec=pltpu.Pr...  23.5 us
    pallas_call x2, Pallas kernels, grad_in_of(): pl.pallas_call(functools.partial(grad_in_kernel, count), grid_spec=pltpu....  21.7 us
    pallas_call x1, Pallas kernels, attend_back(): pl.pallas_call(functools.partial(attend_back_kernel, head_dim ** (-0.5)),...  21.5 us
    pallas_call x1, Pallas kernels, first_forward(): pl.pallas_call(first_kernel, grid=(inner // BLOCK,), in_specs=[whole((tok...  12.4 us
  transfers between devices with their start and end apart: 82, of which 33 were waited for; matrix products, arithmetic and copies ran while one was open for 7% of the time, Pallas kernels for 26%

profile of v2, /device:TPU:0, one launch (start us, length us, event | category | flops | bytes accessed | tf_op | source)
XLA Modules:
  0.0 559.6 jit_solution(10586498589288935579)
XLA Ops:
  3.2 12.4 %first_forward.1 = (f32[384,1024]{1,0:T(8,128)S(1)}, bf16[384,1024]{1,0:T(8,128)(2,1)}, bf16[384,4096]{1,0:T(8,128)(2,1)S(1)}, bf16[384,1024]{1,0:T(8,128)(2,1)S(1)}) custom-call(bf16[384,1024]{1,0:T(8,128)(2,1)S(1)} %bitcast.171, f32[1,1024]{1,0:T(1,128)S(1)} %bitcast.176, f32[1,1024]{1,0:T(1,128)S(1)} %bitcast.173, bf16[1024,4096]{1,0:T(8,128)(2,1)} %refs_5_.6, ...), custom_call_target="tpu_custom_call" | custom-call | flops 3221225472 | bytes 9961472 | tf_op jit(solution)/shard_map/first_forward/pallas_call | solution.py:683
  17.3 3.0 collective-permute-start.1
  21.1 16.8 %collective-permute-done.1.refs_0_.refs_5_.refs_10_ = bf16[384,1024]{1,0:T(8,128)(2,1)} collective-permute-done((bf16[384,1024]{1,0:T(8,128)(2,1)S(1)}, bf16[384,1024]{1,0:T(8,128)(2,1)}, u32[]{:S(2)}, u32[]{:S(2)}) %collective-permute-start.1) | collective-permute-done | bytes 786464 | tf_op jit(solution)/shard_map/ppermute | solution.py:21
  40.9 4.3 bias_rows.1.bias_ref
  50.1 4.4 project.2
  54.6 5.2 project.3
  59.9 11.7 %attend.1 = (bf16[768,512]{1,0:T(8,128)(2,1)S(1)}, f32[4,1,768]{2,1,0:T(1,128)S(1)}) custom-call(s32[25]{0:T(128)S(1)} %pad_add_fusion.1.at, bf16[768,512]{1,0:T(8,128)(2,1)S(1)} %get-tuple-element.85.q_ref, bf16[768,512]{1,0:T(8,128)(2,1)S(1)} %get-tuple-element.86.k_pair, bf16[768,512]{1,0:T(8,128)(2,1)S(1)} %get-tuple-element.87.k_far, ...), custom_call_target="tpu_custom_call" | custom-call | flops 1207959552 | bytes 4587520 | tf_op jit(solution)/shard_map/attend/pallas_call | solution.py:870
  73.6 4.6 mix.1
  81.4 2.3 collective-permute-start.4
  85.0 2.7 collective-permute-done.5.refs_2_.refs_9_
  87.7 4.0 filter_frames.1
  92.8 2.4 collective-permute-start.6
  96.4 3.5 collective-permute-done.7
  101.6 2.2 collective-permute-done.8
  105.5 2.2 collective-permute-done.9
  107.8 2.7 collective-permute-start.10
  110.4 2.0 collective-permute-done.10
  114.9 30.8 %second_both.1 = (bf16[384,1024]{1,0:T(8,128)(2,1)}, bf16[384,1024]{1,0:T(8,128)(2,1)}, bf16[384,1024]{1,0:T(8,128)(2,1)}, bf16[384,1024]{1,0:T(8,128)(2,1)}, f3...) custom-call(s32[4]{0:T(128)S(1)} %pad_add_fusion.info, ...), custom_call_target="tpu_custom_call" | custom-call | flops 7247757312 | bytes 14962688 | tf_op jit(solution)/shard_map/second_both/pallas_call | solution.py:185
  149.7 17.3 %collective-permute-done.14 = f32[2,1024]{1,0:T(2,128)S(1)} collective-permute-done((f32[2,1024]{1,0:T(2,128)S(1)}, f32[2,1024]{1,0:T(2,128)S(1)}, u32[]{:S(2)}, u32[]{:S(2)}) %collective-permute-start.14) | collective-permute-done | bytes 8224 | tf_op jit(solution)/shard_map/ppermute | solution.py:21
  174.3 2.6 collective-permute-start.17
  183.8 11.2 %conv_back.1 = (bf16[384,2048]{1,0:T(8,128)(2,1)S(1)}, f32[384,1024]{1,0:T(8,128)S(1)}, bf16[384,1024]{1,0:T(8,128)(2,1)}, f32[6,1024]{1,0:T(8,128)S(1)}) custom-call(s32[4]{0:T(128)S(1)} %pad_add_fusion.info, f32[384,1024]{1,0:T(8,128)S(1)} %copy-done.46, f32[384,1024]{1,0:T(8,128)S(1)} %copy-done.45, f32[4,1024]{1,0:T(4,128)S(1)} %collective-permute-done.11.refs_2_, ...), custom_call_target="tpu_custom_call" | custom-call | flops 805306368 | bytes 8839168 | tf_op jit(solution)/shard_map/conv_back/pallas_call | solution.py:185
  198.0 2.0 collective-permute-start.18
  203.7 3.4 mixed_back.1.do_ref
  207.1 2.3 copy-done.12
  209.4 21.5 %attend_back.1 = (bf16[768,512]{1,0:T(8,128)(2,1)S(1)}, bf16[1536,512]{1,0:T(8,128)(2,1)S(1)}, bf16[1536,512]{1,0:T(8,128)(2,1)S(1)}, f32[4,8,2304]{2,1,0:T(8,128)S(1)}) custom-call(s32[25]{0:T(128)S(1)} %pad_add_fusion.1.at, bf16[768,512]{1,0:T(8,128)(2,1)S(1)} %copy-done.59, bf16[768,512]{1,0:T(8,128)(2,1)S(1)} %copy-done.61, ...), custom_call_target="tpu_custom_call" | custom-call | flops 3019898880 | bytes 6946816 | tf_op jit(solution)/shard_map/attend_back/pallas_call | solution.py:986
  231.0 3.3 input_back.3
  238.8 12.0 %again.2 = (bf16[1024,1536]{1,0:T(8,128)(2,1)S(1)}, bf16[1024,1536]{1,0:T(8,128)(2,1)S(1)}) custom-call(s32[1]{0:T(128)} %bitcast.25.at, bf16[384,1024]{1,0:T(8,128)(2,1)} %get-tuple-element.118.refs_0_, bf16[384,1024]{1,0:T(8,128)(2,1)} %collective-permute-done.27.refs_1_, bf16[384,1024]{1,0:T(8,128)(2,1)} %collective-permute-done.28.refs_2_, ...), custom_call_target="tpu_custom_call" | custom-call | flops 1610612736 | bytes 5767168 | tf_op jit(solution)/shard_map/again/pallas_call | solution.py:1039
  252.5 4.5 input_back.2
  258.9 2.3 add_convert_fusion.2
  272.6 8.4 %cross_grads.2 = (bf16[1024,1024]{1,0:T(8,128)(2,1)S(1)}, bf16[1024,1024]{1,0:T(8,128)(2,1)S(1)}) custom-call(s32[4]{0:T(128)S(1)} %pad_add_fusion.info, bf16[384,1024]{1,0:T(8,128)(2,1)S(1)} %copy-done.16, bf16[384,1024]{1,0:T(8,128)(2,1)S(1)} %copy-done.18, bf16[768,512]{1,0:T(8,128)(2,1)S(1)} %copy-done.29, bf16[384,1024]{1,0:T(8,128)(2,1)S(1)} %copy-done.16, ...), custom_call_target="tpu_custom_call" | custom-call | flops 2415919104 | bytes 9175040 | tf_op jit(solution)/shard_map/cross_grads/pallas_call | solution.py:185
  281.7 12.7 %collective-permute-done.21 = bf16[384,1024]{1,0:T(8,128)(2,1)} collective-permute-done((bf16[384,1024]{1,0:T(8,128)(2,1)}, bf16[384,1024]{1,0:T(8,128)(2,1)}, u32[]{:S(2)}, u32[]{:S(2)}) %collective-permute-start.21) | collective-permute-done | bytes 786464 | tf_op jit(solution)/shard_map/ppermute | solution.py:21
  294.4 2.3 multiply_reduce_fusion
  299.7 3.4 copy-done.2
  303.1 13.1 %first_backward.1 = (bf16[384,1024]{1,0:T(8,128)(2,1)}, f32[1,1024]{1,0:T(1,128)S(1)}) custom-call(s32[4]{0:T(128)S(1)} %pad_add_fusion.info, f32[384,1024]{1,0:T(8,128)S(1)} %get-tuple-element.151.refs_0_, bf16[384,1024]{1,0:T(8,128)(2,1)S(1)} %bitcast.172, f32[1,1024]{1,0:T(1,128)S(1)} %bitcast.177, bf16[384,4096]{1,0:T(8,128)(2,1)S(1)} %copy-done.38, ...), custom_call_target="tpu_custom_call" | custom-call | flops 3221225472 | bytes 11538432 | tf_op jit(solution)/shard_map/first_backward/pallas_call | solution.py:185
  316.5 11.5 %again.3 = (bf16[1024,1536]{1,0:T(8,128)(2,1)S(1)}, bf16[1024,1536]{1,0:T(8,128)(2,1)S(1)}) custom-call(s32[1]{0:T(128)} %bitcast.25.at, bf16[384,1024]{1,0:T(8,128)(2,1)} %get-tuple-element.142.refs_0_, bf16[384,1024]{1,0:T(8,128)(2,1)S(1)} %copy-done.31, bf16[384,1024]{1,0:T(8,128)(2,1)} %collective-permute-done.66.refs_2_, ...), custom_call_target="tpu_custom_call" | custom-call | flops 1610612736 | bytes 5767168 | tf_op jit(solution)/shard_map/again/pallas_call | solution.py:1039
  328.7 10.9 %grad_in.3 = bf16[1024,1024]{1,0:T(8,128)(2,1)S(1)} custom-call(s32[1]{0:T(128)} %bitcast.25.at, bf16[1024,1536]{1,0:T(8,128)(2,1)S(1)} %get-tuple-element.143.slope_ref, bf16[384,1024]{1,0:T(8,128)(2,1)} %get-tuple-element.142.refs_0_, bf16[384,1024]{1,0:T(8,128)(2,1)S(1)} %copy-done.31, bf16[384,1024]{1,0:T(8,128)(2,1)} %collective-permute-done.66.refs_2_, ...), custom_call_target="tpu_custom_call" | custom-call | flops 3221225472 | bytes 6815744 | tf_op jit(solution)/shard_map/grad_in/pallas_call | solution.py:1123
  346.1 6.4 %cross_grads.3 = (bf16[1024,768]{1,0:T(8,128)(2,1)}, bf16[1024,768]{1,0:T(8,128)(2,1)S(1)}) custom-call(s32[4]{0:T(128)S(1)} %pad_add_fusion.info, bf16[384,1024]{1,0:T(8,128)(2,1)} %get-tuple-element.129.refs_0_, bf16[384,1024]{1,0:T(8,128)(2,1)} %collective-permute-done.53.refs_1_, bf16[384,1024]{1,0:T(8,128)(2,1)S(1)} %copy-done.36, ...), custom_call_target="tpu_custom_call" | custom-call | flops 1207959552 | bytes 4325376 | tf_op jit(solution)/shard_map/cross_grads/pallas_call | solution.py:185
  356.5 6.4 %grad_out.3 = bf16[1024,1024]{1,0:T(8,128)(2,1)S(1)} custom-call(bf16[1024,1536]{1,0:T(8,128)(2,1)S(1)} %get-tuple-element.145.act_ref, bf16[384,1024]{1,0:T(8,128)(2,1)} %get-tuple-element.141.refs_4_.refs_0_, bf16[384,1024]{1,0:T(8,128)(2,1)} %collective-permute-done.68.refs_5_.refs_1_, bf16[384,1024]{1,0:T(8,128)(2,1)} %collective-permute-done.65.refs_6_.refs_2_, ...), custom_call_target="tpu_custom_call" | custom-call | flops 1610612736 | bytes 4194304 | tf_op jit(solution)/shard_map/grad_out/pallas_call | solution.py:1079
  362.9 7.5 %collective-permute-done.25 = f32[11,1024]{1,0:T(8,128)S(1)} collective-permute-done((f32[11,1024]{1,0:T(8,128)S(1)}, f32[11,1024]{1,0:T(8,128)S(1)}, u32[]{:S(2)}, u32[]{:S(2)}) %collective-permute-start.25) | collective-permute-done | bytes 45088 | tf_op jit(solution)/shard_map/ppermute | solution.py:21
  372.6 3.6 collective-permute-done.26
  381.1 2.0 fusion.1
  383.9 15.4 %collective-permute-done.76 = bf16[4,1,128,1024]{3,2,0,1:T(8,128)(2,1)} collective-permute-done((bf16[4,1,128,1024]{3,2,0,1:T(8,128)(2,1)}, bf16[4,1,128,1024]{3,2,0,1:T(8,128)(2,1)}, u32[]{:S(2)}, u32[]{:S(2)}) %collective-permute-start.76) | collective-permute-done | bytes 1048608 | tf_op jit(solution)/shard_map/ppermute | solution.py:21
  401.5 2.2 collective-permute-start.77
  403.7 10.7 %grad_in.2 = bf16[1024,1024]{1,0:T(8,128)(2,1)S(1)} custom-call(s32[1]{0:T(128)} %bitcast.25.at, bf16[1024,1536]{1,0:T(8,128)(2,1)S(1)} %copy-done.40, bf16[384,1024]{1,0:T(8,128)(2,1)} %get-tuple-element.118.refs_0_, bf16[384,1024]{1,0:T(8,128)(2,1)} %collective-permute-done.27.refs_1_, bf16[384,1024]{1,0:T(8,128)(2,1)} %collective-permute-done.28.refs_2_, ...), custom_call_target="tpu_custom_call" | custom-call | flops 3221225472 | bytes 6815744 | tf_op jit(solution)/shard_map/grad_in/pallas_call | solution.py:1123
  415.8 1.9 add_convert_fusion.1
  419.3 2.4 collective-permute-done.71
  423.6 2.1 collective-permute-done.77
  426.7 5.5 grad_out.2
  432.4 15.2 %collective-permute-done.78 = bf16[1,1,128,1024]{3,2,1,0:T(8,128)(2,1)S(1)} collective-permute-done((bf16[1,1,128,1024]{3,2,1,0:T(8,128)(2,1)S(1)}, bf16[1,1,128,1024]{3,2,1,0:T(8,128)(2,1)S(1)}, u32[]{:S(2)}, u32[]{:S(2)}) %collective-permute-start.78) | collective-permute-done | bytes 262176 | tf_op jit(solution)/shard_map/ppermute | solution.py:21
  450.4 6.8 %collective-permute-done.80 = bf16[128,1024]{1,0:T(8,128)(2,1)S(1)} collective-permute-done((bf16[128,1024]{1,0:T(8,128)(2,1)S(1)}, bf16[128,1024]{1,0:T(8,128)(2,1)S(1)}, u32[]{:S(2)}, u32[]{:S(2)}) %collective-permute-start.80) | collective-permute-done | bytes 262176 | tf_op jit(solution)/shard_map/ppermute | solution.py:21
  457.2 5.3 collective-permute-done.74.refs_2_
  464.7 2.8 collective-permute-start.59
  467.6 2.1 lay_columns.7
  476.9 3.2 collective-permute-start.60
  480.1 9.3 %collective-permute-done.39 = bf16[4,1,128,1024]{3,2,0,1:T(8,128)(2,1)S(1)} collective-permute-done((bf16[4,1,128,1024]{3,2,0,1:T(8,128)(2,1)S(1)}, bf16[4,1,128,1024]{3,2,0,1:T(8,128)(2,1)S(1)}, u32[]{:S(2)}, u32[]{:S(2)}) %collective-permute-start.39) | collective-permute-done | bytes 1048608 | tf_op jit(solution)/shard_map/ppermute | solution.py:21
  489.8 2.8 collective-permute-start.40
  492.7 15.7 %collective-permute-done.60 = bf16[1,1,128,768]{3,2,1,0:T(8,128)(2,1)S(1)} collective-permute-done((bf16[1,1,128,768]{3,2,1,0:T(8,128)(2,1)S(1)}, bf16[1,1,128,768]{3,2,1,0:T(8,128)(2,1)S(1)}, u32[]{:S(2)}, u32[]{:S(2)}) %collective-permute-start.60) | collective-permute-done | bytes 196640 | tf_op jit(solution)/shard_map/ppermute | solution.py:21
  511.3 2.8 collective-permute-start.48
  516.0 3.6 collective-permute-done.40
  521.8 12.4 %collective-permute-done.48 = bf16[2,1,128,1024]{3,2,1,0:T(8,128)(2,1)S(1)} collective-permute-done((bf16[2,1,128,1024]{3,2,1,0:T(8,128)(2,1)S(1)}, bf16[2,1,128,1024]{3,2,1,0:T(8,128)(2,1)S(1)}, u32[]{:S(2)}, u32[]{:S(2)}) %collective-permute-start.48) | collective-permute-done | bytes 524320 | tf_op jit(solution)/shard_map/ppermute | solution.py:21
  537.3 9.2 %collective-permute-done.49 = bf16[1,1,128,1024]{3,2,1,0:T(8,128)(2,1)S(1)} collective-permute-done((bf16[1,1,128,1024]{3,2,1,0:T(8,128)(2,1)S(1)}, bf16[1,1,128,1024]{3,2,1,0:T(8,128)(2,1)S(1)}, u32[]{:S(2)}, u32[]{:S(2)}) %collective-permute-start.49) | collective-permute-done | bytes 262176 | tf_op jit(solution)/shard_map/ppermute | solution.py:21
  549.9 5.0 collective-permute-done.51.refs_2_
  554.9 2.1 lay_columns.4
  557.2 2.0 lay_columns.5
  (442 shorter events, 127.7 us)
Async XLA Ops:
  17.3 20.6 %collective-permute-start.1 = (bf16[384,1024]{1,0:T(8,128)(2,1)S(1)}, bf16[384,1024]{1,0:T(8,128)(2,1)}, u32[]{:S(2)}, u32[]{:S(2)}) collective-permute-start(bf16[384,1024]{1,0:T(8,128)(2,1)S(1)} %get-tuple-element.84.refs_0_.refs_3_.refs_8_), channel_id=1, source_target_pairs={{0,2},{1,3},{2,0},{3,1},{4,6},{5,7},{6,4},{7,5},{8,10},{9,11},{10,... | collective-permute-start | bytes 2359304 | tf_op jit(solution)/shard_map/ppermute | solution.py:21
  20.3 25.0 %collective-permute-start = (bf16[384,1024]{1,0:T(8,128)(2,1)S(1)}, bf16[384,1024]{1,0:T(8,128)(2,1)S(1)}, u32[]{:S(2)}, u32[]{:S(2)}) collective-permute-start(bf16[384,1024]{1,0:T(8,128)(2,1)S(1)} %get-tuple-element.84.refs_0_.refs_3_.refs_8_), channel_id=1, source_target_pairs={{0,1},{1,0},{2,3},{3,2},{4,5},{5,4},{6,7},{7,6},{8,9},{9,8},{10,11... | collective-permute-start | bytes 2359304 | tf_op jit(solution)/shard_map/ppermute | solution.py:21
  37.9 16.6 %collective-permute-start.2 = (bf16[384,1024]{1,0:T(8,128)(2,1)}, bf16[384,1024]{1,0:T(8,128)(2,1)}, u32[]{:S(2)}, u32[]{:S(2)}) collective-permute-start(bf16[384,1024]{1,0:T(8,128)(2,1)} %collective-permute-done.1.refs_0_.refs_5_.refs_10_), channel_id=1, source_target_pairs={{0,1},{1,0},{2,3},{3,2},{4,5},{5,4},{6,7},{7,6},{8,9},{9,8},{10,11... | collective-permute-start | bytes 2359304 | tf_op jit(solution)/shard_map/ppermute | solution.py:21
  107.8 4.7 collective-permute-start.10
  146.6 92.1 %collective-permute-start.27 = (bf16[384,1024]{1,0:T(8,128)(2,1)}, bf16[384,1024]{1,0:T(8,128)(2,1)}, u32[]{:S(2)}, u32[]{:S(2)}) collective-permute-start(bf16[384,1024]{1,0:T(8,128)(2,1)} %get-tuple-element.118.refs_0_), channel_id=1, source_target_pairs={{0,1},{1,0},{2,3},{3,2},{4,5},{5,4},{6,7},{7,6},{8,9},{9,8},{10,11... | collective-permute-start | bytes 2359304 | tf_op jit(solution)/shard_map/ppermute | solution.py:21
  147.1 54.0 %collective-permute-start.28 = (bf16[384,1024]{1,0:T(8,128)(2,1)}, bf16[384,1024]{1,0:T(8,128)(2,1)}, u32[]{:S(2)}, u32[]{:S(2)}) collective-permute-start(bf16[384,1024]{1,0:T(8,128)(2,1)} %get-tuple-element.118.refs_0_), channel_id=1, source_target_pairs={{0,2},{1,3},{2,0},{3,1},{4,6},{5,7},{6,4},{7,5},{8,10},{9,11},{10,... | collective-permute-start | bytes 2359304 | tf_op jit(solution)/shard_map/ppermute | solution.py:21
  148.4 18.7 %collective-permute-start.14 = (f32[2,1024]{1,0:T(2,128)S(1)}, f32[2,1024]{1,0:T(2,128)S(1)}, u32[]{:S(2)}, u32[]{:S(2)}) collective-permute-start(f32[2,1024]{1,0:T(2,128)S(1)} %get-tuple-element.187), channel_id=1, source_target_pairs={{0,2},{1,3},{2,0},{3,1},{4,6},{5,7},{6,4},{7,5},{8,10},{9,11},{10,... | collective-permute-start | bytes 24584 | tf_op jit(solution)/shard_map/ppermute | solution.py:21
  172.3 7.9 %collective-permute-start.11 = (f32[4,1024]{1,0:T(4,128)S(1)}, f32[4,1024]{1,0:T(4,128)S(1)}, u32[]{:S(2)}, u32[]{:S(2)}) collective-permute-start(f32[4,1024]{1,0:T(4,128)S(1)} %pad_maximum_fusion.5), channel_id=1, source_target_pairs={{0,1},{1,2},{2,3},{4,5},{5,6},{6,7},{8,9},{9,10},{10,11},{12,13},{... | collective-permute-start | bytes 49160 | tf_op jit(solution)/shard_map/ppermute | solution.py:1241
  174.3 4.5 collective-permute-start.17
  201.1 37.7 %collective-permute-start.29 = (bf16[384,1024]{1,0:T(8,128)(2,1)}, bf16[384,1024]{1,0:T(8,128)(2,1)S(1)}, u32[]{:S(2)}, u32[]{:S(2)}) collective-permute-start(bf16[384,1024]{1,0:T(8,128)(2,1)} %collective-permute-done.28.refs_2_), channel_id=1, source_target_pairs={{0,1},{1,0},{2,3},{3,2},{4,5},{5,4},{6,7},{7,6},{8,9},{9,8},{10,11... | collective-permute-start | bytes 2359304 | tf_op jit(solution)/shard_map/ppermute | solution.py:21
  201.1 66.6 %collective-permute-start.45 = (bf16[384,1024]{1,0:T(8,128)(2,1)}, bf16[384,1024]{1,0:T(8,128)(2,1)}, u32[]{:S(2)}, u32[]{:S(2)}) collective-permute-start(bf16[384,1024]{1,0:T(8,128)(2,1)} %get-tuple-element.121.refs_13_), channel_id=1, source_target_pairs={{0,1},{1,0},{2,3},{3,2},{4,5},{5,4},{6,7},{7,6},{8,9},{9,8},{10,11... | collective-permute-start | bytes 2359304 | tf_op jit(solution)/shard_map/ppermute | solution.py:21
  201.6 56.0 %collective-permute-start.65 = (bf16[384,1024]{1,0:T(8,128)(2,1)}, bf16[384,1024]{1,0:T(8,128)(2,1)}, u32[]{:S(2)}, u32[]{:S(2)}) collective-permute-start(bf16[384,1024]{1,0:T(8,128)(2,1)} %get-tuple-element.141.refs_4_.refs_0_), channel_id=1, source_target_pairs={{0,2},{1,3},{2,0},{3,1},{4,6},{5,7},{6,4},{7,5},{8,10},{9,11},{10,... | collective-permute-start | bytes 2359304 | tf_op jit(solution)/shard_map/ppermute | solution.py:21
  234.3 24.6 %collective-permute-start.20 = (bf16[384,1024]{1,0:T(8,128)(2,1)S(1)}, bf16[384,1024]{1,0:T(8,128)(2,1)}, u32[]{:S(2)}, u32[]{:S(2)}) collective-permute-start(bf16[384,1024]{1,0:T(8,128)(2,1)S(1)} %get-tuple-element.111), channel_id=1, source_target_pairs={{0,1},{1,0},{2,3},{3,2},{4,5},{5,4},{6,7},{7,6},{8,9},{9,8},{10,11... | collective-permute-start | bytes 2359304 | tf_op jit(solution)/shard_map/ppermute | solution.py:21
  238.7 107.4 %collective-permute-start.53 = (bf16[384,1024]{1,0:T(8,128)(2,1)}, bf16[384,1024]{1,0:T(8,128)(2,1)}, u32[]{:S(2)}, u32[]{:S(2)}) collective-permute-start(bf16[384,1024]{1,0:T(8,128)(2,1)} %get-tuple-element.129.refs_0_), channel_id=1, source_target_pairs={{0,1},{1,0},{2,3},{3,2},{4,5},{5,4},{6,7},{7,6},{8,9},{9,8},{10,11... | collective-permute-start | bytes 2359304 | tf_op jit(solution)/shard_map/ppermute | solution.py:21
  257.0 24.0 %collective-permute-start.19 = (bf16[384,1024]{1,0:T(8,128)(2,1)}, bf16[384,1024]{1,0:T(8,128)(2,1)}, u32[]{:S(2)}, u32[]{:S(2)}) collective-permute-start(bf16[384,1024]{1,0:T(8,128)(2,1)} %get-tuple-element.109), channel_id=1, source_target_pairs={{0,1},{1,0},{2,3},{3,2},{4,5},{5,4},{6,7},{7,6},{8,9},{9,8},{10,11... | collective-permute-start | bytes 2359304 | tf_op jit(solution)/shard_map/ppermute | solution.py:21
  257.6 24.0 %collective-permute-start.66 = (bf16[384,1024]{1,0:T(8,128)(2,1)}, bf16[384,1024]{1,0:T(8,128)(2,1)}, u32[]{:S(2)}, u32[]{:S(2)}) collective-permute-start(bf16[384,1024]{1,0:T(8,128)(2,1)} %get-tuple-element.142.refs_0_), channel_id=1, source_target_pairs={{0,2},{1,3},{2,0},{3,1},{4,6},{5,7},{6,4},{7,5},{8,10},{9,11},{10,... | collective-permute-start | bytes 2359304 | tf_op jit(solution)/shard_map/ppermute | solution.py:21
  261.2 33.2 %collective-permute-start.21 = (bf16[384,1024]{1,0:T(8,128)(2,1)}, bf16[384,1024]{1,0:T(8,128)(2,1)}, u32[]{:S(2)}, u32[]{:S(2)}) collective-permute-start(bf16[384,1024]{1,0:T(8,128)(2,1)} %add_convert_fusion.2), channel_id=1, source_target_pairs={{0,2},{1,3},{2,0},{3,1},{4,6},{5,7},{6,4},{7,5},{8,10},{9,11},{10,... | collective-permute-start | bytes 2359304 | tf_op jit(solution)/shard_map/ppermute | solution.py:21
  267.7 29.8 %collective-permute-start.64 = (bf16[384,1024]{1,0:T(8,128)(2,1)}, bf16[384,1024]{1,0:T(8,128)(2,1)S(1)}, u32[]{:S(2)}, u32[]{:S(2)}) collective-permute-start(bf16[384,1024]{1,0:T(8,128)(2,1)} %get-tuple-element.142.refs_0_), channel_id=1, source_target_pairs={{0,1},{1,0},{2,3},{3,2},{4,5},{5,4},{6,7},{7,6},{8,9},{9,8},{10,11... | collective-permute-start | bytes 2359304 | tf_op jit(solution)/shard_map/ppermute | solution.py:21
  281.0 47.0 %collective-permute-start.68 = (bf16[384,1024]{1,0:T(8,128)(2,1)}, bf16[384,1024]{1,0:T(8,128)(2,1)}, u32[]{:S(2)}, u32[]{:S(2)}) collective-permute-start(bf16[384,1024]{1,0:T(8,128)(2,1)} %get-tuple-element.141.refs_4_.refs_0_), channel_id=1, source_target_pairs={{0,1},{1,0},{2,3},{3,2},{4,5},{5,4},{6,7},{7,6},{8,9},{9,8},{10,11... | collective-permute-start | bytes 2359304 | tf_op jit(solution)/shard_map/ppermute | solution.py:21
  281.6 47.0 %collective-permute-start.69 = (bf16[384,1024]{1,0:T(8,128)(2,1)}, bf16[384,1024]{1,0:T(8,128)(2,1)}, u32[]{:S(2)}, u32[]{:S(2)}) collective-permute-start(bf16[384,1024]{1,0:T(8,128)(2,1)} %collective-permute-done.65.refs_6_.refs_2_), channel_id=1, source_target_pairs={{0,1},{1,0},{2,3},{3,2},{4,5},{5,4},{6,7},{7,6},{8,9},{9,8},{10,11... | collective-permute-start | bytes 2359304 | tf_op jit(solution)/shard_map/ppermute | solution.py:21
  298.3 47.8 %collective-permute-start.55 = (bf16[384,1024]{1,0:T(8,128)(2,1)}, bf16[384,1024]{1,0:T(8,128)(2,1)}, u32[]{:S(2)}, u32[]{:S(2)}) collective-permute-start(bf16[384,1024]{1,0:T(8,128)(2,1)} %get-tuple-element.131.refs_4_), channel_id=1, source_target_pairs={{0,1},{1,0},{2,3},{3,2},{4,5},{5,4},{6,7},{7,6},{8,9},{9,8},{10,11... | collective-permute-start | bytes 2359304 | tf_op jit(solution)/shard_map/ppermute | solution.py:21
  299.7 46.4 %collective-permute-start.54 = (bf16[384,1024]{1,0:T(8,128)(2,1)}, bf16[384,1024]{1,0:T(8,128)(2,1)}, u32[]{:S(2)}, u32[]{:S(2)}) collective-permute-start(bf16[384,1024]{1,0:T(8,128)(2,1)} %get-tuple-element.163), channel_id=1, source_target_pairs={{0,1},{1,0},{2,3},{3,2},{4,5},{5,4},{6,7},{7,6},{8,9},{9,8},{10,11... | collective-permute-start | bytes 2359304 | tf_op jit(solution)/shard_map/ppermute | solution.py:21
  328.0 16.5 %collective-permute-start.56 = (bf16[384,512]{1,0:T(8,128)(2,1)S(1)}, bf16[384,512]{1,0:T(8,128)(2,1)S(1)}, u32[]{:S(2)}, u32[]{:S(2)}) collective-permute-start(bf16[384,512]{1,0:T(8,128)(2,1)S(1)} %copy-done.88), channel_id=1, source_target_pairs={{0,1},{1,0},{2,3},{3,2},{4,5},{5,4},{6,7},{7,6},{8,9},{9,8},{10,11... | collective-permute-start | bytes 1179656 | tf_op jit(solution)/shard_map/ppermute | solution.py:21
  328.6 11.1 %collective-permute-start.22 = (f32[11,1024]{1,0:T(8,128)S(1)}, f32[11,1024]{1,0:T(8,128)S(1)}, u32[]{:S(2)}, u32[]{:S(2)}) collective-permute-start(f32[11,1024]{1,0:T(8,128)S(1)} %concatenate.36), channel_id=1, source_target_pairs={{0,1},{1,0},{2,3},{3,2},{4,5},{5,4},{6,7},{7,6},{8,9},{9,8},{10,11... | collective-permute-start | bytes 135176 | tf_op jit(solution)/shard_map/ppermute | solution.py:21
  344.1 37.0 %collective-permute-start.70 = (bf16[2,2,128,1024]{3,2,1,0:T(8,128)(2,1)}, bf16[2,2,128,1024]{3,2,1,0:T(8,128)(2,1)}, u32[]{:S(2)}, u32[]{:S(2)}) collective-permute-start(bf16[2,2,128,1024]{3,2,1,0:T(8,128)(2,1)} %dynamic-slice_bitcast_fusion.1), channel_id=1, source_target_pairs={{0,8},{4,12},{8,0},{12,4},{16,24},{20,28},{24,16},{28,20},{1,9},{5... | collective-permute-start | bytes 3145736 | tf_op jit(solution)/shard_map/ppermute | solution.py:21
  344.5 10.2 %collective-permute-start.24 = (f32[11,1024]{1,0:T(8,128)S(1)}, f32[11,1024]{1,0:T(8,128)S(1)}, u32[]{:S(2)}, u32[]{:S(2)}) collective-permute-start(f32[11,1024]{1,0:T(8,128)S(1)} %add.512), channel_id=1, source_target_pairs={{0,4},{4,0},{8,12},{12,8},{16,20},{20,16},{24,28},{28,24},{1,5},{5... | collective-permute-start | bytes 135176 | tf_op jit(solution)/shard_map/ppermute | solution.py:21
  352.6 48.9 %collective-permute-start.30 = (bf16[384,1024]{1,0:T(8,128)(2,1)S(1)}, bf16[384,1024]{1,0:T(8,128)(2,1)}, u32[]{:S(2)}, u32[]{:S(2)}) collective-permute-start(bf16[384,1024]{1,0:T(8,128)(2,1)S(1)} %get-tuple-element.150.refs_4_.refs_0_), channel_id=1, source_target_pairs={{0,1},{1,0},{2,3},{3,2},{4,5},{5,4},{6,7},{7,6},{8,9},{9,8},{10,11... | collective-permute-start | bytes 2359304 | tf_op jit(solution)/shard_map/ppermute | solution.py:21
  352.7 26.9 %collective-permute-start.31 = (bf16[384,1024]{1,0:T(8,128)(2,1)S(1)}, bf16[384,1024]{1,0:T(8,128)(2,1)}, u32[]{:S(2)}, u32[]{:S(2)}) collective-permute-start(bf16[384,1024]{1,0:T(8,128)(2,1)S(1)} %get-tuple-element.150.refs_4_.refs_0_), channel_id=1, source_target_pairs={{0,2},{1,3},{2,0},{3,1},{4,6},{5,7},{6,4},{7,5},{8,10},{9,11},{10,... | collective-permute-start | bytes 2359304 | tf_op jit(solution)/shard_map/ppermute | solution.py:21
  354.4 60.3 %collective-permute-start.57 = (bf16[1024,768]{1,0:T(8,128)(2,1)}, bf16[1024,768]{1,0:T(8,128)(2,1)}, u32[]{:S(2)}, u32[]{:S(2)}) collective-permute-start(bf16[1024,768]{1,0:T(8,128)(2,1)} %get-tuple-element.135), channel_id=1, source_target_pairs={{0,2},{1,3},{2,0},{3,1},{4,6},{5,7},{6,4},{7,5},{8,10},{9,11},{10,... | collective-permute-start | bytes 4718600 | tf_op jit(solution)/shard_map/ppermute | solution.py:21
  354.8 15.7 %collective-permute-start.25 = (f32[11,1024]{1,0:T(8,128)S(1)}, f32[11,1024]{1,0:T(8,128)S(1)}, u32[]{:S(2)}, u32[]{:S(2)}) collective-permute-start(f32[11,1024]{1,0:T(8,128)S(1)} %add.513), channel_id=1, source_target_pairs={{0,8},{4,12},{8,0},{12,4},{16,24},{20,28},{24,16},{28,20},{1,9},{5... | collective-permute-start | bytes 135176 | tf_op jit(solution)/shard_map/ppermute | solution.py:21
  370.5 5.7 %collective-permute-start.26 = (f32[11,1024]{1,0:T(8,128)S(1)}, f32[11,1024]{1,0:T(8,128)S(1)}, u32[]{:S(2)}, u32[]{:S(2)}) collective-permute-start(f32[11,1024]{1,0:T(8,128)S(1)} %add.514), channel_id=1, source_target_pairs={{0,16},{4,20},{8,24},{12,28},{16,0},{20,4},{24,8},{28,12},{1,17},{... | collective-permute-start | bytes 135176 | tf_op jit(solution)/shard_map/ppermute | solution.py:21
  376.2 23.1 %collective-permute-start.76 = (bf16[4,1,128,1024]{3,2,0,1:T(8,128)(2,1)}, bf16[4,1,128,1024]{3,2,0,1:T(8,128)(2,1)}, u32[]{:S(2)}, u32[]{:S(2)}) collective-permute-start(bf16[4,1,128,1024]{3,2,0,1:T(8,128)(2,1)} %dynamic-slice_bitcast_fusion), channel_id=1, source_target_pairs={{0,4},{4,0},{8,12},{12,8},{16,20},{20,16},{24,28},{28,24},{1,5},{5... | collective-permute-start | bytes 3145736 | tf_op jit(solution)/shard_map/ppermute | solution.py:21
  379.6 90.7 %collective-permute-start.46 = (bf16[1024,1024]{1,0:T(8,128)(2,1)}, bf16[1024,1024]{1,0:T(8,128)(2,1)S(1)}, u32[]{:S(2)}, u32[]{:S(2)}) collective-permute-start(bf16[1024,1024]{1,0:T(8,128)(2,1)} %copy-done.82), channel_id=1, source_target_pairs={{0,2},{1,3},{2,0},{3,1},{4,6},{5,7},{6,4},{7,5},{8,10},{9,11},{10,... | collective-permute-start | bytes 6291464 | tf_op jit(solution)/shard_map/ppermute | solution.py:21
  381.1 22.6 %collective-permute-start.32 = (bf16[384,1024]{1,0:T(8,128)(2,1)}, bf16[384,1024]{1,0:T(8,128)(2,1)S(1)}, u32[]{:S(2)}, u32[]{:S(2)}) collective-permute-start(bf16[384,1024]{1,0:T(8,128)(2,1)} %collective-permute-done.31.refs_6_.refs_2_), channel_id=1, source_target_pairs={{0,1},{1,0},{2,3},{3,2},{4,5},{5,4},{6,7},{7,6},{8,9},{9,8},{10,11... | collective-permute-start | bytes 2359304 | tf_op jit(solution)/shard_map/ppermute | solution.py:21
  399.3 22.5 %collective-permute-start.71 = (bf16[1,2,128,1024]{3,2,1,0:T(8,128)(2,1)}, bf16[1,2,128,1024]{3,2,1,0:T(8,128)(2,1)S(1)}, u32[]{:S(2)}, u32[]{:S(2)}) collective-permute-start(bf16[1,2,128,1024]{3,2,1,0:T(8,128)(2,1)} %constant_dynamic-slice_fusion.2), channel_id=1, source_target_pairs={{0,16},{4,20},{8,24},{12,28},{16,0},{20,4},{24,8},{28,12},{1,17},{... | collective-permute-start | bytes 1572872 | tf_op jit(solution)/shard_map/ppermute | solution.py:21
  401.5 24.2 %collective-permute-start.77 = (bf16[2,1,128,1024]{3,2,1,0:T(8,128)(2,1)S(1)}, bf16[2,1,128,1024]{3,2,1,0:T(8,128)(2,1)S(1)}, u32[]{:S(2)}, u32[]{:S(2)}) collective-permute-start(bf16[2,1,128,1024]{3,2,1,0:T(8,128)(2,1)S(1)} %dynamic-slice_bitcast_fusion.6), channel_id=1, source_target_pairs={{0,8},{4,12},{8,0},{12,4},{16,24},{20,28},{24,16},{28,20},{1,9},{5... | collective-permute-start | bytes 1572872 | tf_op jit(solution)/shard_map/ppermute | solution.py:21
  414.5 55.3 %collective-permute-start.33 = (bf16[2,2,128,1024]{3,2,1,0:T(8,128)(2,1)S(1)}, bf16[2,2,128,1024]{3,2,1,0:T(8,128)(2,1)S(1)}, u32[]{:S(2)}, u32[]{:S(2)}) collective-permute-start(bf16[2,2,128,1024]{3,2,1,0:T(8,128)(2,1)S(1)} %dynamic-slice_bitcast_fusion.4), channel_id=1, source_target_pairs={{0,8},{4,12},{8,0},{12,4},{16,24},{20,28},{24,16},{28,20},{1,9},{5... | collective-permute-start | bytes 3145736 | tf_op jit(solution)/shard_map/ppermute | solution.py:21
  417.8 44.7 %collective-permute-start.58 = (bf16[4,1,128,768]{3,2,0,1:T(8,128)(2,1)S(1)}, bf16[4,1,128,768]{3,2,0,1:T(8,128)(2,1)S(1)}, u32[]{:S(2)}, u32[]{:S(2)}) collective-permute-start(bf16[4,1,128,768]{3,2,0,1:T(8,128)(2,1)S(1)} %dynamic-slice_bitcast_fusion.5), channel_id=1, source_target_pairs={{0,4},{4,0},{8,12},{12,8},{16,20},{20,16},{24,28},{28,24},{1,5},{5... | collective-permute-start | bytes 2359304 | tf_op jit(solution)/shard_map/ppermute | solution.py:21
  422.0 26.0 %collective-permute-start.72 = (bf16[1,1,128,1024]{3,2,1,0:T(8,128)(2,1)S(1)}, bf16[1,1,128,1024]{3,2,1,0:T(8,128)(2,1)S(1)}, u32[]{:S(2)}, u32[]{:S(2)}) collective-permute-start(bf16[1,1,128,1024]{3,2,1,0:T(8,128)(2,1)S(1)} %constant_dynamic-slice_fusion.1), channel_id=1, source_target_pairs={{0,4},{4,0},{8,12},{12,8},{16,20},{20,16},{24,28},{28,24},{1,5},{5... | collective-permute-start | bytes 786440 | tf_op jit(solution)/shard_map/ppermute | solution.py:21
  425.9 21.6 %collective-permute-start.78 = (bf16[1,1,128,1024]{3,2,1,0:T(8,128)(2,1)S(1)}, bf16[1,1,128,1024]{3,2,1,0:T(8,128)(2,1)S(1)}, u32[]{:S(2)}, u32[]{:S(2)}) collective-permute-start(bf16[1,1,128,1024]{3,2,1,0:T(8,128)(2,1)S(1)} %constant_dynamic-slice_fusion), channel_id=1, source_target_pairs={{0,16},{4,20},{8,24},{12,28},{16,0},{20,4},{24,8},{28,12},{1,17},{... | collective-permute-start | bytes 786440 | tf_op jit(solution)/shard_map/ppermute | solution.py:21
  448.0 9.2 %collective-permute-start.80 = (bf16[128,1024]{1,0:T(8,128)(2,1)S(1)}, bf16[128,1024]{1,0:T(8,128)(2,1)S(1)}, u32[]{:S(2)}, u32[]{:S(2)}) collective-permute-start(bf16[128,1024]{1,0:T(8,128)(2,1)S(1)} %fusion.20), channel_id=1, source_target_pairs={{0,2},{1,3},{2,0},{3,1},{4,6},{5,7},{6,4},{7,5},{8,10},{9,11},{10,... | collective-permute-start | bytes 786440 | tf_op jit(solution)/shard_map/ppermute | solution.py:21
  449.3 13.2 %collective-permute-start.74 = (bf16[128,1024]{1,0:T(8,128)(2,1)S(1)}, bf16[128,1024]{1,0:T(8,128)(2,1)S(1)}, u32[]{:S(2)}, u32[]{:S(2)}) collective-permute-start(bf16[128,1024]{1,0:T(8,128)(2,1)S(1)} %fusion.17.refs_0_), channel_id=1, source_target_pairs={{0,2},{1,3},{2,0},{3,1},{4,6},{5,7},{6,4},{7,5},{8,10},{9,11},{10,... | collective-permute-start | bytes 786440 | tf_op jit(solution)/shard_map/ppermute | solution.py:21
  457.2 6.1 %collective-permute-start.73 = (bf16[128,1024]{1,0:T(8,128)(2,1)S(1)}, bf16[128,1024]{1,0:T(8,128)(2,1)S(1)}, u32[]{:S(2)}, u32[]{:S(2)}) collective-permute-start(bf16[128,1024]{1,0:T(8,128)(2,1)S(1)} %fusion.17.refs_0_), channel_id=1, source_target_pairs={{0,1},{1,0},{2,3},{3,2},{4,5},{5,4},{6,7},{7,6},{8,9},{9,8},{10,11... | collective-permute-start | bytes 786440 | tf_op jit(solution)/shard_map/ppermute | solution.py:21
  462.5 7.2 %collective-permute-start.81 = (bf16[128,1024]{1,0:T(8,128)(2,1)S(1)}, bf16[128,1024]{1,0:T(8,128)(2,1)S(1)}, u32[]{:S(2)}, u32[]{:S(2)}) collective-permute-start(bf16[128,1024]{1,0:T(8,128)(2,1)S(1)} %collective-permute-done.80), channel_id=1, source_target_pairs={{0,1},{1,0},{2,3},{3,2},{4,5},{5,4},{6,7},{7,6},{8,9},{9,8},{10,11... | collective-permute-start | bytes 786440 | tf_op jit(solution)/shard_map/ppermute | solution.py:21
  463.3 26.1 %collective-permute-start.39 = (bf16[4,1,128,1024]{3,2,0,1:T(8,128)(2,1)S(1)}, bf16[4,1,128,1024]{3,2,0,1:T(8,128)(2,1)S(1)}, u32[]{:S(2)}, u32[]{:S(2)}) collective-permute-start(bf16[4,1,128,1024]{3,2,0,1:T(8,128)(2,1)S(1)} %dynamic-slice_bitcast_fusion.3), channel_id=1, source_target_pairs={{0,4},{4,0},{8,12},{12,8},{16,20},{20,16},{24,28},{28,24},{1,5},{5... | collective-permute-start | bytes 3145736 | tf_op jit(solution)/shard_map/ppermute | solution.py:21
  464.7 12.0 %collective-permute-start.59 = (bf16[2,1,128,768]{3,2,1,0:T(8,128)(2,1)S(1)}, bf16[2,1,128,768]{3,2,1,0:T(8,128)(2,1)S(1)}, u32[]{:S(2)}, u32[]{:S(2)}) collective-permute-start(bf16[2,1,128,768]{3,2,1,0:T(8,128)(2,1)S(1)} %dynamic-slice_bitcast_fusion.9), channel_id=1, source_target_pairs={{0,8},{4,12},{8,0},{12,4},{16,24},{20,28},{24,16},{28,20},{1,9},{5... | collective-permute-start | bytes 1179656 | tf_op jit(solution)/shard_map/ppermute | solution.py:21
  473.2 37.7 %collective-permute-start.47 = (bf16[4,1,128,1024]{3,2,0,1:T(8,128)(2,1)S(1)}, bf16[4,1,128,1024]{3,2,0,1:T(8,128)(2,1)S(1)}, u32[]{:S(2)}, u32[]{:S(2)}) collective-permute-start(bf16[4,1,128,1024]{3,2,0,1:T(8,128)(2,1)S(1)} %dynamic-slice_bitcast_fusion.2), channel_id=1, source_target_pairs={{0,4},{4,0},{8,12},{12,8},{16,20},{20,16},{24,28},{28,24},{1,5},{5... | collective-permute-start | bytes 3145736 | tf_op jit(solution)/shard_map/ppermute | solution.py:21
  474.3 39.8 %collective-permute-start.34 = (bf16[1,2,128,1024]{3,2,1,0:T(8,128)(2,1)S(1)}, bf16[1,2,128,1024]{3,2,1,0:T(8,128)(2,1)S(1)}, u32[]{:S(2)}, u32[]{:S(2)}) collective-permute-start(bf16[1,2,128,1024]{3,2,1,0:T(8,128)(2,1)S(1)} %constant_dynamic-slice_fusion.13), channel_id=1, source_target_pairs={{0,16},{4,20},{8,24},{12,28},{16,0},{20,4},{24,8},{28,12},{1,17},{... | collective-permute-start | bytes 1572872 | tf_op jit(solution)/shard_map/ppermute | solution.py:21
  476.9 31.5 %collective-permute-start.60 = (bf16[1,1,128,768]{3,2,1,0:T(8,128)(2,1)S(1)}, bf16[1,1,128,768]{3,2,1,0:T(8,128)(2,1)S(1)}, u32[]{:S(2)}, u32[]{:S(2)}) collective-permute-start(bf16[1,1,128,768]{3,2,1,0:T(8,128)(2,1)S(1)} %constant_dynamic-slice_fusion.3), channel_id=1, source_target_pairs={{0,16},{4,20},{8,24},{12,28},{16,0},{20,4},{24,8},{28,12},{1,17},{... | collective-permute-start | bytes 589832 | tf_op jit(solution)/shard_map/ppermute | solution.py:21
  489.8 29.8 %collective-permute-start.40 = (bf16[2,1,128,1024]{3,2,1,0:T(8,128)(2,1)S(1)}, bf16[2,1,128,1024]{3,2,1,0:T(8,128)(2,1)S(1)}, u32[]{:S(2)}, u32[]{:S(2)}) collective-permute-start(bf16[2,1,128,1024]{3,2,1,0:T(8,128)(2,1)S(1)} %dynamic-slice_bitcast_fusion.8), channel_id=1, source_target_pairs={{0,8},{4,12},{8,0},{12,4},{16,24},{20,28},{24,16},{28,20},{1,9},{5... | collective-permute-start | bytes 1572872 | tf_op jit(solution)/shard_map/ppermute | solution.py:21
  508.4 11.6 %collective-permute-start.61 = (bf16[128,768]{1,0:T(8,128)(2,1)S(1)}, bf16[128,768]{1,0:T(8,128)(2,1)S(1)}, u32[]{:S(2)}, u32[]{:S(2)}) collective-permute-start(bf16[128,768]{1,0:T(8,128)(2,1)S(1)} %fusion.18.refs_0_), channel_id=1, source_target_pairs={{0,1},{1,0},{2,3},{3,2},{4,5},{5,4},{6,7},{7,6},{8,9},{9,8},{10,11... | collective-permute-start | bytes 589832 | tf_op jit(solution)/shard_map/ppermute | solution.py:21
  508.5 7.5 %collective-permute-start.62 = (bf16[128,768]{1,0:T(8,128)(2,1)S(1)}, bf16[128,768]{1,0:T(8,128)(2,1)S(1)}, u32[]{:S(2)}, u32[]{:S(2)}) collective-permute-start(bf16[128,768]{1,0:T(8,128)(2,1)S(1)} %fusion.18.refs_0_), channel_id=1, source_target_pairs={{0,2},{1,3},{2,0},{3,1},{4,6},{5,7},{6,4},{7,5},{8,10},{9,11},{10,... | collective-permute-start | bytes 589832 | tf_op jit(solution)/shard_map/ppermute | solution.py:21
  511.3 22.8 %collective-permute-start.48 = (bf16[2,1,128,1024]{3,2,1,0:T(8,128)(2,1)S(1)}, bf16[2,1,128,1024]{3,2,1,0:T(8,128)(2,1)S(1)}, u32[]{:S(2)}, u32[]{:S(2)}) collective-permute-start(bf16[2,1,128,1024]{3,2,1,0:T(8,128)(2,1)S(1)} %dynamic-slice_bitcast_fusion.7), channel_id=1, source_target_pairs={{0,8},{4,12},{8,0},{12,4},{16,24},{20,28},{24,16},{28,20},{1,9},{5... | collective-permute-start | bytes 1572872 | tf_op jit(solution)/shard_map/ppermute | solution.py:21
  514.4 20.3 %collective-permute-start.35 = (bf16[1,1,128,1024]{3,2,1,0:T(8,128)(2,1)S(1)}, bf16[1,1,128,1024]{3,2,1,0:T(8,128)(2,1)S(1)}, u32[]{:S(2)}, u32[]{:S(2)}) collective-permute-start(bf16[1,1,128,1024]{3,2,1,0:T(8,128)(2,1)S(1)} %constant_dynamic-slice_fusion.12), channel_id=1, source_target_pairs={{0,4},{4,0},{8,12},{12,8},{16,20},{20,16},{24,28},{28,24},{1,5},{5... | collective-permute-start | bytes 786440 | tf_op jit(solution)/shard_map/ppermute | solution.py:21
  519.9 16.3 %collective-permute-start.41 = (bf16[1,1,128,1024]{3,2,1,0:T(8,128)(2,1)S(1)}, bf16[1,1,128,1024]{3,2,1,0:T(8,128)(2,1)S(1)}, u32[]{:S(2)}, u32[]{:S(2)}) collective-permute-start(bf16[1,1,128,1024]{3,2,1,0:T(8,128)(2,1)S(1)} %constant_dynamic-slice_fusion.11), channel_id=1, source_target_pairs={{0,16},{4,20},{8,24},{12,28},{16,0},{20,4},{24,8},{28,12},{1,17},{... | collective-permute-start | bytes 786440 | tf_op jit(solution)/shard_map/ppermute | solution.py:21
  534.4 12.1 %collective-permute-start.49 = (bf16[1,1,128,1024]{3,2,1,0:T(8,128)(2,1)S(1)}, bf16[1,1,128,1024]{3,2,1,0:T(8,128)(2,1)S(1)}, u32[]{:S(2)}, u32[]{:S(2)}) collective-permute-start(bf16[1,1,128,1024]{3,2,1,0:T(8,128)(2,1)S(1)} %constant_dynamic-slice_fusion.8), channel_id=1, source_target_pairs={{0,16},{4,20},{8,24},{12,28},{16,0},{20,4},{24,8},{28,12},{1,17},{... | collective-permute-start | bytes 786440 | tf_op jit(solution)/shard_map/ppermute | solution.py:21
  534.8 20.1 %collective-permute-start.36 = (bf16[128,1024]{1,0:T(8,128)(2,1)S(1)}, bf16[128,1024]{1,0:T(8,128)(2,1)S(1)}, u32[]{:S(2)}, u32[]{:S(2)}) collective-permute-start(bf16[128,1024]{1,0:T(8,128)(2,1)S(1)} %fusion.15.refs_0_), channel_id=1, source_target_pairs={{0,1},{1,0},{2,3},{3,2},{4,5},{5,4},{6,7},{7,6},{8,9},{9,8},{10,11... | collective-permute-start | bytes 786440 | tf_op jit(solution)/shard_map/ppermute | solution.py:21
  534.9 13.1 %collective-permute-start.37 = (bf16[128,1024]{1,0:T(8,128)(2,1)S(1)}, bf16[128,1024]{1,0:T(8,128)(2,1)S(1)}, u32[]{:S(2)}, u32[]{:S(2)}) collective-permute-start(bf16[128,1024]{1,0:T(8,128)(2,1)S(1)} %fusion.15.refs_0_), channel_id=1, source_target_pairs={{0,2},{1,3},{2,0},{3,1},{4,6},{5,7},{6,4},{7,5},{8,10},{9,11},{10,... | collective-permute-start | bytes 786440 | tf_op jit(solution)/shard_map/ppermute | solution.py:21
  536.3 13.0 %collective-permute-start.42 = (bf16[128,1024]{1,0:T(8,128)(2,1)S(1)}, bf16[128,1024]{1,0:T(8,128)(2,1)S(1)}, u32[]{:S(2)}, u32[]{:S(2)}) collective-permute-start(bf16[128,1024]{1,0:T(8,128)(2,1)S(1)} %fusion.19), channel_id=1, source_target_pairs={{0,1},{1,0},{2,3},{3,2},{4,5},{5,4},{6,7},{7,6},{8,9},{9,8},{10,11... | collective-permute-start | bytes 786440 | tf_op jit(solution)/shard_map/ppermute | solution.py:21
  536.5 12.7 %collective-permute-start.43 = (bf16[128,1024]{1,0:T(8,128)(2,1)S(1)}, bf16[128,1024]{1,0:T(8,128)(2,1)S(1)}, u32[]{:S(2)}, u32[]{:S(2)}) collective-permute-start(bf16[128,1024]{1,0:T(8,128)(2,1)S(1)} %fusion.19), channel_id=1, source_target_pairs={{0,2},{1,3},{2,0},{3,1},{4,6},{5,7},{6,4},{7,5},{8,10},{9,11},{10,... | collective-permute-start | bytes 786440 | tf_op jit(solution)/shard_map/ppermute | solution.py:21
  546.6 8.3 %collective-permute-start.51 = (bf16[128,1024]{1,0:T(8,128)(2,1)S(1)}, bf16[128,1024]{1,0:T(8,128)(2,1)S(1)}, u32[]{:S(2)}, u32[]{:S(2)}) collective-permute-start(bf16[128,1024]{1,0:T(8,128)(2,1)S(1)} %fusion.16.refs_0_), channel_id=1, source_target_pairs={{0,2},{1,3},{2,0},{3,1},{4,6},{5,7},{6,4},{7,5},{8,10},{9,11},{10,... | collective-permute-start | bytes 786440 | tf_op jit(solution)/shard_map/ppermute | solution.py:21
  548.0 6.9 %collective-permute-start.38 = (bf16[128,1024]{1,0:T(8,128)(2,1)S(1)}, bf16[128,1024]{1,0:T(8,128)(2,1)S(1)}, u32[]{:S(2)}, u32[]{:S(2)}) collective-permute-start(bf16[128,1024]{1,0:T(8,128)(2,1)S(1)} %collective-permute-done.37.refs_2_), channel_id=1, source_target_pairs={{0,1},{1,0},{2,3},{3,2},{4,5},{5,4},{6,7},{7,6},{8,9},{9,8},{10,11... | collective-permute-start | bytes 786440 | tf_op jit(solution)/shard_map/ppermute | solution.py:21
  549.2 7.9 %collective-permute-start.44 = (bf16[128,1024]{1,0:T(8,128)(2,1)S(1)}, bf16[128,1024]{1,0:T(8,128)(2,1)S(1)}, u32[]{:S(2)}, u32[]{:S(2)}) collective-permute-start(bf16[128,1024]{1,0:T(8,128)(2,1)S(1)} %collective-permute-done.43), channel_id=1, source_target_pairs={{0,1},{1,0},{2,3},{3,2},{4,5},{5,4},{6,7},{7,6},{8,9},{9,8},{10,11... | collective-permute-start | bytes 786440 | tf_op jit(solution)/shard_map/ppermute | solution.py:21
  549.3 7.9 %collective-permute-start.50 = (bf16[128,1024]{1,0:T(8,128)(2,1)S(1)}, bf16[128,1024]{1,0:T(8,128)(2,1)S(1)}, u32[]{:S(2)}, u32[]{:S(2)}) collective-permute-start(bf16[128,1024]{1,0:T(8,128)(2,1)S(1)} %fusion.16.refs_0_), channel_id=1, source_target_pairs={{0,1},{1,0},{2,3},{3,2},{4,5},{5,4},{6,7},{7,6},{8,9},{9,8},{10,11... | collective-permute-start | bytes 786440 | tf_op jit(solution)/shard_map/ppermute | solution.py:21
  (116 other events, 1044.2 us)

commit v3 on v2

--- a/solution.py
+++ b/solution.py
@@ -10,10 +10,9 @@
 EPS = 1e-05
 NEGATIVE = -1e30
 LANES = 128
-QUERY_TILE = 768
 MIB = 1024 * 1024
 BLOCK = 1024
-EFFORT = 0.5
+EFFORT = 0.0005
 
 
 def swap(value, axis, bit):
@@ -21,70 +20,39 @@
     return lax.ppermute(value, axis, [(i, i ^ bit) for i in range(count)])
 
 
-def mesh_sum(value):
-    for axis in ("tm", "rows"):
-        bit = 1
-        while bit < lax.axis_size(axis):
-            value = value + swap(value, axis, bit)
-            bit *= 2
+def hops():
+    wide, deep = lax.axis_size("tm"), lax.axis_size("rows")
+    found = [("tm", 1 << b) for b in range(wide.bit_length() - 1)][::-1]
+    return found + [("rows", 1 << b) for b in range(deep.bit_length() - 1)]
+
+
+def mesh_sum(value, steps):
+    for axis, bit in steps:
+        value = value + swap(value, axis, bit)
     return value
 
 
 def mesh_moments(count, mean, spread):
-    for axis in ("tm", "rows"):
-        bit = 1
-        while bit < lax.axis_size(axis):
-            sent = jnp.concatenate([mean[None], spread[None], jnp.broadcast_to(count, (1, mean.shape[0]))])
-            got = swap(sent, axis, bit)
-            other_mean, other_spread, other_count = got[0], got[1], got[2]
-            total = count + other_count
-            safe = jnp.maximum(total, 1.0)
-            gap = other_mean - mean
-            spread = spread + other_spread + gap * gap * (count * other_count / safe)
-            mean = (count * mean + other_count * other_mean) / safe
-            count = total
-            bit *= 2
+    for axis, bit in hops():
+        sent = jnp.concatenate([mean[None], spread[None], jnp.broadcast_to(count, (1, mean.shape[0]))])
+        got = swap(sent, axis, bit)
+        other_mean, other_spread, other_count = got[0], got[1], got[2]
+        total = count + other_count
+        safe = jnp.maximum(total, 1.0)
+        gap = other_mean - mean
+        spread = spread + other_spread + gap * gap * (count * other_count / safe)
+        mean = (count * mean + other_count * other_mean) / safe
+        count = total
     return (count, mean, spread)
 
 
-def after(value, *earlier):
-    return lax.optimization_barrier((value, *earlier))[0]
-
-
-def reduce_rows(partial, far_first=False):
-    size = lax.axis_size("rows")
-    place = lax.axis_index("rows")
-    bits = size.bit_length() - 1
-    order = list(range(bits))
-    if far_first:
-        order = order[1:] + order[:1]
-    inner = (partial.shape[0] // size, partial.shape[1])
-    left = partial.reshape((2,) * bits + inner)
-    held = list(range(bits))[::-1]
-    for bit in order:
-        axis = held.index(bit)
-        mine = (place >> bit) & 1
-        front = left.shape[:axis]
-        rows = 1
-        for n in left.shape[axis + 1 : -2]:
-            rows *= n
-        lead = 1
-        for n in front:
-            lead *= n
-        cut = left.reshape((lead, 2, rows) + inner)
-        keep = lax.dynamic_index_in_dim(cut, mine, 1, keepdims=False)
-        send = lax.dynamic_index_in_dim(cut, 1 - mine, 1, keepdims=False)
-        got = swap(send, "rows", 1 << bit)
-        left = (keep.astype(jnp.float32) + got.astype(jnp.float32)).astype(jnp.bfloat16)
-        held.remove(bit)
-        left = left.reshape((2,) * len(held) + inner)
-    return left
-
-
-def spread_tm(piece, *earlier):
-    near = swap(piece, "tm", 1)
-    far = swap(after(piece, *earlier) if earlier else piece, "tm", 2)
-    return [piece, near, far, swap(far, "tm", 1)]
+def tie(*values):
+    return lax.optimization_barrier(values)
+
+
+def spread_tm(piece):
+    far = swap(piece, "tm", 2)
+    return [piece, swap(piece, "tm", 1), far, swap(far, "tm", 1)]
 
 
 def silu_pair(hidden):
@@ -121,6 +89,10 @@
     return [pl.BlockSpec(memory_space=pltpu.SMEM)]
 
 
+def in_hbm(value):
+    return pltpu.with_memory_space_constraint(value, pltpu.HBM)
+
+
 def struct(*shape, kind=jnp.bfloat16):
     return jax.ShapeDtypeStruct(shape, kind)
 
@@ -146,21 +118,21 @@
 
 class Leaving:
     def __init__(self, source, target, sem):
-        self.copy = pltpu.make_async_copy(source, target, sem)
         self.ref = source
-        self.sent = False
-
-    def send(self):
+        self.target, self.sem = target, sem
+        self.copy = None
+
+    def send(self, source=None):
+        self.copy = pltpu.make_async_copy(self.ref if source is None else source, self.target, self.sem)
         self.copy.start()
-        self.sent = True
-
-
-def flow_call(body, name, outs, scratch, info, operands, flops, mib=24, raw=()):
+
+
+def flow_call(body, name, outs, scratch, info, operands, flops, mib=24, raw=(), late=(), deps=()):
     ins, results = len(operands), len(outs)
 
     def kernel(info, *refs):
-        sources, targets = refs[:ins], refs[ins : ins + results]
-        rest = refs[ins + results :]
+        sources, targets = refs[:ins], refs[ins + len(deps) : ins + len(deps) + results]
+        rest = refs[ins + len(deps) + results :]
         held, made = rest[:ins], rest[ins : ins + results]
         extra, sem_in, sem_out = rest[ins + results : -2], rest[-2], rest[-1]
         arriving = [
@@ -168,12 +140,12 @@
             for k in range(ins)
         ]
         for k in range(ins):
-            if k not in raw:
+            if k not in raw and k not in late:
                 arriving[k].start()
         leaving = [Leaving(made[k], targets[k], sem_out.at[k]) for k in range(results)]
         body(info, arriving, leaving, *extra)
         for item in leaving:
-            if not item.sent:
+            if item.copy is None:
                 item.send()
         for k in range(ins):
             if k not in raw:
@@ -184,16 +156,16 @@
     moved = sum(o.size * o.dtype.itemsize for o in (*operands, *outs))
     return pl.pallas_call(
         kernel,
-        in_specs=scalars() + [pl.BlockSpec(memory_space=pl.ANY)] * ins,
-        out_specs=[pl.BlockSpec(memory_space=pl.ANY)] * results,
-        out_shape=outs,
+        in_specs=scalars() + [pl.BlockSpec(memory_space=pltpu.HBM)] * (ins + len(deps)),
+        out_specs=[pl.BlockSpec(memory_space=pltpu.HBM)] * results,
+        out_shape=[pltpu.HBM(o.shape, o.dtype) for o in outs],
         scratch_shapes=[pltpu.VMEM(o.shape, o.dtype) for o in (*operands, *outs)]
         + list(scratch)
         + [pltpu.SemaphoreType.DMA((ins,)), pltpu.SemaphoreType.DMA((results,))],
         compiler_params=pltpu.CompilerParams(vmem_limit_bytes=mib * MIB),
         cost_estimate=cost(flops, 0, moved),
         name=name,
-    )(info, *operands)
+    )(info, *[in_hbm(o) for o in (*operands, *deps)])
 
 
 def cost(flops, transcendentals, moved):
@@ -202,7 +174,110 @@
     )
 
 
-SIDE, FAR, OFFSET, LENGTH = range(4)
+SIDE, FAR, OFFSET, LENGTH, ROW = range(5)
+
+
+def row_bits():
+    return lax.axis_size("rows").bit_length() - 1
+
+
+def take_half(source, index, lead, size, ways=2):
+    return [
+        source[pl.ds(pl.multiple_of((k * ways + index) * size, size), size)] for k in range(lead)
+    ]
+
+
+def phases():
+    return [(bit, 1) for bit in range(row_bits())]
+
+
+def total_of(parts):
+    total = parts[0].astype(jnp.float32)
+    for part in parts[1:]:
+        total = total + part.astype(jnp.float32)
+    return total.astype(jnp.bfloat16)
+
+
+def merge_kernel(counts, low, wide, share, info, ins, outs):
+    ways = 1 << wide
+    mine = (info[ROW] >> low) & (ways - 1)
+    at = 0
+    groups = []
+    for count in counts:
+        groups.append([item.get for item in ins[at : at + count]])
+        at += count
+    for g, gets in enumerate(groups):
+        held = [get() for get in gets]
+        lead = held[0].shape[0] // share // ways
+        for offset in list(range(1, ways)) + [0]:
+            out = outs[g * ways + (offset - 1) % ways]
+            parts = [take_half(h, mine ^ offset, lead, share, ways) for h in held]
+            for k in range(lead):
+                out.ref[k * share : (k + 1) * share] = total_of([p[k] for p in parts])
+            out.send()
+
+
+def join_kernel(counts, info, ins, outs):
+    begin = at = 0
+    for count in counts:
+        held = [item.get()[...] for item in ins[at : at + count]]
+        at += count
+        width = held[0].shape[1]
+        outs[0].ref[:, begin : begin + width] = total_of(held)
+        begin += width
+
+
+class RowSum:
+    def __init__(self, send, keep, share):
+        self.share = share
+        self.left = phases()
+        self.exchange([send], keep)
+
+    def exchange(self, sends, keep):
+        low, _ = self.left.pop(0)
+        self.terms = [keep] + [swap(x, "rows", (k + 1) << low) for k, x in enumerate(sends)]
+
+
+def merge(info, sums, *deps):
+    low, wide = sums[0].left[0]
+    ways = 1 << wide
+    outs = []
+    for total in sums:
+        rows, columns = total.terms[0].shape
+        outs += [struct(rows // ways, columns)] * ways
+    made = flow_call(
+        functools.partial(merge_kernel, [len(t.terms) for t in sums], low, wide, sums[0].share), "merge",
+        outs, [], info, tuple(x for t in sums for x in t.terms), 0, deps=deps,
+    )
+    for k, total in enumerate(sums):
+        part = made[k * ways : (k + 1) * ways]
+        total.exchange(part[:-1], part[-1])
+    return sums[-1].terms[0]
+
+
+def joined(info, sums, *deps):
+    while sums[0].left:
+        merge(info, sums)
+    return join(info, [t.terms for t in sums], *deps)
+
+
+def join(info, groups, *deps):
+    columns = sum(g[0].shape[1] for g in groups)
+    return flow_call(
+        functools.partial(join_kernel, [len(g) for g in groups]), "join",
+        [struct(groups[0][0].shape[0], columns)], [], info, tuple(x for g in groups for x in g), 0, deps=deps,
+    )[0]
+
+
+def opened(info, keep, got, share, *deps):
+    rows, columns = keep.shape
+    return RowSum(
+        *flow_call(
+            functools.partial(merge_kernel, [2], 0, 1, share), "merge",
+            [struct(rows // 2, columns)] * 2, [], info, (keep, got), 0, deps=deps,
+        ),
+        share,
+    )
 
 
 def project_kernel(info, ins, outs, sem, rows):
@@ -225,7 +300,7 @@
         out.send()
 
 
-def project(info, mine, other, weights):
+def project(info, mine, other, weights, deps=()):
     tokens, model = mine.shape
     pair = 2 * tokens
     return flow_call(
@@ -234,6 +309,7 @@
         [pltpu.SemaphoreType.DMA((len(weights),)), pltpu.VMEM((pair, model), jnp.bfloat16)],
         info, (mine, other, *weights), pair * model * model * len(weights),
         raw=tuple(range(2, 2 + len(weights))),
+        deps=deps,
     )
 
 
@@ -243,7 +319,7 @@
 
 
 def mix_kernel(
-    info, own_ref, other_ref, weight, state_ref, gain_ref, value_w, gate_w,
+    info, own_ref, other_ref, weight, state_ref, gain_ref, value_w, gate_w, dep,
     attended_ref, after_ref, act_ref, value_ref, gate_ref, gated_ref,
 ):
     side = info[SIDE]
@@ -264,7 +340,7 @@
     gated_ref[...] = value * gate * rows_of(info[LENGTH], info[OFFSET], tokens)
 
 
-def mix(info, own, other, weight, state, gain, point_in):
+def mix(info, own, other, weight, state, gain, point_in, dep):
     tokens, model = state.shape
     step = 512
     steps = model // step
@@ -277,11 +353,12 @@
             whole(own.shape), whole(own.shape), whole(weight.shape), whole(flat), whole((1, model)),
             pl.BlockSpec((model, step), lambda i: (0, i)),
             pl.BlockSpec((model, step), lambda i: (0, steps + i)),
+            pl.BlockSpec(memory_space=pl.ANY),
         ],
         out_specs=[whole(flat)] * 3 + [column] * 3,
         out_shape=[
-            struct(*flat), struct(*flat, kind=jnp.float32), struct(*flat),
-            struct(*flat), struct(*flat), struct(*flat, kind=jnp.float32),
+            pltpu.HBM(flat, jnp.bfloat16), pltpu.HBM(flat, jnp.float32), pltpu.HBM(flat, jnp.bfloat16),
+            pltpu.HBM(flat, jnp.bfloat16), pltpu.HBM(flat, jnp.bfloat16), pltpu.HBM(flat, jnp.float32),
         ],
         compiler_params=pltpu.CompilerParams(vmem_limit_bytes=32 * MIB),
         cost_estimate=cost(
@@ -290,7 +367,7 @@
             6 * model * model + 20 * tokens * model,
         ),
         name="mix",
-    )(info, own, other, weight, state, gain[None], point_in, point_in)
+    )(info, own, other, weight, state, gain[None], point_in, point_in, in_hbm(dep))
 
 
 def filter_kernel(info, ins, outs, wide):
@@ -335,18 +412,14 @@
     return at
 
 
-def second_kernel(info, ins, outs, sem, state, grad, total, slopes):
+def second_kernel(info, ins, outs, sem, state, grad, total, slopes, low_ref):
     filtered, stats, state_in, cot, gain, final_gain, point, pair_in, pair_out = ins
     w_in, w_out = pair_in[1], pair_out[1]
-    act_batch, act_out, output, branch_out, grad_out, conv_out, d_norm_out, sums = outs
+    act_batch, act_out, output, branch_out, grad_out, conv_send, conv_keep, d_norm_out, sums = outs
     tokens = filtered.target.shape[0]
     steps = w_in.shape[1] // BLOCK
     valid = rows_of(info[LENGTH], info[OFFSET], tokens)
     copies = weight_copies(pair_in, pair_out, sem, BLOCK)
-    for i in range(steps):
-        for copy in copies(i):
-            copy.start()
-
     filtered_ref, stats_ref = filtered.get(), stats.get()
 
     def normalized():
@@ -355,18 +428,29 @@
 
     act = silu_pair(normalized()[1])[0].astype(jnp.bfloat16)
     act_batch.ref[...] = act
+    point_ref = point.get()
+    for i in range(2):
+        for copy in copies(i):
+            copy.start()
     act_batch.send()
-    values = state_in.get()[...] + dot(act, point.get()[...])
+    values = state_in.get()[...] + dot(act, point_ref[...])
     state[...] = values
     act_ref = act_out.ref
     act_ref[...] = normed_of(values, gain.get()[...])[0].astype(jnp.bfloat16)
     act_out.send()
+    cot.start()
     total[...] = jnp.zeros_like(total)
 
     def forward(i, carry):
         lanes = pl.ds(pl.multiple_of(i * BLOCK, BLOCK), BLOCK)
         for copy in copies(i):
             copy.wait()
+
+        @pl.when(i + 2 < steps)
+        def _():
+            for copy in copies(i + 2):
+                copy.start()
+
         mid, slope = silu_pair(dot(act_ref[...], w_in[:, lanes]))
         slopes[:, lanes] = slope.astype(jnp.bfloat16)
         total[...] += dot(mid.astype(jnp.bfloat16), w_out[lanes, :])
@@ -398,8 +482,11 @@
     grad_out.ref[...] = later
     grad_out.send()
     low = later.astype(jnp.bfloat16)
-    conv_out.ref[...] = low
-    conv_out.send()
+    low_ref[...] = low
+    side = info[SIDE]
+    half = low.shape[1] // 2
+    conv_send.send(low_ref.at[:, pl.ds(pl.multiple_of((1 - side) * half, half), half)])
+    conv_keep.send(low_ref.at[:, pl.ds(pl.multiple_of(side * half, half), half)])
     scaled, normal = normalized()
     d_norm = dot_turned(low, point.get()[...]) * silu_pair(normal)[1] * valid
     d_norm_out.ref[...] = d_norm
@@ -408,32 +495,37 @@
     sums.ref[3:4] = jnp.sum(d_norm * scaled, axis=0, keepdims=True)
 
 
-def second_both(info, filtered, stats, state, cotangent, gain, final_gain, point_out, w_in, w_out):
+def second_both(info, filtered, stats, state, cotangent, gain, final_gain, point_out, w_in, w_out, deps):
     tokens, model = state.shape
     inner = w_in.shape[1]
     flat = (tokens, model)
     low, high = struct(*flat), struct(*flat, kind=jnp.float32)
     return flow_call(
         second_kernel, "second_both",
-        [low, low, low, low, high, low, high, struct(4, model, kind=jnp.float32)],
+        [low, low, low, low, high, struct(tokens, model // 2), struct(tokens, model // 2), high,
+         struct(4, model, kind=jnp.float32)],
         [
             pltpu.SemaphoreType.DMA((2, inner // BLOCK)),
             pltpu.VMEM(flat, jnp.float32), pltpu.VMEM(flat, jnp.float32), pltpu.VMEM(flat, jnp.float32),
-            pltpu.VMEM((tokens, inner), jnp.bfloat16),
+            pltpu.VMEM((tokens, inner), jnp.bfloat16), pltpu.VMEM(flat, jnp.bfloat16),
         ],
         info,
         (filtered, stats, state, cotangent, gain[None], final_gain[None], point_out, w_in, w_out),
         8 * tokens * model * inner + 4 * tokens * model * model,
         mib=48,
         raw=(7, 8),
-    )
-
-
-def conv_back_kernel(info, ins, outs, wide, gated_wide):
+        late=(3,),
+        deps=deps,
+    )
+
+
+def conv_back_kernel(info, ins, outs, wide, gated_wide, joined_ref):
     d_norm_ref, filtered_ref, before_ref, after_ref, stats_ref, sums_ref, taps_ref = [i.get() for i in ins[:7]]
+    for item in ins[10:13]:
+        item.start()
     gated_ref, gated_before, gated_after = [i.get() for i in ins[7:10]]
     value, gate, point, state, gain, grad = ins[10:]
-    joined_ref, out_ref, low_ref, small_ref = [item.ref for item in outs]
+    out_ref, low_ref, small_ref = [item.ref for item in outs[2:]]
     tokens, model = d_norm_ref.shape
     half = gated_before.shape[0]
 
@@ -458,18 +550,22 @@
         small_ref[1 + tap : 2 + tap] = jnp.sum(
             wide[8 : 8 + tokens] * gated_wide[begin : begin + tokens], axis=0, keepdims=True
         )
+    for item in ins[13:]:
+        item.start()
     d_gated = d_gated * rows_of(info[LENGTH], offset, tokens)
     gate = gate.get()[...].astype(jnp.float32)
     d_value = d_gated * gate
     joined_ref[:, :model] = d_value.astype(jnp.bfloat16)
     joined_ref[:, model:] = (d_value * value.get()[...].astype(jnp.float32) * (1.0 - gate)).astype(jnp.bfloat16)
-    outs[0].send()
+    side = info[SIDE]
+    outs[0].send(joined_ref.at[:, pl.ds(pl.multiple_of((1 - side) * model, model), model)])
+    outs[1].send(joined_ref.at[:, pl.ds(pl.multiple_of(side * model, model), model)])
     d_values, small_ref[0:1] = normed_back(
         dot_turned(joined_ref[...], point.get()[...]), state.get()[...], gain.get()[...]
     )
     later = grad.get()[...] + d_values
     low_ref[...] = later.astype(jnp.bfloat16)
-    outs[2].send()
+    outs[3].send()
     out_ref[...] = later
 
 
@@ -479,40 +575,50 @@
     return flow_call(
         conv_back_kernel, "conv_back",
         [
-            struct(tokens, 2 * model), struct(tokens, model, kind=jnp.float32), struct(tokens, model),
+            struct(tokens, model), struct(tokens, model),
+            struct(tokens, model, kind=jnp.float32), struct(tokens, model),
             struct(1 + depth.shape[0], model, kind=jnp.float32),
         ],
-        [pltpu.VMEM((tokens + 16, model), jnp.float32)] * 2,
+        [pltpu.VMEM((tokens + 16, model), jnp.float32)] * 2 + [pltpu.VMEM((tokens, 2 * model), jnp.bfloat16)],
         info,
         (d_norm, filtered, before, later, stats, sums, depth, gated, gated_before, gated_after, value,
          gate, point_in, state, gain[None], grad),
         4 * tokens * model * model,
         mib=32,
-    )
-
-
-def mixed_back_kernel(info, ins, outs, sem):
-    own, near, (source, held) = ins
-    half = source.shape[0] // 2
-    side = info[SIDE]
-    copy = pltpu.make_async_copy(source.at[pl.ds(pl.multiple_of(side * half, half), half), :], held.at[:half], sem.at[0])
-    copy.start()
-    own_ref, near_ref, out_ref = own.get(), near.get(), outs[0].ref
-    tokens = own_ref.shape[0]
-    copy.wait()
-    part = held[:half]
-    mine = pl.ds(pl.multiple_of(side * tokens, tokens), tokens)
-    other = pl.ds(pl.multiple_of((1 - side) * tokens, tokens), tokens)
-    out_ref[mine] = dot_turned(own_ref[...], part).astype(jnp.bfloat16)
-    out_ref[other] = dot_turned(near_ref[...], part).astype(jnp.bfloat16)
-
-
-def mixed_back(info, own, near, weight):
-    tokens, model = own.shape
+        late=tuple(range(10, 16)),
+    )
+
+
+def add_kernel(info, ins, outs):
+    total = ins[0].get()[...].astype(jnp.float32)
+    for item in ins[1:]:
+        total = total + item.get()[...].astype(jnp.float32)
+    outs[0].ref[...] = total.astype(outs[0].ref.dtype)
+
+
+def add(info, terms, kind, *deps):
     return flow_call(
-        mixed_back_kernel, "mixed_back", [struct(2 * tokens, model // 2)], [pltpu.SemaphoreType.DMA((1,))],
-        info, (own, near, weight), 2 * tokens * model * model, raw=(2,),
+        add_kernel, "add", [struct(*terms[0].shape, kind=kind)], [], info, tuple(terms), 0, deps=deps
     )[0]
+
+
+def branch_kernel(info, ins, outs):
+    keep, got, far, state, gain, grad = ins
+    d_input = keep.get()[...] + got.get()[...].astype(jnp.float32) + far.get()[...].astype(jnp.float32)
+    d_values, outs[2].ref[...] = normed_back(d_input, state.get()[...], gain.get()[...])
+    later = grad.get()[...] + d_values
+    outs[1].ref[...] = (0.5 * later).astype(jnp.bfloat16)
+    outs[1].send()
+    outs[0].ref[...] = later
+
+
+def branch_of(info, keep, got, far, state, gain, grad, deps):
+    tokens, model = keep.shape
+    return flow_call(
+        branch_kernel, "branch",
+        [struct(tokens, model, kind=jnp.float32), struct(tokens, model), struct(1, model, kind=jnp.float32)],
+        [], info, (keep, got, far, state, gain[None], grad), 0, deps=deps,
+    )
 
 
 def input_back_kernel(count, base, info, ins, outs, sem):
@@ -545,7 +651,7 @@
     keep_ref[...] = total(side)
 
 
-def input_back(info, grads, base, weights, tokens):
+def input_back(info, grads, base, weights, tokens, deps=()):
     model = weights[0].shape[0]
     count = len(grads)
     return flow_call(
@@ -553,12 +659,11 @@
         [struct(tokens, model), struct(tokens, model, kind=jnp.float32)],
         [pltpu.SemaphoreType.DMA((count,))],
         info, (*grads, *weights), 2 * tokens * model * model * count,
-        mib=32, raw=tuple(range(count, 2 * count)),
-    )
-
-
-def cross_kernel(layout, info, refs, outs, left_rows, right_rows):
-    send_ref, keep_ref = outs[0].ref, outs[1].ref
+        mib=32, raw=tuple(range(count, 2 * count)), deps=deps,
+    )
+
+
+def cross_kernel(layout, split, lead, chunk, info, refs, outs, left_rows, right_rows, *held):
     far, side = info[FAR], info[SIDE]
     at = 0
     begin = 0
@@ -570,40 +675,50 @@
             spot = (k // 2 * 2 + (side if k % 2 == 0 else 1 - side)) * tokens
             left_rows[pl.ds(pl.multiple_of(spot, tokens), tokens)] = left.get()[...]
         size = abs(width)
-        half = size // 2
+        half = size // 2 if split else size
         if len(right) == 2:
             for k, piece in enumerate(right):
                 spot = (side if k == 0 else 1 - side) * tokens
-                right_rows[pl.ds(pl.multiple_of(spot, tokens), tokens), :size] = piece.get()[...]
+                held = piece.get()
+                lanes = pl.ds(0, size)
+                if held.shape[1] != size:
+                    lanes = pl.ds(pl.multiple_of(side * size, size), size)
+                right_rows[pl.ds(pl.multiple_of(spot, tokens), tokens), :size] = held[:, lanes]
             source = right_rows
         else:
             source = right[0].get()
         count = pieces * tokens
-        for which, target in ((1 - far, send_ref), (far, keep_ref)):
+        targets = ((1 - far, outs[0].ref), (far, outs[1].ref)) if split else ((0, held[0]),)
+        for which, target in targets:
             lanes = pl.ds(pl.multiple_of(which * half, half), half)
             target[:, begin : begin + half] = lax.dot_general(
                 left_rows[:count], source[:count, lanes], (((0,), (0,)), ((), ())),
                 preferred_element_type=jnp.float32,
             ).astype(jnp.bfloat16)
         begin += half
-
-
-def cross_grads(info, terms):
+    if not split:
+        store_halves(held[0], info[ROW] & 1, lead, chunk, outs[0].ref, outs[1].ref)
+
+
+def cross_grads(info, terms, split=True, deps=()):
     operands, layout = [], []
     total = flops = 0
-    for lefts, rights in terms:
+    for lefts, rights, width in terms:
         operands += [*lefts, *rights]
-        width = rights[0].shape[1]
         layout.append((len(lefts), -width if len(rights) == 2 else width))
-        total += width // 2
+        total += width // 2 if split else width
         tokens, model = lefts[0].shape
         flops += 2 * len(lefts) * tokens * model * width
-    deepest = max(len(lefts) for lefts, _ in terms) * tokens
-    widest = max(rights[0].shape[1] for _, rights in terms)
+    deepest = max(len(lefts) for lefts, *_ in terms) * tokens
+    widest = max(width for *_, width in terms)
+    size = model >> row_bits()
+    rows = model if split else model // 2
+    scratch = [pltpu.VMEM((deepest, model), jnp.bfloat16), pltpu.VMEM((deepest, widest), jnp.bfloat16)]
+    if not split:
+        scratch.append(pltpu.VMEM((model, total), jnp.bfloat16))
     return flow_call(
-        functools.partial(cross_kernel, layout), "cross_grads", [struct(model, total)] * 2,
-        [pltpu.VMEM((deepest, model), jnp.bfloat16), pltpu.VMEM((deepest, widest), jnp.bfloat16)],
-        info, tuple(operands), flops, mib=40,
+        functools.partial(cross_kernel, layout, split, model // size // 2, size), "cross_grads",
+        [struct(rows, total)] * 2, scratch, info, tuple(operands), flops, mib=40, deps=deps,
     )
 
 
@@ -612,18 +727,25 @@
     w_in, w_out = pair_in[1], pair_out[1]
     steps = w_in.shape[1] // BLOCK
     copies = weight_copies(pair_in, pair_out, sem, BLOCK)
-    for i in range(steps):
+    for i in range(2):
         for copy in copies(i):
             copy.start()
     grad_ref = grad.get()
     branch[...] = (0.5 * grad_ref[...]).astype(jnp.bfloat16)
     total[...] = jnp.zeros_like(total)
     slope_ref = slope.get()
+    x.start()
 
     def backward(i, carry):
         lanes = pl.ds(pl.multiple_of(i * BLOCK, BLOCK), BLOCK)
         for copy in copies(i):
             copy.wait()
+
+        @pl.when(i + 2 < steps)
+        def _():
+            for copy in copies(i + 2):
+                copy.start()
+
         part = dot_turned(branch[...], w_out[lanes, :])
         part = (part * slope_ref[:, lanes].astype(jnp.float32)).astype(jnp.bfloat16)
         total[...] += dot_turned(part, w_in[:, lanes])
@@ -634,7 +756,7 @@
     outs[0].ref[...] = (grad_ref[...] + d_values).astype(jnp.bfloat16)
 
 
-def first_backward(info, grad, features, gain, slope, w_in, w_out):
+def first_backward(info, grad, features, gain, slope, w_in, w_out, deps):
     tokens, model = features.shape
     inner = w_in.shape[1]
     return flow_call(
@@ -642,7 +764,7 @@
         [struct(tokens, model), struct(1, model, kind=jnp.float32)],
         [pltpu.SemaphoreType.DMA((2, inner // BLOCK)), pltpu.VMEM((tokens, model), jnp.bfloat16), pltpu.VMEM((tokens, model), jnp.float32)],
         info, (grad, features, gain[None], slope, w_in, w_out), 4 * tokens * model * inner,
-        mib=40, raw=(4, 5),
+        mib=40, raw=(4, 5), late=(1,), deps=deps,
     )
 
 
@@ -697,10 +819,10 @@
             whole((tokens, model)),
         ],
         out_shape=[
-            jax.ShapeDtypeStruct((tokens, model), jnp.float32),
-            jax.ShapeDtypeStruct((tokens, model), jnp.bfloat16),
-            jax.ShapeDtypeStruct((tokens, inner), jnp.bfloat16),
-            jax.ShapeDtypeStruct((tokens, model), jnp.bfloat16),
+            pltpu.HBM((tokens, model), jnp.float32),
+            pltpu.HBM((tokens, model), jnp.bfloat16),
+            pltpu.HBM((tokens, inner), jnp.bfloat16),
+            pltpu.HBM((tokens, model), jnp.bfloat16),
         ],
         scratch_shapes=[pltpu.VMEM((tokens, model), jnp.float32)],
         compiler_params=pltpu.CompilerParams(vmem_limit_bytes=40 * MIB),
@@ -710,7 +832,7 @@
             4 * model * inner + 2 * tokens * inner,
         ),
         name="first_forward",
-    )(features, gain[None], next_gain[None], w_in, w_out)
+    )(in_hbm(features), gain[None], next_gain[None], in_hbm(w_in), in_hbm(w_out))
 
 
 def take_kernel(place, source, target):
@@ -742,8 +864,7 @@
     return lax.dynamic_index_in_dim(cut, place, 1, keepdims=False).reshape(-1, model)
 
 
-def lay_kernel(widths, groups, places, *refs):
-    parts = 4
+def lay_kernel(parts, widths, groups, places, *refs):
     pieces, targets = refs[:parts], refs[parts:]
     for k in range(parts):
         begin = 0
@@ -770,7 +891,7 @@
             begin += width
         return outs
     return pl.pallas_call(
-        functools.partial(lay_kernel, widths, groups),
+        functools.partial(lay_kernel, parts, widths, groups),
         out_shape=[jax.ShapeDtypeStruct((rows, parts * width), jnp.float32) for width in widths],
         grid_spec=pltpu.PrefetchScalarGridSpec(
             num_scalar_prefetch=1,
@@ -796,7 +917,7 @@
     width = length - LANES
     return pl.pallas_call(
         skew_kernel,
-        out_shape=jax.ShapeDtypeStruct((heads, LANES, width), jnp.float32),
+        out_shape=pltpu.HBM((heads, LANES, width), jnp.float32),
         grid=(heads,),
         in_specs=[pl.BlockSpec((1, 1, length), lambda h: (h, 0, 0))],
         out_specs=pl.BlockSpec((1, LANES, width), lambda h: (h, 0, 0)),
@@ -805,7 +926,8 @@
 
 
 def attend_kernel(
-    scale, at, q_ref, k_pair, k_far, v_pair, v_far, bias_ref, out_ref, lse_ref, k_ref, vt_ref, s_ref, p_ref
+    scale, at, q_ref, k_pair, k_far, v_pair, v_far, bias_ref, own_ref, other_ref, lse_ref,
+    k_ref, vt_ref, s_ref, p_ref, out_ref,
 ):
     tile = q_ref.shape[0]
     blocks = k_ref.shape[0] // LANES
@@ -838,12 +960,16 @@
         p_ref[b * LANES : (b + 1) * LANES] = p.astype(jnp.bfloat16)
     mixed = jnp.dot(vt_ref[...], p_ref[...], preferred_element_type=jnp.float32) / total
     out_ref[...] = mixed.T.astype(jnp.bfloat16)
+    half = tile // 2
+    side = at[blocks * 2 + 1]
+    own_ref[...] = out_ref[pl.ds(pl.multiple_of(side * half, half), half)]
+    other_ref[...] = out_ref[pl.ds(pl.multiple_of((1 - side) * half, half), half)]
     lse_ref[0] = top + jnp.log(total)
 
 
 def attend(at, query, key, key_far, value, value_far, bias, heads, head_dim):
     queries, keys = query.shape[0], 2 * key.shape[0]
-    tile = QUERY_TILE
+    tile = queries
     width = bias.shape[-1]
     grid_spec = pltpu.PrefetchScalarGridSpec(
         num_scalar_prefetch=1,
@@ -857,7 +983,8 @@
             pl.BlockSpec((1, LANES, width), lambda h, i, at: (h, 0, 0)),
         ],
         out_specs=[
-            pl.BlockSpec((tile, head_dim), lambda h, i, at: (i, h)),
+            pl.BlockSpec((tile // 2, head_dim), lambda h, i, at: (0, h)),
+            pl.BlockSpec((tile // 2, head_dim), lambda h, i, at: (0, h)),
             pl.BlockSpec((1, 1, tile), lambda h, i, at: (h, 0, i)),
         ],
         scratch_shapes=[
@@ -865,13 +992,15 @@
             pltpu.VMEM((head_dim, keys), jnp.bfloat16),
             pltpu.VMEM((keys, tile), jnp.float32),
             pltpu.VMEM((keys, tile), jnp.bfloat16),
+            pltpu.VMEM((tile, head_dim), jnp.bfloat16),
         ],
     )
     return pl.pallas_call(
         functools.partial(attend_kernel, head_dim ** (-0.5)),
         out_shape=[
-            jax.ShapeDtypeStruct((queries, heads * head_dim), jnp.bfloat16),
-            jax.ShapeDtypeStruct((heads, 1, queries), jnp.float32),
+            pltpu.HBM((queries // 2, heads * head_dim), jnp.bfloat16),
+            pltpu.HBM((queries // 2, heads * head_dim), jnp.bfloat16),
+            pltpu.HBM((heads, 1, queries), jnp.float32),
         ],
         grid_spec=grid_spec,
         compiler_params=pltpu.CompilerParams(vmem_limit_bytes=24 * MIB),
@@ -881,31 +1010,31 @@
             4 * heads * LANES * width + 4 * heads * head_dim * (queries + keys),
         ),
         name="attend",
-    )(at, query, key, key_far, value, value_far, bias)
+    )(at, query, key, key_far, value, value_far, in_hbm(bias))
 
 
 def attend_back_kernel(
-    scale, at, q_ref, k_pair, k_far, v_pair, v_far, do_ref, lse_ref, bias_ref,
-    dq_ref, dk_ref, dv_ref, line_ref,
-    k_ref, v_ref, kt_ref, s_ref, dp_ref, p_ref, ds_ref, dk_sum, dv_sum, skew_ref,
+    scale, at, q_ref, k_pair, k_far, v_pair, v_far, da_own, da_near, wo_ref, wk_ref, wv_ref, lse_ref, bias_ref,
+    dq_ref, dk_ref, dv_ref, line_ref, send_ref, far_ref,
+    do_ref, all_dk, all_dv, k_ref, v_ref, kt_ref, s_ref, dp_ref, p_ref, ds_ref, skew_ref,
 ):
     tile = q_ref.shape[0]
     blocks = k_ref.shape[0] // LANES
     length = at[blocks * 2]
     pair = k_pair.shape[0]
 
-    @pl.when(pl.program_id(1) == 0)
-    def _():
-        k_ref[:pair] = k_pair[...]
-        k_ref[pair:] = k_far[...]
-        v_ref[:pair] = v_pair[...]
-        v_ref[pair:] = v_far[...]
-        kt_ref[...] = k_ref[...].T
-        dk_sum[...] = jnp.zeros_like(dk_sum)
-        dv_sum[...] = jnp.zeros_like(dv_sum)
-        skew_ref[...] = jnp.zeros_like(skew_ref)
-
-    begin = pl.program_id(1) * tile
+    side = at[blocks * 2 + 1]
+    own = da_own.shape[0]
+    mine = pl.ds(pl.multiple_of(side * own, own), own)
+    other = pl.ds(pl.multiple_of((1 - side) * own, own), own)
+    do_ref[mine] = dot_turned(da_own[...], wo_ref[...]).astype(jnp.bfloat16)
+    do_ref[other] = dot_turned(da_near[...], wo_ref[...]).astype(jnp.bfloat16)
+    k_ref[:pair] = k_pair[...]
+    k_ref[pair:] = k_far[...]
+    v_ref[:pair] = v_pair[...]
+    v_ref[pair:] = v_far[...]
+    kt_ref[...] = k_ref[...].T
+    skew_ref[...] = jnp.zeros_like(skew_ref)
     s_ref[...] = lax.dot_general(
         k_ref[...], q_ref[...], (((1,), (1,)), ((), ())), preferred_element_type=jnp.float32
     )
@@ -917,7 +1046,7 @@
     delta = jnp.zeros((1, tile), jnp.float32)
     for b in range(blocks):
         rows = slice(b * LANES, (b + 1) * LANES)
-        lanes = pl.ds(pl.multiple_of(at[b] + begin, LANES), tile)
+        lanes = pl.ds(pl.multiple_of(at[b], LANES), tile)
         s = s_ref[rows] * scale + bias_ref[0, :, lanes]
         s = jnp.where(frame < length - at[blocks + b], s, NEGATIVE)
         p = jnp.exp(s - lse)
@@ -926,85 +1055,108 @@
         delta = delta + jnp.sum(p * dp_ref[rows], axis=0, keepdims=True)
     for b in range(blocks):
         rows = slice(b * LANES, (b + 1) * LANES)
-        lanes = pl.ds(pl.multiple_of(at[b] + begin, LANES), tile)
+        lanes = pl.ds(pl.multiple_of(at[b], LANES), tile)
         ds = (s_ref[rows] * (dp_ref[rows] - delta)).astype(jnp.bfloat16)
         ds_ref[rows] = ds
         skew_ref[:, lanes] += ds.astype(jnp.float32)
-    dv_sum[...] += jnp.dot(p_ref[...], do_ref[...], preferred_element_type=jnp.float32)
-    dk_sum[...] += jnp.dot(ds_ref[...], q_ref[...], preferred_element_type=jnp.float32)
+    dv = jnp.dot(p_ref[...], do_ref[...], preferred_element_type=jnp.float32).astype(jnp.bfloat16)
+    dk = jnp.dot(ds_ref[...], q_ref[...], preferred_element_type=jnp.float32) * scale
+    dk = dk.astype(jnp.bfloat16)
     dq = jnp.dot(kt_ref[...], ds_ref[...], preferred_element_type=jnp.float32) * scale
     dq_ref[...] = dq.T.astype(jnp.bfloat16)
-
-    @pl.when(pl.program_id(1) == pl.num_programs(1) - 1)
+    dk_ref[...] = dk
+    dv_ref[...] = dv
+    head = pl.program_id(0)
+    all_dk[head] = dk[pair:]
+    all_dv[head] = dv[pair:]
+    lines = jnp.concatenate([skew_ref[...], jnp.zeros((LANES, LANES), jnp.float32)], axis=1)
+    count = LANES // 2
+    while count >= 8:
+        lines = lines[count:] + pltpu.roll(lines[:count], count, 1)
+        count //= 2
+    line_ref[0] = lines
+
+    @pl.when(head == pl.num_programs(0) - 1)
     def _():
-        dk_ref[...] = (dk_sum[...] * scale).astype(jnp.bfloat16)
-        dv_ref[...] = dv_sum[...].astype(jnp.bfloat16)
-        lines = jnp.concatenate([skew_ref[...], jnp.zeros((LANES, LANES), jnp.float32)], axis=1)
-        count = LANES // 2
-        while count >= 8:
-            lines = lines[count:] + pltpu.roll(lines[:count], count, 1)
-            count //= 2
-        line_ref[0] = lines
-
-
-def attend_back(at, query, key, key_far, value, value_far, grad, lse, bias, heads, head_dim):
+        def total(rows):
+            heads = all_dk.shape[0]
+            d_key = jnp.concatenate([all_dk[h, rows] for h in range(heads)], axis=1)
+            d_value = jnp.concatenate([all_dv[h, rows] for h in range(heads)], axis=1)
+            return dot_turned(d_key, wk_ref[...]) + dot_turned(d_value, wv_ref[...])
+
+        send_ref[...] = total(other).astype(jnp.bfloat16)
+        far_ref[...] = total(mine)
+
+
+def attend_back(at, query, key, key_far, value, value_far, own, near, weights, lse, bias, heads, head_dim):
     queries, keys = query.shape[0], 2 * key.shape[0]
-    tile = QUERY_TILE
+    tokens, model = own.shape
     width = bias.shape[-1]
+    blocks = keys // LANES
+    column = lambda h, at: (0, h)
+    half = pl.BlockSpec((keys // 2, head_dim), column)
+    low = jnp.bfloat16
+    wo, wk, wv = weights
     grid_spec = pltpu.PrefetchScalarGridSpec(
         num_scalar_prefetch=1,
-        grid=(heads, queries // tile),
+        grid=(heads,),
         in_specs=[
-            pl.BlockSpec((tile, head_dim), lambda h, i, at: (i, h)),
-            pl.BlockSpec((keys // 2, head_dim), lambda h, i, at: (0, h)),
-            pl.BlockSpec((keys // 2, head_dim), lambda h, i, at: (0, h)),
-            pl.BlockSpec((keys // 2, head_dim), lambda h, i, at: (0, h)),
-            pl.BlockSpec((keys // 2, head_dim), lambda h, i, at: (0, h)),
-            pl.BlockSpec((tile, head_dim), lambda h, i, at: (i, h)),
-            pl.BlockSpec((1, 1, tile), lambda h, i, at: (h, 0, i)),
-            pl.BlockSpec((1, LANES, width), lambda h, i, at: (h, 0, 0)),
+            pl.BlockSpec((queries, head_dim), column), half, half, half, half,
+            whole((tokens, model)), whole((tokens, model)),
+            pl.BlockSpec((head_dim, model), lambda h, at: (at[2 * blocks + 1] * heads + h, 0)),
+            pl.BlockSpec((model, model // 2), lambda h, at: (0, at[2 * blocks + 1])),
+            pl.BlockSpec((model, model // 2), lambda h, at: (0, at[2 * blocks + 1])),
+            pl.BlockSpec((1, 1, queries), lambda h, at: (h, 0, 0)),
+            pl.BlockSpec((1, LANES, width), lambda h, at: (h, 0, 0)),
         ],
         out_specs=[
-            pl.BlockSpec((tile, head_dim), lambda h, i, at: (i, h)),
-            pl.BlockSpec((keys, head_dim), lambda h, i, at: (0, h)),
-            pl.BlockSpec((keys, head_dim), lambda h, i, at: (0, h)),
-            pl.BlockSpec((1, 8, width + LANES), lambda h, i, at: (h, 0, 0)),
+            pl.BlockSpec((queries, head_dim), column),
+            pl.BlockSpec((keys, head_dim), column),
+            pl.BlockSpec((keys, head_dim), column),
+            pl.BlockSpec((1, 8, width + LANES), lambda h, at: (h, 0, 0)),
+            whole((tokens, model)),
+            whole((tokens, model)),
         ],
         scratch_shapes=[
-            pltpu.VMEM((keys, head_dim), jnp.bfloat16),
-            pltpu.VMEM((keys, head_dim), jnp.bfloat16),
-            pltpu.VMEM((head_dim, keys), jnp.bfloat16),
-            pltpu.VMEM((keys, tile), jnp.float32),
-            pltpu.VMEM((keys, tile), jnp.float32),
-            pltpu.VMEM((keys, tile), jnp.bfloat16),
-            pltpu.VMEM((keys, tile), jnp.bfloat16),
-            pltpu.VMEM((keys, head_dim), jnp.float32),
-            pltpu.VMEM((keys, head_dim), jnp.float32),
+            pltpu.VMEM((queries, head_dim), low),
+            pltpu.VMEM((heads, keys // 2, head_dim), low),
+            pltpu.VMEM((heads, keys // 2, head_dim), low),
+            pltpu.VMEM((keys, head_dim), low),
+            pltpu.VMEM((keys, head_dim), low),
+            pltpu.VMEM((head_dim, keys), low),
+            pltpu.VMEM((keys, queries), jnp.float32),
+            pltpu.VMEM((keys, queries), jnp.float32),
+            pltpu.VMEM((keys, queries), low),
+            pltpu.VMEM((keys, queries), low),
             pltpu.VMEM((LANES, width), jnp.float32),
         ],
     )
     return pl.pallas_call(
         functools.partial(attend_back_kernel, head_dim ** (-0.5)),
         out_shape=[
-            jax.ShapeDtypeStruct((queries, heads * head_dim), jnp.bfloat16),
-            jax.ShapeDtypeStruct((keys, heads * head_dim), jnp.bfloat16),
-            jax.ShapeDtypeStruct((keys, heads * head_dim), jnp.bfloat16),
-            jax.ShapeDtypeStruct((heads, 8, width + LANES), jnp.float32),
+            pltpu.HBM((queries, heads * head_dim), low),
+            pltpu.HBM((keys, heads * head_dim), low),
+            pltpu.HBM((keys, heads * head_dim), low),
+            pltpu.HBM((heads, 8, width + LANES), jnp.float32),
+            pltpu.HBM((tokens, model), low),
+            pltpu.HBM((tokens, model), jnp.float32),
         ],
         grid_spec=grid_spec,
-        compiler_params=pltpu.CompilerParams(vmem_limit_bytes=24 * MIB),
+        compiler_params=pltpu.CompilerParams(vmem_limit_bytes=48 * MIB),
         cost_estimate=cost(
             10 * heads * queries * keys * head_dim,
             heads * queries * keys,
             4 * heads * LANES * width + 8 * heads * head_dim * (queries + keys),
         ),
         name="attend_back",
-    )(at, query, key, key_far, value, value_far, grad, lse, bias)
+    )(
+        at, *[in_hbm(x) for x in (query, key, key_far, value, value_far, own, near, wo, wk, wv, lse, bias)]
+    )
 
 
 def again_kernel(count, at, *refs):
     pieces, cuts = refs[:4], refs[4 : 4 + count]
-    act_ref, slope_ref, rows = refs[4 + count :]
+    act_ref, slope_ref, rows = refs[5 + count :]
     tokens = pieces[0].shape[0]
 
     @pl.when(pl.program_id(0) == 0)
@@ -1026,14 +1178,14 @@
     return None, lambda g, at: (0, g)
 
 
-def again(place, pieces, weight, groups):
+def again(place, pieces, weight, groups, dep):
     parts = len(pieces)
     tokens, model = pieces[0].shape
     inner = weight.shape[1] // parts
     width = LANES
     source, where = column_cuts(weight, groups, parts, width)
     if source is None:
-        source = take_columns(weight, groups, place, parts)
+        source = take_columns(weight, groups, place[0], parts)
     count = 2
     cut = inner // width // count
     return pl.pallas_call(
@@ -1045,11 +1197,12 @@
             + [
                 pl.BlockSpec((model, width), lambda i, at, k=k: where(i * count + k, at))
                 for k in range(count)
-            ],
+            ]
+            + [pl.BlockSpec(memory_space=pl.ANY)],
             out_specs=[pl.BlockSpec((count * width, parts * tokens), lambda i, at: (i, 0))] * 2,
             scratch_shapes=[pltpu.VMEM((parts * tokens, model), jnp.bfloat16)],
         ),
-        out_shape=[jax.ShapeDtypeStruct((inner, parts * tokens), jnp.bfloat16)] * 2,
+        out_shape=[pltpu.HBM((inner, parts * tokens), jnp.bfloat16)] * 2,
         compiler_params=pltpu.CompilerParams(vmem_limit_bytes=40 * MIB),
         cost_estimate=cost(
             2 * parts * tokens * model * inner,
@@ -1057,11 +1210,17 @@
             2 * parts * tokens * (2 * inner + model) + 2 * model * inner,
         ),
         name="again",
-    )(place.reshape(1), *pieces, *([source] * count))
-
-
-def grad_out_kernel(act_ref, *refs):
-    pieces, out_ref, rows = refs[:4], refs[4], refs[5]
+    )(place[:1], *[in_hbm(p) for p in pieces], *([in_hbm(source)] * count), in_hbm(dep))
+
+
+def store_halves(held, mine, lead, size, send_ref, keep_ref):
+    for index, target in ((1 - mine, send_ref), (mine, keep_ref)):
+        for k, part in enumerate(take_half(held, index, lead, size)):
+            target[k * size : (k + 1) * size] = part
+
+
+def grad_out_kernel(share, at, act_ref, *refs):
+    pieces, dep, send_ref, keep_ref, rows, held = refs[:4], *refs[4:]
     tokens = pieces[0].shape[0]
 
     @pl.when(pl.program_id(0) == 0)
@@ -1069,34 +1228,39 @@
         for k in range(4):
             rows[k * tokens : (k + 1) * tokens] = pieces[k][...]
 
-    out_ref[...] = dot(act_ref[...], rows[...]).astype(jnp.bfloat16)
-
-
-def grad_out_of(act, pieces):
+    held[...] = dot(act_ref[...], rows[...]).astype(jnp.bfloat16)
+    store_halves(held, at[1] & 1, held.shape[0] // share // 2, share, send_ref, keep_ref)
+
+
+def grad_out_of(place, act, pieces, share, dep):
     inner, frames = act.shape
     tokens, model = pieces[0].shape
-    step = 256
+    step = 512
     return pl.pallas_call(
-        grad_out_kernel,
-        grid=(inner // step,),
-        in_specs=[pl.BlockSpec((step, frames), lambda i: (i, 0))]
-        + [whole((tokens, model))] * len(pieces),
-        out_specs=pl.BlockSpec((step, model), lambda i: (i, 0)),
-        out_shape=jax.ShapeDtypeStruct((inner, model), jnp.bfloat16),
-        scratch_shapes=[pltpu.VMEM((frames, model), jnp.bfloat16)],
+        functools.partial(grad_out_kernel, share),
+        grid_spec=pltpu.PrefetchScalarGridSpec(
+            num_scalar_prefetch=1,
+            grid=(inner // step,),
+            in_specs=[pl.BlockSpec((step, frames), lambda i, at: (i, 0))]
+            + [whole((tokens, model))] * len(pieces)
+            + [pl.BlockSpec(memory_space=pl.ANY)],
+            out_specs=[pl.BlockSpec((step // 2, model), lambda i, at: (i, 0))] * 2,
+            scratch_shapes=[
+                pltpu.VMEM((frames, model), jnp.bfloat16), pltpu.VMEM((step, model), jnp.bfloat16)
+            ],
+        ),
+        out_shape=[pltpu.HBM((inner // 2, model), jnp.bfloat16)] * 2,
         compiler_params=pltpu.CompilerParams(vmem_limit_bytes=40 * MIB),
         cost_estimate=cost(
-            2 * frames * model * inner,
-            0,
-            2 * frames * (inner + model) + 2 * model * inner,
+            2 * frames * model * inner, 0, 2 * frames * (inner + model) + 2 * model * inner
         ),
         name="grad_out",
-    )(act, *pieces)
-
-
-def grad_in_kernel(count, at, slope_ref, *refs):
+    )(place, in_hbm(act), *[in_hbm(p) for p in pieces], in_hbm(dep))
+
+
+def grad_in_kernel(count, share, at, slope_ref, *refs):
     acts, branches, cuts = refs[:4], refs[4:8], refs[8 : 8 + count]
-    out_ref, act_rows, branch_rows = refs[8 + count :]
+    dep, send_ref, keep_ref, act_rows, branch_rows, held = refs[8 + count :]
     tokens = acts[0].shape[0]
 
     @pl.when(pl.program_id(0) == 0)
@@ -1107,21 +1271,22 @@
 
     cut = jnp.concatenate([c[...] for c in cuts], axis=0)
     d_hidden = (dot_turned(cut, branch_rows[...]) * slope_ref[...].astype(jnp.float32)).astype(jnp.bfloat16)
-    out_ref[...] = dot(d_hidden, act_rows[...]).T.astype(jnp.bfloat16)
-
-
-def grad_in_of(place, slope, acts, branches, weight, groups):
+    held[...] = dot(d_hidden, act_rows[...]).astype(jnp.bfloat16).T
+    store_halves(held, at[1] & 1, held.shape[0] // share // 2, share, send_ref, keep_ref)
+
+
+def grad_in_of(place, slope, acts, branches, weight, groups, share, dep):
     inner, frames = slope.shape
     tokens, model = acts[0].shape
     parts = len(acts)
     width = LANES
-    count = 2
+    count = 4
     if weight.shape[0] // groups // parts == width:
         source, where = weight, lambda g, at: (g * parts + at[0], 0)
     else:
-        source, where = take_rows(weight, groups, place, parts), lambda g, at: (g, 0)
+        source, where = take_rows(weight, groups, place[0], parts), lambda g, at: (g, 0)
     return pl.pallas_call(
-        functools.partial(grad_in_kernel, count),
+        functools.partial(grad_in_kernel, count, share),
         grid_spec=pltpu.PrefetchScalarGridSpec(
             num_scalar_prefetch=1,
             grid=(inner // width // count,),
@@ -1130,19 +1295,76 @@
             + [
                 pl.BlockSpec((width, model), lambda i, at, k=k: where(i * count + k, at))
                 for k in range(count)
-            ],
-            out_specs=pl.BlockSpec((model, count * width), lambda i, at: (0, i)),
-            scratch_shapes=[pltpu.VMEM((frames, model), jnp.bfloat16)] * 2,
+            ]
+            + [pl.BlockSpec(memory_space=pl.ANY)],
+            out_specs=[pl.BlockSpec((model // 2, count * width), lambda i, at: (0, i))] * 2,
+            scratch_shapes=[pltpu.VMEM((frames, model), jnp.bfloat16)] * 2
+            + [pltpu.VMEM((model, count * width), jnp.bfloat16)],
         ),
-        out_shape=jax.ShapeDtypeStruct((model, inner), jnp.bfloat16),
-        compiler_params=pltpu.CompilerParams(vmem_limit_bytes=40 * MIB),
+        out_shape=[pltpu.HBM((model // 2, inner), jnp.bfloat16)] * 2,
+        compiler_params=pltpu.CompilerParams(vmem_limit_bytes=48 * MIB),
         cost_estimate=cost(
-            4 * frames * model * inner,
-            0,
-            2 * frames * (inner + 2 * model) + 4 * model * inner,
+            4 * frames * model * inner, 0, 2 * frames * (inner + 2 * model) + 4 * model * inner
         ),
         name="grad_in",
-    )(place.reshape(1), slope, *acts, *branches, *([source] * count))
+    )(place, in_hbm(slope), *[in_hbm(p) for p in (*acts, *branches)], *([in_hbm(source)] * count), in_hbm(dep))
+
+
+def both_kernel(count, share, in_share, at, *refs):
+    acts, branches = refs[:4], refs[4:8]
+    ins, outs = refs[8 : 8 + count], refs[8 + count : 8 + 2 * count]
+    dep, out_send, out_keep, in_send, in_keep, act_rows, branch_rows, out_held, in_held = refs[8 + 2 * count :]
+    tokens = acts[0].shape[0]
+
+    @pl.when(pl.program_id(0) == 0)
+    def _():
+        for k in range(4):
+            act_rows[k * tokens : (k + 1) * tokens] = acts[k][...]
+            branch_rows[k * tokens : (k + 1) * tokens] = branches[k][...]
+
+    w_in = jnp.concatenate([c[...] for c in ins], axis=1).T
+    w_out = jnp.concatenate([c[...] for c in outs], axis=0)
+    mid, slope = silu_pair(dot_turned(w_in, act_rows[...]))
+    d_hidden = (dot_turned(w_out, branch_rows[...]) * slope).astype(jnp.bfloat16)
+    out_held[...] = dot(mid.astype(jnp.bfloat16), branch_rows[...]).astype(jnp.bfloat16)
+    in_held[...] = dot(d_hidden, act_rows[...]).astype(jnp.bfloat16).T
+    store_halves(out_held, at[1] & 1, out_held.shape[0] // share // 2, share, out_send, out_keep)
+    store_halves(in_held, at[1] & 1, in_held.shape[0] // in_share // 2, in_share, in_send, in_keep)
+
+
+def grads_of_both(place, acts, branches, w_in, w_out, groups, dep):
+    tokens, model = acts[0].shape
+    parts = len(acts)
+    frames = parts * tokens
+    inner = w_in.shape[1] // parts
+    width, count = LANES, 4
+    if w_in.shape[1] // groups // parts == width:
+        source_in, at_in = w_in, lambda g, at: (0, g * parts + at[0])
+        source_out, at_out = w_out, lambda g, at: (g * parts + at[0], 0)
+    else:
+        source_in, at_in = take_columns(w_in, groups, place[0], parts), lambda g, at: (0, g)
+        source_out, at_out = take_rows(w_out, groups, place[0], parts), lambda g, at: (g, 0)
+    step = count * width
+    return pl.pallas_call(
+        functools.partial(both_kernel, count, inner // groups, model // groups),
+        grid_spec=pltpu.PrefetchScalarGridSpec(
+            num_scalar_prefetch=1,
+            grid=(inner // step,),
+            in_specs=[whole((tokens, model))] * (2 * parts)
+            + [pl.BlockSpec((model, width), lambda i, at, k=k: at_in(i * count + k, at)) for k in range(count)]
+            + [pl.BlockSpec((width, model), lambda i, at, k=k: at_out(i * count + k, at)) for k in range(count)]
+            + [pl.BlockSpec(memory_space=pl.ANY)],
+            out_specs=[pl.BlockSpec((step // 2, model), lambda i, at: (i, 0))] * 2
+            + [pl.BlockSpec((model // 2, step), lambda i, at: (0, i))] * 2,
+            scratch_shapes=[pltpu.VMEM((frames, model), jnp.bfloat16)] * 2
+            + [pltpu.VMEM((step, model), jnp.bfloat16), pltpu.VMEM((model, step), jnp.bfloat16)],
+        ),
+        out_shape=[pltpu.HBM((inner // 2, model), jnp.bfloat16)] * 2
+        + [pltpu.HBM((model // 2, inner), jnp.bfloat16)] * 2,
+        compiler_params=pltpu.CompilerParams(vmem_limit_bytes=56 * MIB),
+        cost_estimate=cost(8 * frames * model * inner, 2 * frames * inner, 4 * frames * model + 8 * model * inner),
+        name="grads_of_both",
+    )(place, *[in_hbm(p) for p in (*acts, *branches)], *([in_hbm(source_in)] * count), *([in_hbm(source_out)] * count), in_hbm(dep))
 
 
 def shards(
@@ -1186,18 +1408,14 @@
     offset = place * width
     near_heads = heads // 2
     pair = 2 * width
-    info = jnp.stack([side, far, offset, lengths[0]]).astype(jnp.int32)
-
-    def near_half(array, axis, index):
-        size = array.shape[axis] // 2
-        return lax.dynamic_slice_in_dim(array, index * size, size, axis)
+    places = jnp.stack([place, row_place]).astype(jnp.int32)
+    info = jnp.stack([side, far, offset, lengths[0], row_place]).astype(jnp.int32)
 
     flat_features = features.reshape(tokens, model)
     after_first, act_first, slope_first, act_attend = first_forward(
         flat_features, gain_first, gain_attend, first_in, first_out
     )
     act_near, act_far = swap(act_attend, "tm", 1), swap(act_attend, "tm", 2)
-    act_cross = swap(act_far, "tm", 1)
 
     near_table = lax.dynamic_slice_in_dim(bias_table, side * near_heads, near_heads, 0)
     span = pair + frames
@@ -1211,17 +1429,22 @@
     key_blocks = frames // LANES
     block = jnp.arange(key_blocks)
     block = (block + far * (key_blocks // 2)) % key_blocks
-    at = jnp.concatenate([frames - LANES - LANES * block, LANES * block, lengths[:1]]).astype(jnp.int32)
+    at = jnp.concatenate([frames - LANES - LANES * block, LANES * block, lengths[:1], side[None]]).astype(jnp.int32)
 
     query, key, value = project(info, act_attend, act_near, (query_weight, key_weight, value_weight))
+    act_far, act_first, key, bias = tie(act_far, act_first, key, bias)
+    act_cross = swap(act_far, "tm", 1)
+    act_first_near, act_first_far = swap(act_first, "tm", 1), swap(act_first, "tm", 2)
     key_far, value_far = project(info, act_far, act_cross, (key_weight, value_weight))
-    mixed, lse = attend(at, query, key, key_far, value, value_far, bias, near_heads, head_dim)
-    own_mixed = near_half(mixed, 0, side)
-    other_mixed = swap(near_half(mixed, 0, 1 - side), "tm", 1)
+    own_mixed, other_mixed, lse = attend(
+        at, query, key, key_far, value, value_far, bias, near_heads, head_dim
+    )
+    other_mixed = swap(other_mixed, "tm", 1)
 
     attended, after_attend, act_conv, joined_value, gate, gated = mix(
-        info, own_mixed, other_mixed, output_weight, after_first, gain_conv, point_in
-    )
+        info, own_mixed, other_mixed, output_weight, after_first, gain_conv, point_in, act_first_far
+    )
+    act_first_all = [act_first, act_first_near, act_first_far, swap(act_first_far, "tm", 1)]
     up = [(i, i + 1) for i in range(parts - 1)]
     down = [(j, i) for i, j in up]
     gated_before = lax.ppermute(gated[width - half :].astype(jnp.bfloat16), "tm", up)
@@ -1232,9 +1455,11 @@
     count = count[0]
     rstd_batch = lax.rsqrt(spread / count + EPS)
     stats = jnp.stack([batch_mean, rstd_batch, batch_scale, batch_shift])
-    act_batch, act_second, output, branch_second, grad, d_branch, d_normal, second_sums = second_both(
-        info, filtered, stats, after_attend, cotangent.reshape(tokens, model), gain_second, gain_final,
-        point_out, second_in, second_out,
+    (
+        act_batch, act_second, output, branch_second, grad, d_branch_send, d_branch, d_normal, second_sums,
+    ) = second_both(
+        info, filtered, stats, after_attend, cotangent.reshape(tokens, model),
+        gain_second, gain_final, point_out, second_in, second_out, (act_first_all[3],),
     )
     output = output.reshape(row_count, width, model)
 
@@ -1242,84 +1467,80 @@
         jnp.concatenate([d_normal[width - half :], filtered[width - half :]], axis=0), "tm", up
     )
     edge_after = lax.ppermute(jnp.concatenate([d_normal[:half], filtered[:half]], axis=0), "tm", down)
-    batch_grads = mesh_sum(second_sums[2:])
-    branch_second = after(branch_second, batch_grads)
-    d_joined, grad, d_attend, conv_small = conv_back(
+    first_step = second_sums[2:] + swap(second_sums[2:], *hops()[0])
+    first_step, act_second = tie(first_step, act_second)
+    act_second_far = swap(act_second, "tm", 2)
+    act_second_far, branch_second = tie(act_second_far, branch_second)
+    branch_second_far = swap(branch_second, "tm", 2)
+    batch_grads = mesh_sum(first_step, hops()[1:])
+    joined_send, d_joined, grad, d_attend, conv_small = conv_back(
         info, d_normal, filtered, edge_before, edge_after, stats, batch_grads / count, depth_weight,
         gated, gated_before, gated_after, joined_value, gate, point_in, after_attend, gain_conv, grad,
     )
     d_attend_near = swap(d_attend, "tm", 1)
-    d_mixed = mixed_back(info, d_attend, d_attend_near, output_weight)
-    d_query, d_key, d_value, skew_lines = attend_back(
-        at, query, key, key_far, value, value_far, d_mixed, lse, bias, near_heads, head_dim
-    )
-    far_send, far_keep = input_back(info, (d_key, d_value), (pair, pair), (key_weight, value_weight), width)
-    far_mine = far_keep + swap(far_send, "tm", 1).astype(jnp.float32)
-    far_back = swap(far_mine.astype(jnp.bfloat16), "tm", 2)
-    pair_send, pair_keep = input_back(
-        info, (d_query, d_key, d_value), (0, 0, 0), (query_weight, key_weight, value_weight), width
-    )
-    d_input = pair_keep + swap(pair_send, "tm", 1).astype(jnp.float32) + far_back.astype(jnp.float32)
-    _, scaled_attend, rstd_attend = normed_of(after_first, gain_attend)
-    d_values, grad_gain_attend = norm_backward(d_input, scaled_attend, rstd_attend, gain_attend)
-    grad = grad + d_values
-    branch_first = (0.5 * grad).astype(jnp.bfloat16)
-    branch_first_all = spread_tm(branch_first)
-    grad_features, grad_gain_first = first_backward(
-        info, grad, flat_features, gain_first, slope_first, first_in, first_out
-    )
-    grad_features = grad_features.reshape(row_count, width, model)
-
-    act_first_all = spread_tm(act_first, act_far)
-    mid_first, slope_first_part = again(place, act_first_all, first_in, groups)
-    branch_second_all = spread_tm(branch_second)
-    act_second_all = spread_tm(act_second, branch_second_all[2])
-    mid_second, slope_second_part = again(place, act_second_all, second_in, groups)
-    second_out_piece = reduce_rows(grad_out_of(mid_second, branch_second_all))
-    second_in_piece = reduce_rows(
-        grad_in_of(place, slope_second_part, act_second_all, branch_second_all, second_out, groups), True
-    )
-    first_out_piece = reduce_rows(grad_out_of(mid_first, branch_first_all))
-    first_in_piece = reduce_rows(
-        grad_in_of(place, slope_first_part, act_first_all, branch_first_all, first_out, groups), True
-    )
-
-    def near_exchange(array):
-        return (near_half(array, 1, side), swap(near_half(array, 1, 1 - side), "tm", 1))
-
+
+    held = near_heads * head_dim
+    share = model // groups
     conv_send, conv_keep = cross_grads(
         info,
         [
-            ((act_conv, swap(act_conv, "tm", 1)), near_exchange(d_joined)),
-            ((act_batch, swap(act_batch, "tm", 1)), near_exchange(d_branch)),
-        ],
-    )
-    attend_send, attend_keep = cross_grads(
+            ((act_conv, swap(act_conv, "tm", 1)), (d_joined, swap(joined_send, "tm", 1)), model),
+            ((act_batch, swap(act_batch, "tm", 1)), (d_branch, swap(d_branch_send, "tm", 1)), held),
+            ((attended, swap(attended, "tm", 1)), (d_attend, d_attend_near), held),
+        ],
+    )
+
+    act_second_all = [
+        act_second, swap(act_second, "tm", 1), act_second_far, swap(act_second_far, "tm", 1)
+    ]
+    branch_second_far, conv_send = tie(branch_second_far, conv_send)
+    conv_got = swap(conv_send, "tm", 2)
+    branch_second_all = [
+        branch_second, swap(branch_second, "tm", 1), branch_second_far, swap(branch_second_far, "tm", 1)
+    ]
+    out_send, out_keep, in_send, in_keep = grads_of_both(
+        places, act_second_all, branch_second_all, second_in, second_out, groups, conv_keep
+    )
+    d_attend_near, in_keep = tie(d_attend_near, in_keep)
+    second_sums_of = [RowSum(out_send, out_keep, share), RowSum(in_send, in_keep, share)]
+
+    d_query, d_key, d_value, skew_lines, far_send, far_keep = attend_back(
+        at, query, key, key_far, value, value_far, d_attend, d_attend_near,
+        (output_weight, key_weight, value_weight), lse, bias, near_heads, head_dim,
+    )
+    far_mine = add(info, (far_keep, swap(far_send, "tm", 1)), jnp.bfloat16, second_sums_of[0].terms[1])
+    far_back = swap(far_mine, "tm", 2)
+    conv_sum = opened(info, conv_keep, conv_got, share, far_mine)
+    kept = conv_sum.terms[0]
+    pair_send, pair_keep = input_back(
+        info, (d_query, d_key, d_value), (0, 0, 0), (query_weight, key_weight, value_weight), width, (kept,)
+    )
+    attend_sum = RowSum(*cross_grads(
         info,
         [
-            ((act_attend, act_near), (d_query,)),
-            ((act_attend, act_near, act_far, act_cross), (d_key,)),
-            ((act_attend, act_near, act_far, act_cross), (d_value,)),
-            (
-                (attended, swap(attended, "tm", 1)),
-                (near_half(d_attend, 1, side), near_half(d_attend_near, 1, side)),
-            ),
-        ],
-    )
-
-    def far_sum(send, keep, *earlier):
-        got = swap(after(send, *earlier), "tm", 2)
-        return (keep.astype(jnp.float32) + got.astype(jnp.float32)).astype(jnp.bfloat16)
-
-    conv_piece = reduce_rows(far_sum(conv_send, conv_keep, far_back))
-    attend_piece = reduce_rows(far_sum(attend_send, attend_keep, branch_first_all[2]))
-    second_in_pieces = spread_tm(second_in_piece, branch_first_all[2])
-    second_out_pieces = spread_tm(second_out_piece, branch_first_all[2])
-    conv_pieces = spread_tm(conv_piece, branch_first_all[2])
-    attend_pieces = spread_tm(attend_piece)
-    first_out_pieces = spread_tm(first_out_piece)
-    first_in_pieces = spread_tm(first_in_piece)
-
+            ((act_attend, act_near), (d_query,), held),
+            ((act_attend, act_near, act_far, act_cross), (d_key,), held),
+            ((act_attend, act_near, act_far, act_cross), (d_value,), held),
+        ],
+        split=False,
+        deps=(pair_keep, second_sums_of[1].terms[1]),
+    ), share)
+    mid_first, slope_first_part = again(places, act_first_all, first_in, groups, attend_sum.terms[0])
+    grad, branch_first, grad_gain_attend = branch_of(
+        info, pair_keep, swap(pair_send, "tm", 1), far_back, after_first, gain_attend, grad, (mid_first,)
+    )
+    branch_far = swap(branch_first, "tm", 2)
+    grad_features, grad_gain_first = first_backward(
+        info, grad, flat_features, gain_first, slope_first, first_in, first_out, ()
+    )
+    grad_features = grad_features.reshape(row_count, width, model)
+    early_sums = [*second_sums_of, conv_sum]
+    kept = merge(info, early_sums, grad_gain_first)
+    branch_far, conv_sum.terms[0] = tie(branch_far, kept)
+    branch_first_all = [branch_first, swap(branch_first, "tm", 1), branch_far, swap(branch_far, "tm", 1)]
+    first_out_sum = RowSum(
+        *grad_out_of(places, mid_first, branch_first_all, share, attend_sum.terms[1]), share
+    )
     table_lines = sum(jnp.pad(skew_lines[:, r], ((0, 0), (7 - r, 0)))[:, :span] for r in range(8))
     near_grad = lax.dot_general(
         table_lines, one_hot, (((1,), (0,)), ((), ())), precision=lax.Precision.HIGHEST
@@ -1330,23 +1551,45 @@
     small = jnp.concatenate(
         [
             grad_gain_first,
-            grad_gain_attend[None],
+            grad_gain_attend,
             second_sums[:2],
             conv_small,
             jnp.pad(grad_table.reshape(1, -1), ((0, 0), (0, model - heads * bucket_count))),
         ],
         axis=0,
     )
-    small = mesh_sum(small)
-    share = model // groups
+    first_in_sum = RowSum(*grad_in_of(
+        places, slope_first_part, act_first_all, branch_first_all, first_out, groups, share,
+        first_out_sum.terms[0],
+    ), share)
+    steps = hops()
+    kept = merge(info, early_sums, first_in_sum.terms[0])
+    small = add(info, (small, swap(small, *steps[0])), jnp.float32, kept)
+    late_sums = [attend_sum, first_out_sum]
+    kept = merge(info, late_sums, small)
+    small = add(info, (small, swap(small, *steps[1])), jnp.float32, kept)
+    early = joined(info, early_sums, small)
+    early_pieces = spread_tm(early)
+    kept = merge(info, [first_in_sum], early)
+    for step in steps[2:-2]:
+        small = add(info, (small, swap(small, *step)), jnp.float32, kept)
+    kept = merge(info, late_sums, small)
+    small = add(info, (small, swap(small, *steps[-2])), jnp.float32, kept)
+    kept = merge(info, [first_in_sum], small)
+    attend_piece = joined(info, [attend_sum], kept)
+    attend_got = swap(attend_piece, "tm", 2)
+    first_out_piece = joined(info, [first_out_sum], attend_piece)
+    first_out_pieces = spread_tm(first_out_piece)
+    small = add(info, (small, swap(small, *steps[-1])), jnp.float32, first_out_piece)
+    attend_piece = join(info, [[attend_piece, attend_got]], small)
+    attend_pieces = [attend_piece, swap(attend_piece, "tm", 1)]
     gains = lax.dynamic_slice_in_dim(small[:5], row_place * share, share, 1)
     grad_depth = small[5 : 5 + taps]
     grad_table = small[5 + taps, : heads * bucket_count].reshape(heads, bucket_count)
 
     relative = jnp.arange(parts) ^ place
     crossed = (relative % 2) * 2 + relative // 2
-    (grad_first_in,) = lay_columns(first_in_pieces, (model,), groups, relative)
-    (grad_second_in,) = lay_columns(second_in_pieces, (model,), groups, relative)
+    quarter = model // parts
 
     def lay_rows(pieces):
         size = pieces[0].shape[0]
@@ -1355,11 +1598,19 @@
             out = lax.dynamic_update_index_in_dim(out, pieces[k].astype(jnp.float32), place ^ k, 0)
         return out.reshape(parts * size, model)
 
+    (grad_second_in,) = lay_columns([p[:, model : 2 * model] for p in early_pieces], (model,), groups, relative)
+    grad_second_out = lay_rows([p[:, :model] for p in early_pieces])
+    grad_point_in, grad_point_out, grad_output = lay_columns(
+        [p[:, 2 * model :] for p in early_pieces], (2 * quarter, quarter, quarter), 1, crossed
+    )
+    grad_query, grad_key, grad_value = lay_columns(
+        attend_pieces, (2 * quarter,) * 3, 1, jnp.stack([side, 1 - side])
+    )
+    first_in_pieces = spread_tm(
+        joined(info, [first_in_sum], grad_second_in, grad_second_out, grad_point_out, grad_query)
+    )
     grad_first_out = lay_rows(first_out_pieces)
-    grad_second_out = lay_rows(second_out_pieces)
-    quarter = model // parts
-    grad_query, grad_key, grad_value, grad_output = lay_columns(attend_pieces, (quarter,) * 4, 1, crossed)
-    grad_point_in, grad_point_out = lay_columns(conv_pieces, (2 * quarter, quarter), 1, crossed)
+    (grad_first_in,) = lay_columns(first_in_pieces, (model,), groups, relative)
     return (
         output,
         grad_features,

time: 570 us -> 544 us (0.954)
  Pallas kernels: 214 us -> 285 us
  waiting for transfers between devices: 185 us -> 127 us
  local copies, waits for them, and re-layouts: 57.7 us -> 36.6 us
  other arithmetic: 19.3 us -> 8.81 us
  starting transfers between devices: 77.2 us -> 70 us
    pallas_call x11 -> x28, Pallas kernels: 94.8 us -> 156 us  [flow_call(): pl.pallas_call(kernel, in_specs=scalars() + [pl.BlockSpec(memory_space=pl...]
    ppermute x78 -> x70, waiting for transfers between devices: 182 us -> 124 us  [swap(): return lax.ppermute(value, axis, [(i, i ^ bit) for i in range(count)])]
    unnamed x198 -> x180, local copies, waits for them, and re-layouts: 41.1 us -> 25.9 us
    convert_element_type x16 -> x0, other arithmetic: 11.9 us -> none  [the longest x12 6.12 us: reduce_rows(): (keep.astype(jnp.float32) + got.astype(jnp.float32)).astype(jnp.bfloat16)]
    pallas_call x2 -> x1, Pallas kernels: 23.5 us -> 13.1 us  [again(): pl.pallas_call(functools.partial(again_kernel, count), grid_spec=pltpu.Pr...]
    pallas_call x9 -> x8, Pallas kernels: 45.9 us -> 53.7 us  [the longest x1 20.6 us: grads_of_both(): pl.pallas_call(functools.partial(both_kernel, count, inner // groups, mod...]
    ppermute x78 -> x70, starting transfers between devices: 71 us -> 63.9 us  [swap(): return lax.ppermute(value, axis, [(i, i ^ bit) for i in range(count)])]
    pallas_call x1, Pallas kernels: 21.5 us -> 28.5 us  [attend_back(): pl.pallas_call(functools.partial(attend_back_kernel, head_dim ** (-0.5)),...]
  transfers between devices with their start and end apart: 82 -> 74, of which waited for: 33 -> 32; matrix products, arithmetic and copies ran while one was open for 7% -> 3% of each run, Pallas kernels for 26% -> 43%
where the time goes in v3:
time: 544 us; the launch traced here: 534 us
  Pallas kernels  285 us (52%)
  waiting for transfers between devices  127 us (23%)
  starting transfers between devices  70 us (13%)
  local copies, waits for them, and re-layouts  36.6 us (7%)
  other arithmetic  8.81 us (2%)
    pallas_call x28, Pallas kernels, flow_call(): pl.pallas_call(kernel, in_specs=scalars() + [pl.BlockSpec(memory_space=pl...  156 us
    ppermute x70, waiting for transfers between devices, swap(): return lax.ppermute(value, axis, [(i, i ^ bit) for i in range(count)])  124 us
    ppermute x70, starting transfers between devices, swap(): return lax.ppermute(value, axis, [(i, i ^ bit) for i in range(count)])  63.9 us
    pallas_call x1, Pallas kernels, attend_back(): pl.pallas_call(functools.partial(attend_back_kernel, head_dim ** (-0.5)),...  28.5 us
    unnamed x180, local copies, waits for them, and re-layouts  25.9 us
    pallas_call x1, Pallas kernels, grads_of_both(): pl.pallas_call(functools.partial(both_kernel, count, inner // groups, mod...  20.6 us
    pallas_call x1, Pallas kernels, first_forward(): pl.pallas_call(first_kernel, grid=(inner // BLOCK,), in_specs=[whole((tok...  14.5 us
    pallas_call x1, Pallas kernels, attend(): pl.pallas_call(functools.partial(attend_kernel, head_dim ** (-0.5)), out_...  14 us
  transfers between devices with their start and end apart: 74, of which 32 were waited for; matrix products, arithmetic and copies ran while one was open for 3% of the time, Pallas kernels for 43%

profile of v3, /device:TPU:0, one launch (start us, length us, event | category | flops | bytes accessed | tf_op | source)
XLA Modules:
  0.0 533.6 jit_solution(14775308717349302042)
XLA Ops:
  2.1 14.5 %first_forward.1 = (f32[384,1024]{1,0:T(8,128)}, bf16[384,1024]{1,0:T(8,128)(2,1)}, bf16[384,4096]{1,0:T(8,128)(2,1)}, bf16[384,1024]{1,0:T(8,128)(2,1)}) custom-call(bf16[384,1024]{1,0:T(8,128)(2,1)} %bitcast.92, f32[1,1024]{1,0:T(1,128)S(1)} %bitcast.89, f32[1,1024]{1,0:T(1,128)S(1)} %bitcast.87, bf16[1024,4096]{1,0:T(8,128)(2,1)} %refs_4_.7, ...), custom_call_target="tpu_custom_call" | custom-call | flops 3221225 | bytes 9961 | tf_op jit(solution)/shard_map/first_forward/pallas_call | solution.py:805
  17.0 2.6 collective-permute-start.1
  22.8 4.1 bias_rows.1.bias_ref
  27.9 6.6 %project.2 = (bf16[768,512]{1,0:T(8,128)(2,1)}, bf16[768,512]{1,0:T(8,128)(2,1)}, bf16[768,512]{1,0:T(8,128)(2,1)}) custom-call(s32[5]{0:T(128)S(1)} %stack.44.info, bf16[384,1024]{1,0:T(8,128)(2,1)} %get-tuple-element.128.refs_0_.refs_3_.refs_8_, bf16[384,1024]{1,0:T(8,128)(2,1)} %copy-done.17, bf16[1024,1024]{1,0:T(8,128)(2,1)} %refs_3_.7, ...), custom_call_target="tpu_custom_call" | custom-call | flops 1207959 | bytes 5111 | tf_op jit(solution)/shard_map/project/pallas_call | solution.py:157
  34.5 3.5 collective-permute-done.1.refs_0_.refs_5_.refs_10_
  41.1 5.2 project.3
  48.7 14.0 %attend.1 = (bf16[384,512]{1,0:T(8,128)(2,1)}, bf16[384,512]{1,0:T(8,128)(2,1)}, f32[4,1,768]{2,1,0:T(1,128)}) custom-call(s32[26]{0:T(128)S(1)} %pad_add_fusion.at, bf16[768,512]{1,0:T(8,128)(2,1)S(1)} %copy-done.5, bf16[768,512]{1,0:T(8,128)(2,1)S(1)} %copy-done.6, bf16[768,512]{1,0:T(8,128)(2,1)S(1)} %copy-done.8, bf16[768,512]{1,0:T(8,128)(2,1)S(1)} %copy-done.7, ...), custom_call_target="tpu_custom_call" | custom-call | flops 1207959 | bytes 4587 | tf_op jit(solution)/shard_map/attend/pallas_call | solution.py:998
  65.6 6.1 %mix.1 = (bf16[384,1024]{1,0:T(8,128)(2,1)}, f32[384,1024]{1,0:T(8,128)}, bf16[384,1024]{1,0:T(8,128)(2,1)}, bf16[384,1024]{1,0:T(8,128)(2,1)}, bf16[384,1024]{1,0:T(8,128)(2,1)}, /*index=5*/f32[384,1024]{1,0:T(8,128)}) custom-call(s32[5]{0:T(128)S(1)} %stack.44.info, bf16[384,512]{1,0:T(8,128)(2,1)S(1)} %copy-done.12, ...), custom_call_target="tpu_custom_call" | custom-call | flops 1207959 | bytes 7077 | tf_op jit(solution)/shard_map/mix/pallas_call | solution.py:349
  76.7 3.0 collective-permute-done.6.refs_2_.refs_9_
  80.3 5.3 filter_frames.1
  86.3 2.3 collective-permute-start.7
  95.4 2.2 collective-permute-done.9
  99.3 2.2 collective-permute-done.10
  101.6 2.6 collective-permute-start.11
  109.0 26.3 %second_both.1 = (bf16[384,1024]{1,0:T(8,128)(2,1)}, bf16[384,1024]{1,0:T(8,128)(2,1)}, bf16[384,1024]{1,0:T(8,128)(2,1)}, bf16[384,1024]{1,0:T(8,128)(2,1)}, f3...) custom-call(s32[5]{0:T(128)S(1)} %stack.44.info, ...), custom_call_target="tpu_custom_call" | custom-call | flops 7247757 | bytes 14962 | tf_op jit(solution)/shard_map/second_both/pallas_call | solution.py:157
  137.5 2.2 collective-permute-done.15
  150.3 2.6 collective-permute-start.19
  157.6 3.3 collective-permute-start.30
  161.5 13.4 %conv_back.1 = (bf16[384,1024]{1,0:T(8,128)(2,1)}, bf16[384,1024]{1,0:T(8,128)(2,1)}, f32[384,1024]{1,0:T(8,128)}, bf16[384,1024]{1,0:T(8,128)(2,1)}, f32[6,1024]{1,0:T(8,128)}) custom-call(s32[5]{0:T(128)S(1)} %stack.44.info, f32[384,1024]{1,0:T(8,128)} %get-tuple-element.147.refs_0_, f32[384,1024]{1,0:T(8,128)} %get-tuple-element.143.refs_0_.refs_1_, ...), custom_call_target="tpu_custom_call" | custom-call | flops 805306 | bytes 8839 | tf_op jit(solution)/shard_map/conv_back/pallas_call | solution.py:157
  179.6 9.2 %cross_grads.2 = (bf16[1024,1024]{1,0:T(8,128)(2,1)}, bf16[1024,1024]{1,0:T(8,128)(2,1)}) custom-call(s32[5]{0:T(128)S(1)} %stack.44.info, bf16[384,1024]{1,0:T(8,128)(2,1)} %get-tuple-element.159.refs_0_, bf16[384,1024]{1,0:T(8,128)(2,1)} %copy-done.50, bf16[384,1024]{1,0:T(8,128)(2,1)} %get-tuple-element.160.refs_2_, bf16[384,1024]{1,0:T(8,128)(2,1)} %copy-done.55, ...), custom_call_target="tpu_custom_call" | custom-call | flops 1610612 | bytes 6422 | tf_op jit(solution)/shard_map/cross_grads/pallas_call | solution.py:157
  188.7 6.4 %collective-permute-done.25.refs_6_ = bf16[384,1024]{1,0:T(8,128)(2,1)S(1)} collective-permute-done((bf16[384,1024]{1,0:T(8,128)(2,1)S(1)}, bf16[384,1024]{1,0:T(8,128)(2,1)S(1)}, u32[]{:S(2)}, u32[]{:S(2)}) %collective-permute-start.25) | collective-permute-done | bytes 786464 | tf_op jit(solution)/shard_map/ppermute | solution.py:20
  198.6 2.2 collective-permute-done.23.refs_3_
  202.9 20.6 %grads_of_both.1 = (bf16[512,1024]{1,0:T(8,128)(2,1)}, bf16[512,1024]{1,0:T(8,128)(2,1)}, bf16[512,1024]{1,0:T(8,128)(2,1)}, bf16[512,1024]{1,0:T(8,128)(2,1)}) custom-call(s32[2]{0:T(128)} %pad_add_fusion.1.at, bf16[384,1024]{1,0:T(8,128)(2,1)} %get-tuple-element.155.refs_0_, bf16[384,1024]{1,0:T(8,128)(2,1)} %copy-done.44, bf16[384,1024]{1,0:T(8,128)(2,1)} %copy-done.42, ...), custom_call_target="tpu_custom_call" | custom-call | flops 6442450 | bytes 7340 | tf_op jit(solution)/shard_map/grads_of_both/pallas_call | solution.py:1348
  225.0 28.5 %attend_back.1 = (bf16[768,512]{1,0:T(8,128)(2,1)}, bf16[1536,512]{1,0:T(8,128)(2,1)}, bf16[1536,512]{1,0:T(8,128)(2,1)}, f32[4,8,2304]{2,1,0:T(8,128)}, bf16[384,1024]{1,0:T(8,128)(2,1)}, /*index=5*/f32[384,1024]{1,0:T(8,128)}) custom-call(s32[26]{0:T(128)S(1)} %pad_add_fusion.at, bf16[768,512]{1,0:T(8,128)(2,1)} %get-tuple-element.129.q_ref, ...), custom_call_target="tpu_custom_call" | custom-call | flops 3019898 | bytes 6946 | tf_op jit(solution)/shard_map/attend_back/pallas_call | solution.py:1134
  257.3 3.2 add.476.refs_2_
  262.8 4.4 merge.7
  267.2 7.5 %input_back.1 = (bf16[384,1024]{1,0:T(8,128)(2,1)}, f32[384,1024]{1,0:T(8,128)}) custom-call(s32[5]{0:T(128)S(1)} %stack.44.info, bf16[768,512]{1,0:T(8,128)(2,1)} %get-tuple-element.172.refs_0_.refs_2_, bf16[1536,512]{1,0:T(8,128)(2,1)} %get-tuple-element.173.refs_1_.refs_7_, bf16[1536,512]{1,0:T(8,128)(2,1)} %get-tuple-element.174.refs_2_.refs_12_, ...), custom_call_target="tpu_custom_call" | custom-call | flops 1207959 | bytes 6291 | tf_op jit(solution)/shard_map/input_back/pallas_call | solution.py:157
  275.4 4.3 collective-permute-done.38.refs_14_.refs_3_
  280.6 9.8 %cross_grads.3 = (bf16[512,1536]{1,0:T(8,128)(2,1)}, bf16[512,1536]{1,0:T(8,128)(2,1)}) custom-call(s32[5]{0:T(128)S(1)} %stack.44.info, bf16[384,1024]{1,0:T(8,128)(2,1)} %get-tuple-element.128.refs_0_.refs_3_.refs_8_, bf16[384,1024]{1,0:T(8,128)(2,1)} %copy-done.17, bf16[768,512]{1,0:T(8,128)(2,1)} %get-tuple-element.172.refs_0_.refs_2_, ...), custom_call_target="tpu_custom_call" | custom-call | flops 2013265 | bytes 7471 | tf_op jit(solution)/shard_map/cross_grads/pallas_call | solution.py:157
  291.3 13.1 %again.1 = (bf16[1024,1536]{1,0:T(8,128)(2,1)}, bf16[1024,1536]{1,0:T(8,128)(2,1)}) custom-call(s32[1]{0:T(128)} %bitcast.16.at, bf16[384,1024]{1,0:T(8,128)(2,1)} %get-tuple-element.141.refs_0_, bf16[384,1024]{1,0:T(8,128)(2,1)} %copy-done.30, bf16[384,1024]{1,0:T(8,128)(2,1)} %copy-done.20, bf16[384,1024]{1,0:T(8,128)(2,1)} %copy-done.19, ...), custom_call_target="tpu_custom_call" | custom-call | flops 1610612 | bytes 5767 | tf_op jit(solution)/shard_map/again/pallas_call | solution.py:1191
  305.5 5.7 %branch.1 = (f32[384,1024]{1,0:T(8,128)}, bf16[384,1024]{1,0:T(8,128)(2,1)}, f32[1,1024]{1,0:T(1,128)}) custom-call(s32[5]{0:T(128)S(1)} %stack.44.info, f32[384,1024]{1,0:T(8,128)} %get-tuple-element.180.refs_13_.refs_0_, bf16[384,1024]{1,0:T(8,128)(2,1)} %copy-done.54, bf16[384,1024]{1,0:T(8,128)(2,1)} %copy-done.53, ...), custom_call_target="tpu_custom_call" | custom-call | bytes 4329 | tf_op jit(solution)/shard_map/branch/pallas_call | solution.py:157
  312.7 14.7 %first_backward.1 = (bf16[384,1024]{1,0:T(8,128)(2,1)}, f32[1,1024]{1,0:T(1,128)}) custom-call(s32[5]{0:T(128)S(1)} %stack.44.info, f32[384,1024]{1,0:T(8,128)} %get-tuple-element.186.refs_0_, bf16[384,1024]{1,0:T(8,128)(2,1)} %bitcast.93, f32[1,1024]{1,0:T(1,128)} %bitcast.88, bf16[384,4096]{1,0:T(8,128)(2,1)} %get-tuple-element.187.refs_3_, ...), custom_call_target="tpu_custom_call" | custom-call | flops 3221225 | bytes 11538 | tf_op jit(solution)/shard_map/first_backward/pallas_call | solution.py:157
  328.5 4.9 merge.8
  336.2 11.2 %collective-permute-done.47.refs_4_.refs_1_ = bf16[512,1536]{1,0:T(8,128)(2,1)S(1)} collective-permute-done((bf16[512,1536]{1,0:T(8,128)(2,1)S(1)}, bf16[512,1536]{1,0:T(8,128)(2,1)S(1)}, u32[]{:S(2)}, u32[]{:S(2)}) %collective-permute-start.47) | collective-permute-done | bytes 1572896 | tf_op jit(solution)/shard_map/ppermute | solution.py:20
  350.8 7.9 %grad_out.1 = (bf16[512,1024]{1,0:T(8,128)(2,1)}, bf16[512,1024]{1,0:T(8,128)(2,1)}) custom-call(s32[2]{0:T(128)S(1)} %copy-done.16, bf16[1024,1536]{1,0:T(8,128)(2,1)} %get-tuple-element.185.refs_6_.act_ref, bf16[384,1024]{1,0:T(8,128)(2,1)} %get-tuple-element.200.refs_0_.refs_4_, bf16[384,1024]{1,0:T(8,128)(2,1)} %copy-done.32, ...), custom_call_target="tpu_custom_call" | custom-call | flops 1610612 | bytes 4194 | tf_op jit(solution)/shard_map/grad_out/pallas_call | solution.py:1239
  359.3 13.0 %grad_in.1 = (bf16[512,1024]{1,0:T(8,128)(2,1)}, bf16[512,1024]{1,0:T(8,128)(2,1)}) custom-call(s32[2]{0:T(128)S(1)} %copy-done.16, bf16[1024,1536]{1,0:T(8,128)(2,1)} %get-tuple-element.204.slope_ref, bf16[384,1024]{1,0:T(8,128)(2,1)} %get-tuple-element.141.refs_0_, bf16[384,1024]{1,0:T(8,128)(2,1)} %copy-done.30, bf16[384,1024]{1,0:T(8,128)(2,1)} %copy-done.20, ...), custom_call_target="tpu_custom_call" | custom-call | flops 3221225 | bytes 6815 | tf_op jit(solution)/shard_map/grad_in/pallas_call | solution.py:1288
  377.2 3.3 merge.9
  380.6 2.7 collective-permute-start.52
  383.6 2.6 collective-permute-start.54
  386.2 2.1 add.477.refs_4_.refs_0_
  389.3 4.2 merge.10
  394.1 2.1 add.478.refs_6_.refs_0_
  396.8 7.2 %collective-permute-done.52.refs_1_ = bf16[128,1024]{1,0:T(8,128)(2,1)S(1)} collective-permute-done((bf16[128,1024]{1,0:T(8,128)(2,1)}, bf16[128,1024]{1,0:T(8,128)(2,1)S(1)}, u32[]{:S(2)}, u32[]{:S(2)}) %collective-permute-start.52) | collective-permute-done | bytes 262176 | tf_op jit(solution)/shard_map/ppermute | solution.py:20
  404.7 5.1 collective-permute-done.53.refs_3_
  410.3 4.8 collective-permute-done.54.refs_5_
  415.1 2.9 join.5.refs_2_
  420.0 3.2 merge.11
  424.0 2.1 add.479.refs_4_.refs_0_
  426.1 17.0 %collective-permute-done.57.refs_3_ = bf16[256,1024]{1,0:T(8,128)(2,1)S(1)} collective-permute-done((bf16[256,1024]{1,0:T(8,128)(2,1)}, bf16[256,1024]{1,0:T(8,128)(2,1)S(1)}, u32[]{:S(2)}, u32[]{:S(2)}) %collective-permute-start.57) | collective-permute-done | bytes 524320 | tf_op jit(solution)/shard_map/ppermute | solution.py:20
  444.3 3.1 merge.12
  447.4 3.5 collective-permute-start.60
  450.9 5.5 %collective-permute-done.55.refs_1_ = f32[11,1024]{1,0:T(8,128)S(1)} collective-permute-done((f32[11,1024]{1,0:T(8,128)}, f32[11,1024]{1,0:T(8,128)S(1)}, u32[]{:S(2)}, u32[]{:S(2)}) %collective-permute-start.55) | collective-permute-done | bytes 45088 | tf_op jit(solution)/shard_map/ppermute | solution.py:20
  457.9 2.1 add.480.refs_2_.refs_0_
  461.5 2.6 merge.13
  468.0 13.9 %collective-permute-done.60.refs_1_ = bf16[128,1536]{1,0:T(8,128)(2,1)S(1)} collective-permute-done((bf16[128,1536]{1,0:T(8,128)(2,1)}, bf16[128,1536]{1,0:T(8,128)(2,1)S(1)}, u32[]{:S(2)}, u32[]{:S(2)}) %collective-permute-start.60) | collective-permute-done | bytes 393248 | tf_op jit(solution)/shard_map/ppermute | solution.py:20
  482.7 2.5 join.6.refs_2_.refs_0_
  485.2 2.3 collective-permute-done.59.refs_1_
  488.2 2.4 join.7.refs_2_
  497.2 10.9 %collective-permute-done.66.refs_1_ = bf16[128,1536]{1,0:T(8,128)(2,1)S(1)} collective-permute-done((bf16[128,1536]{1,0:T(8,128)(2,1)}, bf16[128,1536]{1,0:T(8,128)(2,1)S(1)}, u32[]{:S(2)}, u32[]{:S(2)}) %collective-permute-start.66) | collective-permute-done | bytes 393248 | tf_op jit(solution)/shard_map/ppermute | solution.py:20
  508.8 2.5 join.8.refs_0_
  513.4 2.1 lay_columns.4.refs_2_
  518.2 2.4 join.9.refs_0_
  523.5 6.0 %collective-permute-done.69.refs_2_ = bf16[128,1024]{1,0:T(8,128)(2,1)S(1)} collective-permute-done((bf16[128,1024]{1,0:T(8,128)(2,1)}, bf16[128,1024]{1,0:T(8,128)(2,1)S(1)}, u32[]{:S(2)}, u32[]{:S(2)}) %collective-permute-start.69) | collective-permute-done | bytes 262176 | tf_op jit(solution)/shard_map/ppermute | solution.py:20
  531.0 2.1 lay_columns.7
  (372 shorter events, 118.9 us)
Async XLA Ops:
  16.6 10.5 %collective-permute-start = (bf16[384,1024]{1,0:T(8,128)(2,1)}, bf16[384,1024]{1,0:T(8,128)(2,1)S(1)}, u32[]{:S(2)}, u32[]{:S(2)}) collective-permute-start(bf16[384,1024]{1,0:T(8,128)(2,1)} %get-tuple-element.128.refs_0_.refs_3_.refs_8_), channel_id=1, source_target_pairs={{0,1},{1,0},{2,3},{3,2},{4,5},{5,4},{6,7},{7,6},{8,9},{9,8},{10,11... | collective-permute-start | bytes 2359304 | tf_op jit(solution)/shard_map/ppermute | solution.py:20
  17.0 20.9 %collective-permute-start.1 = (bf16[384,1024]{1,0:T(8,128)(2,1)}, bf16[384,1024]{1,0:T(8,128)(2,1)S(1)}, u32[]{:S(2)}, u32[]{:S(2)}) collective-permute-start(bf16[384,1024]{1,0:T(8,128)(2,1)} %get-tuple-element.128.refs_0_.refs_3_.refs_8_), channel_id=1, source_target_pairs={{0,2},{1,3},{2,0},{3,1},{4,6},{5,7},{6,4},{7,5},{8,10},{9,11},{10,... | collective-permute-start | bytes 2359304 | tf_op jit(solution)/shard_map/ppermute | solution.py:20
  38.0 24.8 %collective-permute-start.4 = (bf16[384,1024]{1,0:T(8,128)(2,1)S(1)}, bf16[384,1024]{1,0:T(8,128)(2,1)S(1)}, u32[]{:S(2)}, u32[]{:S(2)}) collective-permute-start(bf16[384,1024]{1,0:T(8,128)(2,1)S(1)} %copy-done.29), channel_id=1, source_target_pairs={{0,2},{1,3},{2,0},{3,1},{4,6},{5,7},{6,4},{7,5},{8,10},{9,11},{10,... | collective-permute-start | bytes 2359304 | tf_op jit(solution)/shard_map/ppermute | solution.py:20
  75.4 4.3 collective-permute-start.6
  86.3 4.0 collective-permute-start.7
  93.8 3.8 collective-permute-start.9
  97.7 3.8 collective-permute-start.10
  99.3 8.8 %collective-permute-start.12 = (bf16[384,1024]{1,0:T(8,128)(2,1)S(1)}, bf16[384,1024]{1,0:T(8,128)(2,1)S(1)}, u32[]{:S(2)}, u32[]{:S(2)}) collective-permute-start(bf16[384,1024]{1,0:T(8,128)(2,1)S(1)} %copy-done.21), channel_id=1, source_target_pairs={{0,1},{1,0},{2,3},{3,2},{4,5},{5,4},{6,7},{7,6},{8,9},{9,8},{10,11... | collective-permute-start | bytes 2359304 | tf_op jit(solution)/shard_map/ppermute | solution.py:20
  101.6 4.7 collective-permute-start.11
  136.1 3.7 collective-permute-start.15
  137.5 38.0 %collective-permute-start.26 = (bf16[384,1024]{1,0:T(8,128)(2,1)S(1)}, bf16[384,1024]{1,0:T(8,128)(2,1)S(1)}, u32[]{:S(2)}, u32[]{:S(2)}) collective-permute-start(bf16[384,1024]{1,0:T(8,128)(2,1)S(1)} %copy-done.49), channel_id=1, source_target_pairs={{0,1},{1,0},{2,3},{3,2},{4,5},{5,4},{6,7},{7,6},{8,9},{9,8},{10,11... | collective-permute-start | bytes 2359304 | tf_op jit(solution)/shard_map/ppermute | solution.py:20
  140.6 34.4 %collective-permute-start.22 = (bf16[384,1024]{1,0:T(8,128)(2,1)}, bf16[384,1024]{1,0:T(8,128)(2,1)S(1)}, u32[]{:S(2)}, u32[]{:S(2)}) collective-permute-start(bf16[384,1024]{1,0:T(8,128)(2,1)} %get-tuple-element.155.refs_0_), channel_id=1, source_target_pairs={{0,2},{1,3},{2,0},{3,1},{4,6},{5,7},{6,4},{7,5},{8,10},{9,11},{10,... | collective-permute-start | bytes 2359304 | tf_op jit(solution)/shard_map/ppermute | solution.py:20
  142.9 3.7 collective-permute-start.17
  145.3 29.7 %collective-permute-start.29 = (bf16[384,512]{1,0:T(8,128)(2,1)}, bf16[384,512]{1,0:T(8,128)(2,1)S(1)}, u32[]{:S(2)}, u32[]{:S(2)}) collective-permute-start(bf16[384,512]{1,0:T(8,128)(2,1)} %get-tuple-element.164), channel_id=1, source_target_pairs={{0,1},{1,0},{2,3},{3,2},{4,5},{5,4},{6,7},{7,6},{8,9},{9,8},{10,11... | collective-permute-start | bytes 1179656 | tf_op jit(solution)/shard_map/ppermute | solution.py:20
  146.6 3.7 collective-permute-start.18
  148.2 9.3 %collective-permute-start.14 = (f32[4,1024]{1,0:T(4,128)S(1)}, f32[4,1024]{1,0:T(4,128)S(1)}, u32[]{:S(2)}, u32[]{:S(2)}) collective-permute-start(f32[4,1024]{1,0:T(4,128)S(1)} %pad_maximum_fusion.6), channel_id=1, source_target_pairs={{1,0},{2,1},{3,2},{5,4},{6,5},{7,6},{9,8},{10,9},{11,10},{13,12},{... | collective-permute-start | bytes 49160 | tf_op jit(solution)/shard_map/ppermute | solution.py:1469
  150.3 4.5 collective-permute-start.19
  154.8 6.0 %collective-permute-start.13 = (f32[4,1024]{1,0:T(4,128)S(1)}, f32[4,1024]{1,0:T(4,128)S(1)}, u32[]{:S(2)}, u32[]{:S(2)}) collective-permute-start(f32[4,1024]{1,0:T(4,128)S(1)} %pad_maximum_fusion.5), channel_id=1, source_target_pairs={{0,1},{1,2},{2,3},{4,5},{5,6},{6,7},{8,9},{9,10},{10,11},{12,13},{... | collective-permute-start | bytes 49160 | tf_op jit(solution)/shard_map/ppermute | solution.py:1466
  157.6 19.2 %collective-permute-start.30 = (bf16[384,1024]{1,0:T(8,128)(2,1)S(1)}, bf16[384,1024]{1,0:T(8,128)(2,1)S(1)}, u32[]{:S(2)}, u32[]{:S(2)}) collective-permute-start(bf16[384,1024]{1,0:T(8,128)(2,1)S(1)} %copy-done.48), channel_id=1, source_target_pairs={{0,1},{1,0},{2,3},{3,2},{4,5},{5,4},{6,7},{7,6},{8,9},{9,8},{10,11... | collective-permute-start | bytes 2359304 | tf_op jit(solution)/shard_map/ppermute | solution.py:20
  160.9 15.9 %collective-permute-start.28 = (bf16[384,1024]{1,0:T(8,128)(2,1)}, bf16[384,1024]{1,0:T(8,128)(2,1)S(1)}, u32[]{:S(2)}, u32[]{:S(2)}) collective-permute-start(bf16[384,1024]{1,0:T(8,128)(2,1)} %get-tuple-element.162.refs_4_), channel_id=1, source_target_pairs={{0,1},{1,0},{2,3},{3,2},{4,5},{5,4},{6,7},{7,6},{8,9},{9,8},{10,11... | collective-permute-start | bytes 2359304 | tf_op jit(solution)/shard_map/ppermute | solution.py:20
  175.5 19.6 %collective-permute-start.25 = (bf16[384,1024]{1,0:T(8,128)(2,1)S(1)}, bf16[384,1024]{1,0:T(8,128)(2,1)S(1)}, u32[]{:S(2)}, u32[]{:S(2)}) collective-permute-start(bf16[384,1024]{1,0:T(8,128)(2,1)S(1)} %copy-done.41), channel_id=1, source_target_pairs={{0,2},{1,3},{2,0},{3,1},{4,6},{5,7},{6,4},{7,5},{8,10},{9,11},{10,... | collective-permute-start | bytes 2359304 | tf_op jit(solution)/shard_map/ppermute | solution.py:20
  195.1 66.4 %collective-permute-start.32 = (bf16[1024,1024]{1,0:T(8,128)(2,1)}, bf16[1024,1024]{1,0:T(8,128)(2,1)S(1)}, u32[]{:S(2)}, u32[]{:S(2)}) collective-permute-start(bf16[1024,1024]{1,0:T(8,128)(2,1)} %get-tuple-element.175), channel_id=1, source_target_pairs={{0,2},{1,3},{2,0},{3,1},{4,6},{5,7},{6,4},{7,5},{8,10},{9,11},{10,... | collective-permute-start | bytes 6291464 | tf_op jit(solution)/shard_map/ppermute | solution.py:20
  196.4 4.5 collective-permute-start.24
  196.9 4.0 collective-permute-start.23
  196.9 5.1 collective-permute-start.31
  223.5 32.6 %collective-permute-start.34 = (bf16[512,1024]{1,0:T(8,128)(2,1)}, bf16[512,1024]{1,0:T(8,128)(2,1)S(1)}, u32[]{:S(2)}, u32[]{:S(2)}) collective-permute-start(bf16[512,1024]{1,0:T(8,128)(2,1)} %get-tuple-element.178), channel_id=1, source_target_pairs={{0,4},{4,0},{8,12},{12,8},{16,20},{20,16},{24,28},{28,24},{1,5},{5... | collective-permute-start | bytes 3145736 | tf_op jit(solution)/shard_map/ppermute | solution.py:20
  253.6 26.0 %collective-permute-start.38 = (bf16[512,1024]{1,0:T(8,128)(2,1)S(1)}, bf16[512,1024]{1,0:T(8,128)(2,1)S(1)}, u32[]{:S(2)}, u32[]{:S(2)}) collective-permute-start(bf16[512,1024]{1,0:T(8,128)(2,1)S(1)} %copy-done.87), channel_id=1, source_target_pairs={{0,4},{4,0},{8,12},{12,8},{16,20},{20,16},{24,28},{28,24},{1,5},{5... | collective-permute-start | bytes 3145736 | tf_op jit(solution)/shard_map/ppermute | solution.py:20
  254.3 36.2 %collective-permute-start.37 = (bf16[384,1024]{1,0:T(8,128)(2,1)S(1)}, bf16[384,1024]{1,0:T(8,128)(2,1)S(1)}, u32[]{:S(2)}, u32[]{:S(2)}) collective-permute-start(bf16[384,1024]{1,0:T(8,128)(2,1)S(1)} %copy-done.29), channel_id=1, source_target_pairs={{0,1},{1,0},{2,3},{3,2},{4,5},{5,4},{6,7},{7,6},{8,9},{9,8},{10,11... | collective-permute-start | bytes 2359304 | tf_op jit(solution)/shard_map/ppermute | solution.py:20
  260.6 43.8 %collective-permute-start.36 = (bf16[384,1024]{1,0:T(8,128)(2,1)}, bf16[384,1024]{1,0:T(8,128)(2,1)S(1)}, u32[]{:S(2)}, u32[]{:S(2)}) collective-permute-start(bf16[384,1024]{1,0:T(8,128)(2,1)} %add.476.refs_2_), channel_id=1, source_target_pairs={{0,2},{1,3},{2,0},{3,1},{4,6},{5,7},{6,4},{7,5},{8,10},{9,11},{10,... | collective-permute-start | bytes 2359304 | tf_op jit(solution)/shard_map/ppermute | solution.py:20
  274.7 29.7 %collective-permute-start.35 = (bf16[384,1024]{1,0:T(8,128)(2,1)}, bf16[384,1024]{1,0:T(8,128)(2,1)S(1)}, u32[]{:S(2)}, u32[]{:S(2)}) collective-permute-start(bf16[384,1024]{1,0:T(8,128)(2,1)} %get-tuple-element.181), channel_id=1, source_target_pairs={{0,1},{1,0},{2,3},{3,2},{4,5},{5,4},{6,7},{7,6},{8,9},{9,8},{10,11... | collective-permute-start | bytes 2359304 | tf_op jit(solution)/shard_map/ppermute | solution.py:20
  274.8 52.7 %collective-permute-start.40 = (bf16[512,1024]{1,0:T(8,128)(2,1)S(1)}, bf16[512,1024]{1,0:T(8,128)(2,1)S(1)}, u32[]{:S(2)}, u32[]{:S(2)}) collective-permute-start(bf16[512,1024]{1,0:T(8,128)(2,1)S(1)} %copy-done.88), channel_id=1, source_target_pairs={{0,4},{4,0},{8,12},{12,8},{16,20},{20,16},{24,28},{28,24},{1,5},{5... | collective-permute-start | bytes 3145736 | tf_op jit(solution)/shard_map/ppermute | solution.py:20
  311.2 22.2 %collective-permute-start.43 = (bf16[384,1024]{1,0:T(8,128)(2,1)}, bf16[384,1024]{1,0:T(8,128)(2,1)S(1)}, u32[]{:S(2)}, u32[]{:S(2)}) collective-permute-start(bf16[384,1024]{1,0:T(8,128)(2,1)} %get-tuple-element.200.refs_0_.refs_4_), channel_id=1, source_target_pairs={{0,2},{1,3},{2,0},{3,1},{4,6},{5,7},{6,4},{7,5},{8,10},{9,11},{10,... | collective-permute-start | bytes 2359304 | tf_op jit(solution)/shard_map/ppermute | solution.py:20
  312.2 35.2 %collective-permute-start.47 = (bf16[512,1536]{1,0:T(8,128)(2,1)S(1)}, bf16[512,1536]{1,0:T(8,128)(2,1)S(1)}, u32[]{:S(2)}, u32[]{:S(2)}) collective-permute-start(bf16[512,1536]{1,0:T(8,128)(2,1)S(1)} %copy-done.86), channel_id=1, source_target_pairs={{0,4},{4,0},{8,12},{12,8},{16,20},{20,16},{24,28},{28,24},{1,5},{5... | collective-permute-start | bytes 4718600 | tf_op jit(solution)/shard_map/ppermute | solution.py:20
  312.7 36.2 %collective-permute-start.45 = (bf16[384,1024]{1,0:T(8,128)(2,1)}, bf16[384,1024]{1,0:T(8,128)(2,1)S(1)}, u32[]{:S(2)}, u32[]{:S(2)}) collective-permute-start(bf16[384,1024]{1,0:T(8,128)(2,1)} %get-tuple-element.200.refs_0_.refs_4_), channel_id=1, source_target_pairs={{0,1},{1,0},{2,3},{3,2},{4,5},{5,4},{6,7},{7,6},{8,9},{9,8},{10,11... | collective-permute-start | bytes 2359304 | tf_op jit(solution)/shard_map/ppermute | solution.py:20
  333.4 15.6 %collective-permute-start.46 = (bf16[384,1024]{1,0:T(8,128)(2,1)S(1)}, bf16[384,1024]{1,0:T(8,128)(2,1)S(1)}, u32[]{:S(2)}, u32[]{:S(2)}) collective-permute-start(bf16[384,1024]{1,0:T(8,128)(2,1)S(1)} %collective-permute-done.43.refs_2_.refs_6_), channel_id=1, source_target_pairs={{0,1},{1,0},{2,3},{3,2},{4,5},{5,4},{6,7},{7,6},{8,9},{9,8},{10,11... | collective-permute-start | bytes 2359304 | tf_op jit(solution)/shard_map/ppermute | solution.py:20
  334.1 41.1 %collective-permute-start.41 = (bf16[256,1024]{1,0:T(8,128)(2,1)}, bf16[256,1024]{1,0:T(8,128)(2,1)S(1)}, u32[]{:S(2)}, u32[]{:S(2)}) collective-permute-start(bf16[256,1024]{1,0:T(8,128)(2,1)} %get-tuple-element.197), channel_id=1, source_target_pairs={{0,8},{4,12},{8,0},{12,4},{16,24},{20,28},{24,16},{28,20},{1,9},{5... | collective-permute-start | bytes 1572872 | tf_op jit(solution)/shard_map/ppermute | solution.py:20
  335.7 40.7 %collective-permute-start.42 = (bf16[256,1024]{1,0:T(8,128)(2,1)}, bf16[256,1024]{1,0:T(8,128)(2,1)S(1)}, u32[]{:S(2)}, u32[]{:S(2)}) collective-permute-start(bf16[256,1024]{1,0:T(8,128)(2,1)} %get-tuple-element.199), channel_id=1, source_target_pairs={{0,8},{4,12},{8,0},{12,4},{16,24},{20,28},{24,16},{28,20},{1,9},{5... | collective-permute-start | bytes 1572872 | tf_op jit(solution)/shard_map/ppermute | solution.py:20
  347.4 29.1 %collective-permute-start.44 = (bf16[256,1024]{1,0:T(8,128)(2,1)}, bf16[256,1024]{1,0:T(8,128)(2,1)}, u32[]{:S(2)}, u32[]{:S(2)}) collective-permute-start(bf16[256,1024]{1,0:T(8,128)(2,1)} %get-tuple-element.203), channel_id=1, source_target_pairs={{0,8},{4,12},{8,0},{12,4},{16,24},{20,28},{24,16},{28,20},{1,9},{5... | collective-permute-start | bytes 1572872 | tf_op jit(solution)/shard_map/ppermute | solution.py:20
  358.7 29.6 %collective-permute-start.49 = (bf16[512,1024]{1,0:T(8,128)(2,1)}, bf16[512,1024]{1,0:T(8,128)(2,1)S(1)}, u32[]{:S(2)}, u32[]{:S(2)}) collective-permute-start(bf16[512,1024]{1,0:T(8,128)(2,1)} %get-tuple-element.210), channel_id=1, source_target_pairs={{0,4},{4,0},{8,12},{12,8},{16,20},{20,16},{24,28},{28,24},{1,5},{5... | collective-permute-start | bytes 3145736 | tf_op jit(solution)/shard_map/ppermute | solution.py:20
  372.3 46.8 %collective-permute-start.51 = (bf16[512,1024]{1,0:T(8,128)(2,1)}, bf16[512,1024]{1,0:T(8,128)(2,1)S(1)}, u32[]{:S(2)}, u32[]{:S(2)}) collective-permute-start(bf16[512,1024]{1,0:T(8,128)(2,1)} %get-tuple-element.212), channel_id=1, source_target_pairs={{0,4},{4,0},{8,12},{12,8},{16,20},{20,16},{24,28},{28,24},{1,5},{5... | collective-permute-start | bytes 3145736 | tf_op jit(solution)/shard_map/ppermute | solution.py:20
  375.2 8.4 %collective-permute-start.39 = (f32[11,1024]{1,0:T(8,128)S(1)}, f32[11,1024]{1,0:T(8,128)S(1)}, u32[]{:S(2)}, u32[]{:S(2)}) collective-permute-start(f32[11,1024]{1,0:T(8,128)S(1)} %concatenate.36.refs_0_), channel_id=1, source_target_pairs={{0,2},{1,3},{2,0},{3,1},{4,6},{5,7},{6,4},{7,5},{8,10},{9,11},{10,... | collective-permute-start | bytes 135176 | tf_op jit(solution)/shard_map/ppermute | solution.py:20
  380.6 23.4 %collective-permute-start.52 = (bf16[128,1024]{1,0:T(8,128)(2,1)}, bf16[128,1024]{1,0:T(8,128)(2,1)S(1)}, u32[]{:S(2)}, u32[]{:S(2)}) collective-permute-start(bf16[128,1024]{1,0:T(8,128)(2,1)} %get-tuple-element.214), channel_id=1, source_target_pairs={{0,16},{4,20},{8,24},{12,28},{16,0},{20,4},{24,8},{28,12},{1,17},{... | collective-permute-start | bytes 786440 | tf_op jit(solution)/shard_map/ppermute | solution.py:20
  383.3 26.5 %collective-permute-start.53 = (bf16[128,1024]{1,0:T(8,128)(2,1)}, bf16[128,1024]{1,0:T(8,128)(2,1)S(1)}, u32[]{:S(2)}, u32[]{:S(2)}) collective-permute-start(bf16[128,1024]{1,0:T(8,128)(2,1)} %get-tuple-element.216), channel_id=1, source_target_pairs={{0,16},{4,20},{8,24},{12,28},{16,0},{20,4},{24,8},{28,12},{1,17},{... | collective-permute-start | bytes 786440 | tf_op jit(solution)/shard_map/ppermute | solution.py:20
  383.6 31.6 %collective-permute-start.54 = (bf16[128,1024]{1,0:T(8,128)(2,1)}, bf16[128,1024]{1,0:T(8,128)(2,1)}, u32[]{:S(2)}, u32[]{:S(2)}) collective-permute-start(bf16[128,1024]{1,0:T(8,128)(2,1)} %get-tuple-element.217), channel_id=1, source_target_pairs={{0,16},{4,20},{8,24},{12,28},{16,0},{20,4},{24,8},{28,12},{1,17},{... | collective-permute-start | bytes 786440 | tf_op jit(solution)/shard_map/ppermute | solution.py:20
  388.3 5.2 collective-permute-start.48
  396.2 27.0 %collective-permute-start.50 = (f32[11,1024]{1,0:T(8,128)}, f32[11,1024]{1,0:T(8,128)S(1)}, u32[]{:S(2)}, u32[]{:S(2)}) collective-permute-start(f32[11,1024]{1,0:T(8,128)} %add.478.refs_6_.refs_0_), channel_id=1, source_target_pairs={{0,4},{4,0},{8,12},{12,8},{16,20},{20,16},{24,28},{28,24},{1,5},{5... | collective-permute-start | bytes 135176 | tf_op jit(solution)/shard_map/ppermute | solution.py:20
  404.0 39.4 %collective-permute-start.56 = (bf16[256,1536]{1,0:T(8,128)(2,1)}, bf16[256,1536]{1,0:T(8,128)(2,1)S(1)}, u32[]{:S(2)}, u32[]{:S(2)}) collective-permute-start(bf16[256,1536]{1,0:T(8,128)(2,1)} %get-tuple-element.220), channel_id=1, source_target_pairs={{0,8},{4,12},{8,0},{12,4},{16,24},{20,28},{24,16},{28,20},{1,9},{5... | collective-permute-start | bytes 2359304 | tf_op jit(solution)/shard_map/ppermute | solution.py:20
  409.7 33.4 %collective-permute-start.57 = (bf16[256,1024]{1,0:T(8,128)(2,1)}, bf16[256,1024]{1,0:T(8,128)(2,1)S(1)}, u32[]{:S(2)}, u32[]{:S(2)}) collective-permute-start(bf16[256,1024]{1,0:T(8,128)(2,1)} %get-tuple-element.221), channel_id=1, source_target_pairs={{0,8},{4,12},{8,0},{12,4},{16,24},{20,28},{24,16},{28,20},{1,9},{5... | collective-permute-start | bytes 1572872 | tf_op jit(solution)/shard_map/ppermute | solution.py:20
  418.0 46.1 %collective-permute-start.64 = (bf16[128,3072]{1,0:T(8,128)(2,1)}, bf16[128,3072]{1,0:T(8,128)(2,1)}, u32[]{:S(2)}, u32[]{:S(2)}) collective-permute-start(bf16[128,3072]{1,0:T(8,128)(2,1)} %join.5.refs_2_), channel_id=1, source_target_pairs={{0,2},{1,3},{2,0},{3,1},{4,6},{5,7},{6,4},{7,5},{8,10},{9,11},{10,... | collective-permute-start | bytes 2359304 | tf_op jit(solution)/shard_map/ppermute | solution.py:20
  419.1 47.7 %collective-permute-start.63 = (bf16[128,3072]{1,0:T(8,128)(2,1)}, bf16[128,3072]{1,0:T(8,128)(2,1)S(1)}, u32[]{:S(2)}, u32[]{:S(2)}) collective-permute-start(bf16[128,3072]{1,0:T(8,128)(2,1)} %join.5.refs_2_), channel_id=1, source_target_pairs={{0,1},{1,0},{2,3},{3,2},{4,5},{5,4},{6,7},{7,6},{8,9},{9,8},{10,11... | collective-permute-start | bytes 2359304 | tf_op jit(solution)/shard_map/ppermute | solution.py:20
  423.3 36.8 %collective-permute-start.61 = (bf16[256,1024]{1,0:T(8,128)(2,1)}, bf16[256,1024]{1,0:T(8,128)(2,1)S(1)}, u32[]{:S(2)}, u32[]{:S(2)}) collective-permute-start(bf16[256,1024]{1,0:T(8,128)(2,1)} %get-tuple-element.226), channel_id=1, source_target_pairs={{0,8},{4,12},{8,0},{12,4},{16,24},{20,28},{24,16},{28,20},{1,9},{5... | collective-permute-start | bytes 1572872 | tf_op jit(solution)/shard_map/ppermute | solution.py:20
  443.1 13.3 %collective-permute-start.55 = (f32[11,1024]{1,0:T(8,128)}, f32[11,1024]{1,0:T(8,128)S(1)}, u32[]{:S(2)}, u32[]{:S(2)}) collective-permute-start(f32[11,1024]{1,0:T(8,128)} %add.479.refs_4_.refs_0_), channel_id=1, source_target_pairs={{0,8},{4,12},{8,0},{12,4},{16,24},{20,28},{24,16},{28,20},{1,9},{5... | collective-permute-start | bytes 135176 | tf_op jit(solution)/shard_map/ppermute | solution.py:20
  447.4 34.5 %collective-permute-start.60 = (bf16[128,1536]{1,0:T(8,128)(2,1)}, bf16[128,1536]{1,0:T(8,128)(2,1)S(1)}, u32[]{:S(2)}, u32[]{:S(2)}) collective-permute-start(bf16[128,1536]{1,0:T(8,128)(2,1)} %get-tuple-element.225), channel_id=1, source_target_pairs={{0,16},{4,20},{8,24},{12,28},{16,0},{20,4},{24,8},{28,12},{1,17},{... | collective-permute-start | bytes 1179656 | tf_op jit(solution)/shard_map/ppermute | solution.py:20
  456.4 31.1 %collective-permute-start.59 = (bf16[128,1024]{1,0:T(8,128)(2,1)}, bf16[128,1024]{1,0:T(8,128)(2,1)S(1)}, u32[]{:S(2)}, u32[]{:S(2)}) collective-permute-start(bf16[128,1024]{1,0:T(8,128)(2,1)} %get-tuple-element.223), channel_id=1, source_target_pairs={{0,16},{4,20},{8,24},{12,28},{16,0},{20,4},{24,8},{28,12},{1,17},{... | collective-permute-start | bytes 786440 | tf_op jit(solution)/shard_map/ppermute | solution.py:20
  460.0 31.6 %collective-permute-start.58 = (f32[11,1024]{1,0:T(8,128)}, f32[11,1024]{1,0:T(8,128)S(1)}, u32[]{:S(2)}, u32[]{:S(2)}) collective-permute-start(f32[11,1024]{1,0:T(8,128)} %add.480.refs_2_.refs_0_), channel_id=1, source_target_pairs={{0,16},{4,20},{8,24},{12,28},{16,0},{20,4},{24,8},{28,12},{1,17},{... | collective-permute-start | bytes 135176 | tf_op jit(solution)/shard_map/ppermute | solution.py:20
  464.2 53.3 %collective-permute-start.62 = (bf16[128,1024]{1,0:T(8,128)(2,1)}, bf16[128,1024]{1,0:T(8,128)(2,1)S(1)}, u32[]{:S(2)}, u32[]{:S(2)}) collective-permute-start(bf16[128,1024]{1,0:T(8,128)(2,1)} %get-tuple-element.228), channel_id=1, source_target_pairs={{0,16},{4,20},{8,24},{12,28},{16,0},{20,4},{24,8},{28,12},{1,17},{... | collective-permute-start | bytes 786440 | tf_op jit(solution)/shard_map/ppermute | solution.py:20
  466.8 44.6 %collective-permute-start.65 = (bf16[128,3072]{1,0:T(8,128)(2,1)}, bf16[128,3072]{1,0:T(8,128)(2,1)S(1)}, u32[]{:S(2)}, u32[]{:S(2)}) collective-permute-start(bf16[128,3072]{1,0:T(8,128)(2,1)} %collective-permute-done.64), channel_id=1, source_target_pairs={{0,1},{1,0},{2,3},{3,2},{4,5},{5,4},{6,7},{7,6},{8,9},{9,8},{10,11... | collective-permute-start | bytes 2359304 | tf_op jit(solution)/shard_map/ppermute | solution.py:20
  490.6 32.5 %collective-permute-start.71 = (bf16[128,1024]{1,0:T(8,128)(2,1)}, bf16[128,1024]{1,0:T(8,128)(2,1)S(1)}, u32[]{:S(2)}, u32[]{:S(2)}) collective-permute-start(bf16[128,1024]{1,0:T(8,128)(2,1)} %join.7.refs_2_), channel_id=1, source_target_pairs={{0,1},{1,0},{2,3},{3,2},{4,5},{5,4},{6,7},{7,6},{8,9},{9,8},{10,11... | collective-permute-start | bytes 786440 | tf_op jit(solution)/shard_map/ppermute | solution.py:20
  490.7 32.2 %collective-permute-start.72 = (bf16[128,1024]{1,0:T(8,128)(2,1)}, bf16[128,1024]{1,0:T(8,128)(2,1)S(1)}, u32[]{:S(2)}, u32[]{:S(2)}) collective-permute-start(bf16[128,1024]{1,0:T(8,128)(2,1)} %join.7.refs_2_), channel_id=1, source_target_pairs={{0,2},{1,3},{2,0},{3,1},{4,6},{5,7},{6,4},{7,5},{8,10},{9,11},{10,... | collective-permute-start | bytes 786440 | tf_op jit(solution)/shard_map/ppermute | solution.py:20
  491.6 16.4 %collective-permute-start.66 = (bf16[128,1536]{1,0:T(8,128)(2,1)}, bf16[128,1536]{1,0:T(8,128)(2,1)S(1)}, u32[]{:S(2)}, u32[]{:S(2)}) collective-permute-start(bf16[128,1536]{1,0:T(8,128)(2,1)} %join.6.refs_2_.refs_0_), channel_id=1, source_target_pairs={{0,2},{1,3},{2,0},{3,1},{4,6},{5,7},{6,4},{7,5},{8,10},{9,11},{10,... | collective-permute-start | bytes 1179656 | tf_op jit(solution)/shard_map/ppermute | solution.py:20
  511.3 4.3 collective-permute-start.67
  520.5 9.0 %collective-permute-start.69 = (bf16[128,1024]{1,0:T(8,128)(2,1)}, bf16[128,1024]{1,0:T(8,128)(2,1)S(1)}, u32[]{:S(2)}, u32[]{:S(2)}) collective-permute-start(bf16[128,1024]{1,0:T(8,128)(2,1)} %join.9.refs_0_), channel_id=1, source_target_pairs={{0,2},{1,3},{2,0},{3,1},{4,6},{5,7},{6,4},{7,5},{8,10},{9,11},{10,... | collective-permute-start | bytes 786440 | tf_op jit(solution)/shard_map/ppermute | solution.py:20
  522.9 6.7 %collective-permute-start.73 = (bf16[128,1024]{1,0:T(8,128)(2,1)S(1)}, bf16[128,1024]{1,0:T(8,128)(2,1)S(1)}, u32[]{:S(2)}, u32[]{:S(2)}) collective-permute-start(bf16[128,1024]{1,0:T(8,128)(2,1)S(1)} %collective-permute-done.72), channel_id=1, source_target_pairs={{0,1},{1,0},{2,3},{3,2},{4,5},{5,4},{6,7},{7,6},{8,9},{9,8},{10,11... | collective-permute-start | bytes 786440 | tf_op jit(solution)/shard_map/ppermute | solution.py:20
  523.1 6.5 %collective-permute-start.68 = (bf16[128,1024]{1,0:T(8,128)(2,1)}, bf16[128,1024]{1,0:T(8,128)(2,1)S(1)}, u32[]{:S(2)}, u32[]{:S(2)}) collective-permute-start(bf16[128,1024]{1,0:T(8,128)(2,1)} %join.9.refs_0_), channel_id=1, source_target_pairs={{0,1},{1,0},{2,3},{3,2},{4,5},{5,4},{6,7},{7,6},{8,9},{9,8},{10,11... | collective-permute-start | bytes 786440 | tf_op jit(solution)/shard_map/ppermute | solution.py:20
  (99 other events, 662.0 us)
